TPU v7x, 32 devices: a whole 2x2x4 slice. The times are simulated.
32 devices in a mesh: batch: 4 (over y, x), ctx: 2 (over core), tp: 4 (over z).
Axes of the slice: x: 2, y: 2, z: 4, core: 2. Of those that a mesh axis runs over, the one named last changes fastest.
Arguments:
- hidden_in: bfloat16 [4, 4, 128, 640], P('batch', 'ctx'), may hold values from -6 to 6
- positions: int32 [4, 512], P('batch'), may hold values from 0 to 255, as said below
- block_table: int32 [4], replicated, may hold values from 0 to 3, as said below
- norm_gains: float32 [4, 640], replicated, may hold values from 0.1 to 1.9
- head_norm_gains: float32 [2, 256], replicated, may hold values from 0.6 to 4.5
- query_weight: bfloat16 [640, 1024], P(None, 'tp')
- key_value_weight: bfloat16 [640, 512], replicated
- output_weight: bfloat16 [1024, 640], P('tp'), may hold values from -0.1875 to 0.1875
- gate_weight: bfloat16 [640, 2048], P(None, 'tp'), may hold values from -0.25 to 0.25
- up_weight: bfloat16 [640, 2048], P(None, 'tp'), may hold values from -0.25 to 0.25
- down_weight: bfloat16 [2048, 640], P('tp'), may hold values from -0.125 to 0.125
- out_cotangent: bfloat16 [4, 4, 128, 640], P('batch', 'ctx'), may hold values from -6 to 6
Outputs:
- hidden_out: bfloat16 [4, 4, 128, 640], P('batch', 'ctx')
- input_grad: bfloat16 [4, 4, 128, 640], P('batch', 'ctx')
- query_weight_grad: float32 [640, 1024], P(('batch', 'ctx'), 'tp')
- key_value_weight_grad: float32 [640, 512], P(('batch', 'ctx'))
- output_weight_grad: float32 [1024, 640], P('tp', ('batch', 'ctx'))
- gate_weight_grad: float32 [640, 2048], P(('batch', 'ctx'), 'tp')
- up_weight_grad: float32 [640, 2048], P(('batch', 'ctx'), 'tp')
- down_weight_grad: float32 [2048, 640], P('tp', ('batch', 'ctx'))
- norm_gains_grad: float32 [4, 640], P(None, ('batch', 'ctx'))
- head_norm_gains_grad: float32 [2, 256], P(None, ('batch', 'ctx'))
Inputs may be any that keep to these rules, and one draw needn't show every extreme that they name: `positions`: in each sequence the first token has position 0 and every later token has position 0 (a new document begins) or its predecessor's position plus 1; a sequence holds at most 4 documents, and its longest document has exactly 256 tokens. `block_table`: slots 2 k and 2 k + 1 hold two blocks whose numbers add up to 3; every block number appears once.
All inputs are finite; a program needn't handle non-finite values.
Results may differ from a plain program's by a relative error of at most 0.023.
Values may be sent and summed in bfloat16 or wider, within the bound.
No kernel may reach another device: no remote copies, remote signals or barrier semaphores. Data moves between devices by JAX's collectives and lax.ppermute only.
A program may use at most 128 MiB of HBM per device.

v0:
```python
import functools

import jax
import jax.numpy as jnp
from jax import lax
from jax.experimental import pallas as pl
from jax.experimental.pallas import tpu as pltpu
from jax.sharding import PartitionSpec as P


epsilon = 1e-06
rope_base = 1000000.0
gelu_coef = 0.7978845608028654
f32 = jnp.float32
bf16 = jnp.bfloat16


def rms_scale(v):
    return lax.rsqrt(jnp.mean(v * v, axis=-1, keepdims=True) + epsilon)


def rms_back(grad, unit, scale, gain):
    weighted = grad * gain
    return scale * (weighted - unit * jnp.mean(unit * weighted, axis=-1, keepdims=True))


def rotate(v, cosine, sine):
    half = v.shape[-1] // 2
    first, second = (v[..., :half], v[..., half:])
    return jnp.concatenate(
        [first * cosine - second * sine, second * cosine + first * sine], axis=-1
    )


def rotate_back(g, cosine, sine):
    half = g.shape[-1] // 2
    first, second = (g[..., :half], g[..., half:])
    return jnp.concatenate(
        [first * cosine + second * sine, second * cosine - first * sine], axis=-1
    )


def product(left, right):
    return jnp.dot(left, right, preferred_element_type=f32)


def lead_product(left, right):
    return lax.dot_general(left, right, (((0,), (0,)), ((), ())), preferred_element_type=f32)


def back_product(left, right):
    return lax.dot_general(left, right, (((1,), (1,)), ((), ())), preferred_element_type=f32)


def kernel_call(body, args, outs, scratch=(), tables=0, flops=0):
    moved = sum(a.size * a.dtype.itemsize for a in args)
    moved += sum(functools.reduce(lambda m, n: m * n, s, 1) * jnp.dtype(d).itemsize for s, d in outs)
    work = sum(functools.reduce(lambda m, n: m * n, s.shape, 1) * jnp.dtype(s.dtype).itemsize for s in scratch)
    limit = min(60 << 20, (8 << 20) + 2 * (moved + work))
    return pl.pallas_call(
        body,
        out_shape=[jax.ShapeDtypeStruct(s, d) for s, d in outs],
        in_specs=[pl.BlockSpec(memory_space=pltpu.SMEM)] * tables
        + [pl.BlockSpec(memory_space=pltpu.VMEM)] * (len(args) - tables),
        out_specs=[pl.BlockSpec(memory_space=pltpu.VMEM)] * len(outs),
        scratch_shapes=list(scratch),
        cost_estimate=pl.CostEstimate(flops=flops, bytes_accessed=moved, transcendentals=0),
        compiler_params=pltpu.CompilerParams(vmem_limit_bytes=limit),
    )(*args)


def swap(x, axis, size, k):
    return lax.ppermute(x, axis, [(i, i ^ k) for i in range(size)])


def after(x, *others):
    return lax.optimization_barrier((x, *others))[0]


def on_device(
    hidden_in,
    positions,
    block_table,
    norm_gains,
    head_norm_gains,
    query_weight,
    key_value_weight,
    output_weight,
    gate_weight,
    up_weight,
    down_weight,
    out_cotangent,
):
    n_tp = lax.axis_size("tp")
    n_ctx = lax.axis_size("ctx")
    n_batch = lax.axis_size("batch")
    blocks, block_len, width = hidden_in.shape[1:]
    rows = blocks * block_len
    head_dim = key_value_weight.shape[1] // 2
    half = head_dim // 2
    heads = query_weight.shape[1] // head_dim
    q_width = heads * head_dim
    ff = gate_weight.shape[1]
    seq = positions.shape[1]
    root = head_dim ** (-0.5)
    share = rows // 2
    unit_len = min(share, block_len)
    peers = tuple(range(2, n_tp, 2))
    copies = n_tp // 2
    shards = n_batch * n_ctx
    out_rows = width // shards
    head_rows = head_dim // shards
    paired = n_ctx == 2 and n_batch in (2, 4)

    hidden = hidden_in.reshape(rows, width)
    cot = out_cotangent.reshape(rows, width)
    freq = (rope_base ** (-(jnp.arange(half, dtype=f32) * 2.0 / head_dim))).reshape(1, half)

    def part(k):
        return slice(k * share, (k + 1) * share)

    def own_rows(k):
        return pl.ds(pl.multiple_of(((lax.axis_index("tp") & 1) ^ k) * share, share), share)

    def neighbour(x):
        return swap(x, "tp", n_tp, 1)

    def other_core(x):
        return swap(x, "ctx", n_ctx, 1)

    def exchanged(x):
        return [x] + [swap(x, "tp", n_tp, k) for k in peers]

    def joined(refs, columns=slice(None)):
        return jnp.concatenate([r[:, columns] for r in refs], axis=0)

    def summed(refs):
        total = refs[0][...].astype(f32)
        for r in refs[1:]:
            total = total + r[...].astype(f32)
        return total

    def own_half(length):
        half_length = length // 2
        return pl.ds(pl.multiple_of((lax.axis_index("ctx") & 1) * half_length, half_length), half_length)

    def own_piece(length):
        piece = length // (2 * n_batch)
        place = ((lax.axis_index("ctx") & 1) * n_batch + lax.axis_index("batch")) * piece
        return pl.ds(pl.multiple_of(place, piece), piece)

    up_piece = width // (2 * n_batch)
    down_piece = ff // (2 * n_batch)
    piece_rows = max(up_piece, down_piece)

    def pack_body(gate, up, down, gate_o, piece_o, sem):
        if up_piece < piece_rows:
            piece_o[up_piece:, :ff] = jnp.zeros((piece_rows - up_piece, ff), bf16)
        if down_piece < piece_rows:
            piece_o[down_piece:, ff:] = jnp.zeros((piece_rows - down_piece, width), bf16)
        moves = [
            pltpu.make_async_copy(up.at[own_piece(width), :], piece_o.at[:up_piece, :ff], sem.at[0]),
            pltpu.make_async_copy(down.at[own_piece(ff), :], piece_o.at[:down_piece, ff:], sem.at[1]),
            pltpu.make_async_copy(gate.at[own_half(width), :], gate_o, sem.at[2]),
        ]
        for move in moves:
            move.start()
        for move in moves:
            move.wait()

    gate_pack, piece_pack = pl.pallas_call(
        pack_body,
        out_shape=[jax.ShapeDtypeStruct((width // 2, ff), bf16), jax.ShapeDtypeStruct((piece_rows, ff + width), bf16)],
        in_specs=[pl.BlockSpec(memory_space=pltpu.HBM)] * 3,
        out_specs=[pl.BlockSpec(memory_space=pltpu.VMEM)] * 2,
        scratch_shapes=[pltpu.SemaphoreType.DMA((3,))],
        name="pack",
        compiler_params=pltpu.CompilerParams(vmem_limit_bytes=16 << 20),
    )(*(pltpu.with_memory_space_constraint(w, pltpu.HBM) for w in (gate_weight, up_weight, down_weight)))
    gate_near = neighbour(gate_pack)
    piece_near = neighbour(piece_pack)
    pieces = [piece_near] + [swap(piece_near, "batch", n_batch, k) for k in range(1, n_batch)]

    def stack_body(*refs):
        up_o, down_o = refs[n_batch:]
        for k in range(n_batch):
            b = lax.axis_index("batch") ^ k
            up_o[pl.ds(pl.multiple_of(b * up_piece, up_piece), up_piece), :] = refs[k][:up_piece, :ff]
            down_o[pl.ds(pl.multiple_of(b * down_piece, down_piece), down_piece), :] = refs[k][
                :down_piece, ff:
            ]

    up_near, down_near = kernel_call(stack_body, tuple(pieces), [((width // 2, ff), bf16), ((ff // 2, width), bf16)])

    def whole_body(*refs):
        for mine, far, whole in zip(refs[:3], refs[3:6], refs[6:]):
            length = mine.shape[0]
            for k, ref in enumerate((mine, far)):
                place = ((lax.axis_index("ctx") & 1) ^ k) * length
                whole[pl.ds(pl.multiple_of(place, length), length), :] = ref[...]

    halves = (gate_near, up_near, down_near)
    near_weights = kernel_call(
        whole_body,
        halves + tuple(other_core(h) for h in halves),
        [((width, ff), bf16), ((width, ff), bf16), ((ff, width), bf16)],
    )

    def pre_body(table, hid, pos, gains, hgains, freqs, wkv, normed_o, kv_o, unit_o, scale_o, cos_o, sin_o, idx_o, start_o, col_pos, col_idx):
        eye = lax.broadcasted_iota(jnp.int32, (block_len, block_len), 0) == lax.broadcasted_iota(
            jnp.int32, (block_len, block_len), 1
        )
        for j in range(blocks):
            t = table[lax.axis_index("ctx") * blocks + j]
            line = pos[:, pl.ds(pl.multiple_of(t * block_len, block_len), block_len)].astype(f32)
            column = jnp.sum(jnp.where(eye, line, 0.0), axis=1, keepdims=True)
            place = lax.broadcasted_iota(jnp.int32, (block_len, 1), 0) + t * block_len
            col_pos[j * block_len : (j + 1) * block_len, :] = column
            col_idx[j * block_len : (j + 1) * block_len, :] = place.astype(f32)
        for k in range(2):
            at = own_rows(k)
            x = hid[at, :].astype(f32)
            normed_o[part(k), :] = (x * rms_scale(x) * gains[0:1, :]).astype(bf16)
            p = col_pos[at, :]
            angle = p * freqs[...]
            cos_o[part(k), :] = jnp.cos(angle)
            sin_o[part(k), :] = jnp.sin(angle)
            idx_o[part(k), :] = col_idx[at, :]
            start_o[part(k), :] = col_idx[at, :] - p
        kv = product(normed_o[...], wkv[...])
        key = kv[:, :head_dim]
        scale = rms_scale(key)
        unit = key * scale
        unit_o[...] = unit
        scale_o[...] = scale
        kv_o[:, :head_dim] = rotate(unit * hgains[1:2, :], cos_o[...], sin_o[...]).astype(bf16)
        kv_o[:, head_dim:] = kv[:, head_dim:].astype(bf16)

    normed, kv_mine, unit_k, scale_k, cosine, sine, idx, start = kernel_call(
        pre_body,
        (block_table, hidden, positions, norm_gains, head_norm_gains, freq, key_value_weight),
        [
            ((rows, width), bf16),
            ((rows, 2 * head_dim), bf16),
            ((rows, head_dim), f32),
            ((rows, 1), f32),
            ((rows, half), f32),
            ((rows, half), f32),
            ((rows, 1), f32),
            ((rows, 1), f32),
        ],
        scratch=[pltpu.VMEM((rows, 1), f32), pltpu.VMEM((rows, 1), f32)],
        tables=1,
    )

    if paired:
        kvs = [kv_mine, other_core(kv_mine)]
    else:
        kvs = [lax.all_gather(kv_mine, "ctx", axis=0, tiled=True)]

    def query_body(nrm, wq, hgains, cos, sin, q_o, unit_o, scale_o):
        raw = product(nrm[...], wq[...])
        for h in range(heads):
            cols = slice(h * head_dim, (h + 1) * head_dim)
            scale = rms_scale(raw[:, cols])
            unit = raw[:, cols] * scale
            unit_o[:, cols] = unit
            scale_o[:, h : h + 1] = scale
            q_o[:, cols] = (rotate(unit * hgains[0:1, :], cos[...], sin[...]) * root).astype(bf16)

    queries, unit_q, scale_q = kernel_call(
        query_body,
        (normed, query_weight, head_norm_gains, cosine, sine),
        [((rows, q_width), bf16), ((rows, q_width), f32), ((rows, heads), f32)],
    )

    def attend_body(*refs):
        table, q, idx_r, start_r, wo = refs[:5]
        kv = refs[5 : 5 + len(kvs)]
        probs_o, context_o, mine_o, send_o = refs[5 + len(kvs) :]
        low = lax.axis_index("tp") & 1
        ctx = lax.axis_index("ctx")
        order = [ctx, ctx ^ 1] if paired else list(range(n_ctx))
        lane = lax.broadcasted_iota(jnp.int32, (1, seq), 1)
        key_idx = lane
        for m, rank in enumerate(order):
            for at in range(0, rows, unit_len):
                first = (low ^ (at // share)) * share + at % share
                base = table[rank * blocks + lax.div(first, block_len)] * block_len
                base = base + lax.rem(first, block_len)
                begin = m * rows + at
                key_idx = jnp.where(
                    (lane >= begin) & (lane < begin + unit_len), lane + (base - begin), key_idx
                )
        key_idx = key_idx.astype(f32)
        allowed = (key_idx <= idx_r[...]) & (key_idx >= start_r[...])
        length = seq // len(kvs)
        for h in range(heads):
            cols = slice(h * head_dim, (h + 1) * head_dim)
            scores = jnp.concatenate(
                [back_product(q[:, cols], r[:, :head_dim]) for r in kv], axis=1
            )
            scores = jnp.where(allowed, scores, -jnp.inf)
            top = jnp.max(scores, axis=1, keepdims=True)
            expo = jnp.exp(scores - top)
            inverse = 1.0 / jnp.sum(expo, axis=1, keepdims=True)
            probs_o[h] = expo * inverse
            probs = expo.astype(bf16)
            mixed = product(probs[:, :length], kv[0][:, head_dim:])
            for m in range(1, len(kvs)):
                mixed = mixed + product(probs[:, m * length : (m + 1) * length], kv[m][:, head_dim:])
            context_o[:, cols] = (mixed * inverse).astype(bf16)
        total = product(context_o[...], wo[...])
        mine_o[...] = total[part(0)]
        send_o[...] = total[part(1)].astype(bf16)

    probs, context, attn_mine, attn_send = kernel_call(
        attend_body,
        (block_table, queries, idx, start, output_weight, *kvs),
        [
            ((heads, rows, seq), f32),
            ((rows, q_width), bf16),
            ((share, width), f32),
            ((share, width), bf16),
        ],
        tables=1,
    )

    def meet_body(a, b, o):
        o[...] = (a[...] + b[...].astype(f32)).astype(bf16)

    def meet(mine, got):
        return kernel_call(meet_body, (mine, got), [((share, width), bf16)])[0]

    attn_met = meet(attn_mine, neighbour(attn_send))
    attn_terms = exchanged(attn_met)
    n_terms = len(attn_terms)
    weights = (gate_weight, up_weight, down_weight, *near_weights)

    def ff_groups(refs):
        return [
            (refs[0][...], refs[1][...], refs[2][...], slice(0, ff)),
            (refs[3][...], refs[4][...], refs[5][...], slice(ff, 2 * ff)),
        ]

    def feed_body(*refs):
        hid, gains = refs[:2]
        groups = ff_groups(refs[2:8])
        attn = summed(refs[8 : 8 + n_terms])
        unit_o, scale_o, mixed_o, x_o, act_o, gate_o, up_o, send_o = refs[8 + n_terms :]
        scale = rms_scale(attn)
        unit = attn * scale
        mixed = hid[own_rows(0), :].astype(f32) + unit * gains[1:2, :]
        unit_o[...] = unit
        scale_o[...] = scale
        mixed_o[...] = mixed
        x = (mixed * rms_scale(mixed) * gains[2:3, :]).astype(bf16)
        x_o[...] = x
        total = None
        for wg, wu, wd, cols in groups:
            gate = product(x, wg)
            up = product(x, wu)
            gate_o[:, cols] = gate
            up_o[:, cols] = up
            inner = gelu_coef * (gate + 0.044715 * gate * gate * gate)
            act = (0.5 * gate * (1.0 + jnp.tanh(inner)) * up).astype(bf16)
            term = product(act, wd)
            total = term if total is None else total + term
            act_o[:, cols] = act
        send_o[...] = total.astype(bf16)

    unit_a, scale_a, mixed, ff_in, activated, gate, up, ff_send = kernel_call(
        feed_body,
        (hidden, norm_gains, *weights, *attn_terms),
        [
            ((share, width), f32),
            ((share, 1), f32),
            ((share, width), f32),
            ((share, width), bf16),
            ((share, 2 * ff), bf16),
            ((share, 2 * ff), f32),
            ((share, 2 * ff), f32),
            ((share, width), bf16),
        ],
    )
    ff_terms = exchanged(ff_send)

    def slope_body(gate_r, up_r, gelu_o, slope_o):
        v = gate_r[...]
        inner = gelu_coef * (v + 0.044715 * v * v * v)
        tanh_val = jnp.tanh(inner)
        gelu_o[...] = 0.5 * v * (1.0 + tanh_val)
        slope = 0.5 * (1.0 + tanh_val) + 0.5 * v * (1.0 - tanh_val * tanh_val) * gelu_coef * (
            1.0 + 3.0 * 0.044715 * v * v
        )
        slope_o[...] = slope * up_r[...]

    gelu, up_slope = kernel_call(slope_body, (gate, up), [((share, 2 * ff), f32), ((share, 2 * ff), f32)])

    def back_body(*refs):
        gains, mixed_r, cot_r, gelu_r, slope_r = refs[:5]
        groups = ff_groups(refs[5:11])
        ff_out = summed(refs[11 : 11 + n_terms])
        hidden_o, gain_o, dout_o, dgate_o, dup_o, send_o = refs[11 + n_terms :]
        scale = rms_scale(ff_out)
        unit = ff_out * scale
        hidden_o[...] = (mixed_r[...] + unit * gains[3:4, :]).astype(bf16)
        grad = cot_r[own_rows(0), :].astype(f32)
        gain_o[...] = jnp.sum(grad * unit, axis=0, keepdims=True) * (1.0 / copies)
        d_out = rms_back(grad, unit, scale, gains[3:4, :]).astype(bf16)
        dout_o[...] = d_out
        total = None
        for wg, wu, wd, cols in groups:
            d_act = back_product(d_out, wd)
            d_gate = (d_act * slope_r[:, cols]).astype(bf16)
            d_up = (d_act * gelu_r[:, cols]).astype(bf16)
            term = back_product(d_gate, wg) + back_product(d_up, wu)
            total = term if total is None else total + term
            dgate_o[:, cols] = d_gate
            dup_o[:, cols] = d_up
        send_o[...] = total.astype(bf16)

    hidden_mine, gain_o, d_ff_out, d_gate, d_up, dff_send = kernel_call(
        back_body,
        (norm_gains, mixed, cot, gelu, up_slope, *weights, *ff_terms),
        [
            ((share, width), bf16),
            ((1, width), f32),
            ((share, width), bf16),
            ((share, 2 * ff), bf16),
            ((share, 2 * ff), bf16),
            ((share, width), bf16),
        ],
    )
    dffin_terms = exchanged(dff_send)
    hidden_near = neighbour(hidden_mine)

    def arrange(acc, outs):
        if not paired:
            outs[0][...] = acc[...]
            return
        batch = lax.axis_index("batch")
        ctx = lax.axis_index("ctx")
        for side in range(2):
            for k in range(n_batch):
                first = ((batch ^ k) * n_ctx + (ctx ^ side)) * out_rows
                outs[side][k * out_rows : (k + 1) * out_rows, :] = acc[
                    pl.ds(pl.multiple_of(first, out_rows), out_rows), :
                ].astype(bf16)

    def grad_call(body, args, columns):
        if paired:
            outs = [((n_batch * out_rows, columns), bf16)] * 2
        else:
            outs = [((width, columns), f32)]
        return kernel_call(body, args, outs, scratch=[pltpu.VMEM((width, columns), f32)])

    def reduce_grads(grads):
        if not paired:
            return [lax.psum_scatter(grads[0], ("batch", "ctx"), scatter_dimension=0, tiled=True)]
        keep, send = grads
        columns = keep.shape[1]
        got = other_core(send)

        def add_body(a, b, *outs):
            total = a[...].astype(f32) + b[...].astype(f32)
            for k in range(n_batch):
                outs[k][...] = total[k * out_rows : (k + 1) * out_rows].astype(outs[k].dtype)

        parts = kernel_call(
            add_body, (keep, got), [((out_rows, columns), f32)] + [((out_rows, columns), bf16)] * (n_batch - 1)
        )
        return [parts[0]] + [swap(parts[k], "batch", n_batch, k) for k in range(1, n_batch)]

    def ff_grad_body(x, d_out, act, dgate, dup, *refs):
        acc = refs[-1]
        for at, left, right in ((0, x, dgate), (1, x, dup), (2, d_out, act)):
            total = lead_product(left[...], right[...])
            acc[:, at * ff : (at + 1) * ff] = total[:, :ff]
            acc[:, (3 + at) * ff : (4 + at) * ff] = total[:, ff:]
        arrange(acc, refs[:-1])

    ff_grads = grad_call(ff_grad_body, (ff_in, d_ff_out, activated, d_gate, d_up), 6 * ff)
    mid_terms = reduce_grads(ff_grads)

    def mix_back_body(gains, mixed_r, unit_r, scale_r, cot_r, *refs):
        d_in = summed(refs[:n_terms])
        dmixed_o, dattn_o, gain_f_o, gain_a_o = refs[n_terms:]
        mixed_v = mixed_r[...]
        scale = rms_scale(mixed_v)
        unit_f = mixed_v * scale
        gain_f_o[...] = jnp.sum(d_in * unit_f, axis=0, keepdims=True) * (1.0 / copies)
        d_mix = cot_r[own_rows(0), :].astype(f32) + rms_back(d_in, unit_f, scale, gains[2:3, :])
        dmixed_o[...] = d_mix
        unit = unit_r[...]
        gain_a_o[...] = jnp.sum(d_mix * unit, axis=0, keepdims=True) * (1.0 / copies)
        dattn_o[...] = rms_back(d_mix, unit, scale_r[...], gains[1:2, :]).astype(bf16)

    d_mixed, dattn_mine, gain_f, gain_a = kernel_call(
        mix_back_body,
        (norm_gains, mixed, unit_a, scale_a, cot, dffin_terms[0], *(after(t, ff_grads[0]) for t in dffin_terms[1:])),
        [((share, width), f32), ((share, width), bf16), ((1, width), f32), ((1, width), f32)],
    )
    d_attn = (dattn_mine, after(neighbour(dattn_mine), mid_terms[0]))

    def attend_back_body(*refs):
        wo, probs_r, q = refs[:3]
        kv = refs[3 : 3 + len(kvs)]
        d_out = joined(refs[3 + len(kvs) : 5 + len(kvs)])
        dq_o = refs[5 + len(kvs)]
        dkv_o = refs[6 + len(kvs) :]
        d_context = back_product(d_out, wo[...]).astype(bf16)
        length = seq // len(kvs)
        for h in range(heads):
            cols = slice(h * head_dim, (h + 1) * head_dim)
            probs_v = probs_r[h]
            d_probs = jnp.concatenate(
                [back_product(d_context[:, cols], r[:, head_dim:]) for r in kv], axis=1
            )
            delta = jnp.sum(probs_v * d_probs, axis=1, keepdims=True)
            d_scores = (probs_v * (d_probs - delta)).astype(bf16)
            rounded = probs_v.astype(bf16)
            d_q = None
            for m, r in enumerate(kv):
                span = slice(m * length, (m + 1) * length)
                term = product(d_scores[:, span], r[:, :head_dim])
                d_q = term if d_q is None else d_q + term
                d_k = lead_product(d_scores[:, span], q[:, cols])
                d_v = lead_product(rounded[:, span], d_context[:, cols])
                if h > 0:
                    d_k = d_k + dkv_o[m][:, :head_dim].astype(f32)
                    d_v = d_v + dkv_o[m][:, head_dim:].astype(f32)
                dkv_o[m][:, :head_dim] = d_k.astype(dkv_o[m].dtype)
                dkv_o[m][:, head_dim:] = d_v.astype(dkv_o[m].dtype)
            dq_o[:, cols] = d_q

    if paired:
        dkv_outs = [((rows, 2 * head_dim), f32), ((rows, 2 * head_dim), f32 if heads > 1 else bf16)]
    else:
        dkv_outs = [((seq, 2 * head_dim), f32)]
    attended_back = kernel_call(
        attend_back_body, (output_weight, probs, queries, *kvs, *d_attn), [((rows, q_width), f32)] + dkv_outs
    )
    d_q = attended_back[0]
    if paired:
        dkv_terms = [attended_back[1], other_core(attended_back[2])]
    else:
        dkv_terms = [lax.psum_scatter(attended_back[1], "ctx", scatter_dimension=0, tiled=True)]

    def query_back_body(dq, unit_r, scale_r, cos, sin, hgains, wq, draw_o, dn_o, gain_o):
        gain = jnp.zeros((1, head_dim), f32)
        for h in range(heads):
            cols = slice(h * head_dim, (h + 1) * head_dim)
            d_unit = rotate_back(dq[:, cols], cos[...], sin[...]) * root
            unit = unit_r[:, cols]
            gain = gain + jnp.sum(d_unit * unit, axis=0, keepdims=True)
            draw_o[:, cols] = rms_back(d_unit, unit, scale_r[:, h : h + 1], hgains[0:1, :]).astype(bf16)
        gain_o[...] = gain
        dn_o[...] = back_product(draw_o[...], wq[...])

    d_query_raw, dn_query, gain_q = kernel_call(
        query_back_body,
        (d_q, unit_q, scale_q, cosine, sine, head_norm_gains, query_weight),
        [((rows, q_width), bf16), ((rows, width), f32), ((1, head_dim), f32)],
    )

    def pre_back_body(dn, unit_r, scale_r, cos, sin, hgains, wkv, *refs):
        count = len(dkv_terms)
        d_kv = summed(refs[:count])
        draw_o, gain_o, mine_o, send_o = refs[count:]
        d_unit = rotate_back(d_kv[:, :head_dim], cos[...], sin[...])
        unit = unit_r[...]
        gain_o[...] = jnp.sum(d_unit * unit, axis=0, keepdims=True)
        draw_o[:, :head_dim] = rms_back(d_unit, unit, scale_r[...], hgains[1:2, :]).astype(bf16)
        draw_o[:, head_dim:] = d_kv[:, head_dim:].astype(bf16)
        total = dn[...] + back_product(draw_o[...], wkv[...])
        mine_o[...] = total[part(0)]
        send_o[...] = total[part(1)].astype(bf16)

    d_kv_raw, gain_k, dn_mine, dn_send = kernel_call(
        pre_back_body,
        (dn_query, unit_k, scale_k, cosine, sine, head_norm_gains, key_value_weight, *dkv_terms),
        [
            ((rows, 2 * head_dim), bf16),
            ((1, head_dim), f32),
            ((share, width), f32),
            ((share, width), bf16),
        ],
    )
    dn_terms = exchanged(meet(dn_mine, neighbour(dn_send)))

    def mid_body(*refs):
        count = len(mid_terms)
        total = summed(refs[:count])
        refs[count][...] = total[:, : 3 * ff]
        refs[count + 1][...] = total[:, 3 * ff :].astype(bf16)

    mid_mine, mid_send = kernel_call(
        mid_body, tuple(mid_terms), [((out_rows, 3 * ff), f32), ((out_rows, 3 * ff), bf16)]
    )

    def ff_out_body(mine, near, *outs):
        for k in range(3):
            cols = slice(k * ff, (k + 1) * ff)
            outs[k][...] = mine[:, cols] + near[:, cols].astype(f32)

    gate_grad, up_grad, down_grad = kernel_call(
        ff_out_body, (mid_mine, neighbour(mid_send)), [((out_rows, ff), f32)] * 3
    )

    lanes = 128
    kv_at = q_width
    gain_at = q_width + 2 * head_dim
    out_at = gain_at + lanes

    def last_grad_body(nrm, draw, dkv, hid, g_o, g_f, g_a, g_q, g_k, mine, send, ctx_r, da, da_near, *refs):
        acc = refs[-1]
        acc[:, :kv_at] = lead_product(nrm[...], draw[...])
        acc[:, out_at:] = lead_product(joined((da, da_near)), ctx_r[...])
        acc[:, kv_at:gain_at] = lead_product(nrm[...], dkv[...])
        g_in = jnp.zeros((1, width), f32)
        for k, terms in enumerate((mine, send)):
            x = hid[own_rows(k), :].astype(f32)
            g_in = g_in + jnp.sum(terms[...].astype(f32) * x * rms_scale(x), axis=0, keepdims=True)
        line = lax.broadcasted_iota(jnp.int32, (lanes, width), 0)
        packed = jnp.where(line == 0, g_in, 0.0)
        for at, row in enumerate((g_a, g_f, g_o), 1):
            packed = jnp.where(line == at, row[...], packed)
        acc[:, gain_at:out_at] = packed.T
        line = lax.broadcasted_iota(jnp.int32, (lanes, head_dim), 0)
        packed = jnp.where(line == 4, g_q[...], jnp.where(line == 5, g_k[...], 0.0)).T
        for d in range(shards):
            at = slice(d * out_rows, d * out_rows + head_rows)
            acc[at, gain_at:out_at] = acc[at, gain_at:out_at] + packed[d * head_rows : (d + 1) * head_rows]
        arrange(acc, refs[:-1])

    last_terms = reduce_grads(
        grad_call(
            last_grad_body,
            (normed, d_query_raw, d_kv_raw, hidden, gain_o, gain_f, gain_a, gain_q, gain_k, dn_mine, dn_send, context, *d_attn),
            out_at + q_width,
        ),
    )

    def last_body(*refs):
        count = len(last_terms)
        total = summed(refs[:count])
        refs[count][...] = total[:, :kv_at]
        refs[count + 1][...] = total[:, kv_at:out_at].astype(bf16)
        refs[count + 2][...] = total[:, out_at:]

    query_grad, kv_mine_sum, out_grad = kernel_call(
        last_body,
        tuple(last_terms),
        [((out_rows, q_width), f32), ((out_rows, 2 * head_dim + lanes), bf16), ((out_rows, q_width), f32)],
    )
    kv_sums = [kv_mine_sum] + [swap(kv_mine_sum, "tp", n_tp, k) for k in range(1, n_tp)]

    def kv_body(*refs):
        terms = [r[...].astype(f32) for r in refs[:n_tp]]
        while len(terms) > 1:
            terms = [a + b for a, b in zip(terms[::2], terms[1::2])]
        refs[n_tp][...] = terms[0][:, : 2 * head_dim]
        lines = terms[0][:, 2 * head_dim :].T
        refs[n_tp + 1][...] = lines[:4]
        refs[n_tp + 2][...] = lines[4:6, :head_rows]

    kv_grad, gain_grad, head_gain_grad = kernel_call(
        kv_body, tuple(kv_sums), [((out_rows, 2 * head_dim), f32), ((4, out_rows), f32), ((2, head_rows), f32)]
    )

    def input_back_body(hid, gains, dmix, *refs):
        d_normed = summed(refs[:n_terms])
        x = hid[own_rows(0), :].astype(f32)
        scale = rms_scale(x)
        refs[n_terms][...] = (dmix[...] + rms_back(d_normed, x * scale, scale, gains[0:1, :])).astype(bf16)

    (input_mine,) = kernel_call(input_back_body, (hidden, norm_gains, d_mixed, *dn_terms), [((share, width), bf16)])

    def place_body(a, b, o):
        o[own_rows(0), :] = a[...]
        o[own_rows(1), :] = b[...]

    def placed(mine, near):
        (whole,) = kernel_call(place_body, (mine, near), [((rows, width), bf16)])
        return whole.reshape(hidden_in.shape)

    return (
        placed(hidden_mine, hidden_near),
        placed(input_mine, neighbour(input_mine)),
        query_grad,
        kv_grad,
        out_grad.T,
        gate_grad,
        up_grad,
        down_grad.T,
        gain_grad,
        head_gain_grad,
    )


def solution(mesh):
    return jax.shard_map(
        on_device,
        mesh=mesh,
        in_specs=(
            P("batch", "ctx", None, None),
            P("batch", None),
            P(),
            P(),
            P(),
            P(None, "tp"),
            P(),
            P("tp", None),
            P(None, "tp"),
            P(None, "tp"),
            P("tp", None),
            P("batch", "ctx", None, None),
        ),
        out_specs=(
            P("batch", "ctx", None, None),
            P("batch", "ctx", None, None),
            P(("batch", "ctx"), "tp"),
            P(("batch", "ctx"), None),
            P("tp", ("batch", "ctx")),
            P(("batch", "ctx"), "tp"),
            P(("batch", "ctx"), "tp"),
            P("tp", ("batch", "ctx")),
            P(None, ("batch", "ctx")),
            P(None, ("batch", "ctx")),
        ),
        check_vma=False,
    )
```

profile of v0, /device:TPU:0, one launch (start us, length us, event | category | flops | bytes accessed | tf_op | source)
XLA Modules:
  0.0 112.7 jit_solution(7568008384761187657)
XLA Ops:
  0.7 1.2 %pack.1 = (bf16[320,512]{1,0:T(8,128)(2,1)S(1)}, bf16[80,1152]{1,0:T(8,128)(2,1)S(1)}) custom-call(bf16[640,512]{1,0:T(8,128)(2,1)} %refs_5_.1, bf16[640,512]{1,0:T(8,128)(2,1)} %refs_6_.1, bf16[512,640]{1,0:T(8,128)(2,1)} %refs_7_.1), custom_call_target="tpu_custom_call" | custom-call | tf_op jit(solution)/shard_map/pack/pallas_call | solution.py:171
  1.9 3.1 %collective-permute-start.1 = (bf16[80,1152]{1,0:T(8,128)(2,1)S(1)}, bf16[80,1152]{1,0:T(8,128)(2,1)S(1)}, u32[]{:S(2)}, u32[]{:S(2)}) collective-permute-start(bf16[80,1152]{1,0:T(8,128)(2,1)S(1)} %get-tuple-element.88), channel_id=1, source_target_pairs={{0,1},{1,0},{2,3},{3,2},{4,5},{5,4},{6,7},{7,6},{8,9},{9,8},{10,11... | collective-permute-start | bytes 552968 | tf_op jit(solution)/shard_map/ppermute | solution.py:73
  5.2 1.4 %shard_map.197 = (bf16[256,640]{1,0:T(8,128)(2,1)S(1)}, bf16[256,512]{1,0:T(8,128)(2,1)S(1)}, f32[256,256]{1,0:T(8,128)S(1)}, f32[256,1]{1,0:T(8,128)S(1)}, f32[...) custom-call(s32[4]{0:T(128)S(1)} %copy-done.11, ...), custom_call_target="tpu_custom_call" | custom-call | bytes 2115088 | tf_op jit(solution)/shard_map/pallas_call | solution.py:60
  6.7 3.8 %collective-permute-done.1.refs_0_ = bf16[80,1152]{1,0:T(8,128)(2,1)S(1)} collective-permute-done((bf16[80,1152]{1,0:T(8,128)(2,1)S(1)}, bf16[80,1152]{1,0:T(8,128)(2,1)S(1)}, u32[]{:S(2)}, u32[]{:S(2)}) %collective-permute-start.1) | collective-permute-done | bytes 184352 | tf_op jit(solution)/shard_map/ppermute | solution.py:73
  10.5 2.9 %collective-permute-start.4 = (bf16[80,1152]{1,0:T(8,128)(2,1)S(1)}, bf16[80,1152]{1,0:T(8,128)(2,1)S(1)}, u32[]{:S(2)}, u32[]{:S(2)}) collective-permute-start(bf16[80,1152]{1,0:T(8,128)(2,1)S(1)} %collective-permute-done.1.refs_0_), channel_id=1, source_target_pairs={{0,24},{8,16},{16,8},{24,0},{1,25},{9,17},{17,9},{25,1},{2,26},{10... | collective-permute-start | bytes 552968 | tf_op jit(solution)/shard_map/ppermute | solution.py:73
  13.4 0.5 collective-permute-start.3
  14.0 0.4 shard_map.198
  14.4 1.3 %shard_map.199 = (f32[1,256,512]{2,1,0:T(8,128)S(1)}, bf16[256,256]{1,0:T(8,128)(2,1)S(1)}, f32[128,640]{1,0:T(8,128)S(1)}, bf16[128,640]{1,0:T(8,128)(2,1)S(1)}) custom-call(s32[4]{0:T(128)S(1)} %copy-done.11, bf16[256,256]{1,0:T(8,128)(2,1)S(1)} %get-tuple-element.97.refs_1_.refs_2_, f32[256,1]{1,0:T(8,128)S(1)} %get-tuple-element.98.refs_2_, ...), custom_call_target="tpu_custom_call" | custom-call | bytes 2131984 | tf_op jit(solution)/shard_map/pallas_call | solution.py:60
  15.8 2.1 %collective-permute-start.9 = (bf16[128,640]{1,0:T(8,128)(2,1)S(1)}, bf16[128,640]{1,0:T(8,128)(2,1)S(1)}, u32[]{:S(2)}, u32[]{:S(2)}) collective-permute-start(bf16[128,640]{1,0:T(8,128)(2,1)S(1)} %get-tuple-element.102), channel_id=1, source_target_pairs={{0,1},{1,0},{2,3},{3,2},{4,5},{5,4},{6,7},{7,6},{8,9},{9,8},{10,11... | collective-permute-start | bytes 491528 | tf_op jit(solution)/shard_map/ppermute | solution.py:73
  17.9 0.9 collective-permute-done.4.refs_3_
  18.8 1.5 %collective-permute-done.3.refs_2_ = bf16[80,1152]{1,0:T(8,128)(2,1)S(1)} collective-permute-done((bf16[80,1152]{1,0:T(8,128)(2,1)S(1)}, bf16[80,1152]{1,0:T(8,128)(2,1)S(1)}, u32[]{:S(2)}, u32[]{:S(2)}) %collective-permute-start.3) | collective-permute-done | bytes 184352 | tf_op jit(solution)/shard_map/ppermute | solution.py:73
  20.5 0.5 collective-permute-start.7
  21.2 3.1 %collective-permute-start.10 = (bf16[128,640]{1,0:T(8,128)(2,1)S(1)}, bf16[128,640]{1,0:T(8,128)(2,1)S(1)}, u32[]{:S(2)}, u32[]{:S(2)}) collective-permute-start(bf16[128,640]{1,0:T(8,128)(2,1)S(1)} %shard_map.200.refs_8_), channel_id=1, source_target_pairs={{0,2},{1,3},{2,0},{3,1},{4,6},{5,7},{6,4},{7,5},{8,10},{9,11},{10,... | collective-permute-start | bytes 491528 | tf_op jit(solution)/shard_map/ppermute | solution.py:73
  24.5 7.2 %collective-permute-done.10.refs_9_ = bf16[128,640]{1,0:T(8,128)(2,1)S(1)} collective-permute-done((bf16[128,640]{1,0:T(8,128)(2,1)S(1)}, bf16[128,640]{1,0:T(8,128)(2,1)S(1)}, u32[]{:S(2)}, u32[]{:S(2)}) %collective-permute-start.10) | collective-permute-done | bytes 163872 | tf_op jit(solution)/shard_map/ppermute | solution.py:73
  31.7 1.1 %shard_map.201 = (f32[128,640]{1,0:T(8,128)S(1)}, f32[128,1]{1,0:T(8,128)S(1)}, f32[128,640]{1,0:T(8,128)S(1)}, bf16[128,640]{1,0:T(8,128)(2,1)S(1)}, bf16[128,1...) custom-call(bf16[256,640]{1,0:T(8,128)(2,1)S(1)} %bitcast.7, ...), custom_call_target="tpu_custom_call" | custom-call | bytes 6892032 | tf_op jit(solution)/shard_map/pallas_call | solution.py:60
  32.9 0.4 shard_map.202
  33.4 9.2 %collective-permute-done.11.refs_12_ = bf16[128,640]{1,0:T(8,128)(2,1)S(1)} collective-permute-done((bf16[128,640]{1,0:T(8,128)(2,1)S(1)}, bf16[128,640]{1,0:T(8,128)(2,1)S(1)}, u32[]{:S(2)}, u32[]{:S(2)}) %collective-permute-start.11) | collective-permute-done | bytes 163872 | tf_op jit(solution)/shard_map/ppermute | solution.py:73
  42.6 1.7 %shard_map.203 = (bf16[128,640]{1,0:T(8,128)(2,1)S(1)}, f32[1,640]{1,0:T(1,128)S(1)}, bf16[128,640]{1,0:T(8,128)(2,1)S(1)}, bf16[128,1024]{1,0:T(8,128)(2,1)S(1)...) custom-call(f32[4,640]{1,0:T(4,128)S(1)} %copy-done.8, f32[128,640]{1,0:T(8,128)S(1)} %get-tuple-element.103.refs_1_.mixed_r, ...), custom_call_target="tpu_custom_call" | custom-call | bytes 6992384 | tf_op jit(solution)/shard_map/pallas_call | solution.py:60
  44.2 1.6 %shard_map.205 = (bf16[320,3072]{1,0:T(8,128)(2,1)S(1)}, bf16[320,3072]{1,0:T(8,128)(2,1)S(1)}) custom-call(bf16[128,640]{1,0:T(8,128)(2,1)S(1)} %get-tuple-element.113.x, bf16[128,640]{1,0:T(8,128)(2,1)S(1)} %get-tuple-element.114.d_out, bf16[128,1024]{1,0:T(8,128)(2,1)S(1)} %get-tuple-element.115.act, bf16[128,1024]{1,0:T(8,128)(2,1)S(1)} %get-tuple-element.116.dgate, ...), custom_call_target="tpu_custom_call" | custom-call | bytes 5046272 | tf_op jit(solution)/shard_map/pallas_call | solution.py:60
  46.0 9.4 %collective-permute-done.13.refs_1_ = bf16[128,640]{1,0:T(8,128)(2,1)S(1)} collective-permute-done((bf16[128,640]{1,0:T(8,128)(2,1)S(1)}, bf16[128,640]{1,0:T(8,128)(2,1)S(1)}, u32[]{:S(2)}, u32[]{:S(2)}) %collective-permute-start.13) | collective-permute-done | bytes 163872 | tf_op jit(solution)/shard_map/ppermute | solution.py:73
  55.3 0.4 shard_map.206
  55.8 0.4 shard_map.207
  56.3 5.7 %collective-permute-done.14.refs_6_.da_near = bf16[128,640]{1,0:T(8,128)(2,1)S(1)} collective-permute-done((bf16[128,640]{1,0:T(8,128)(2,1)S(1)}, bf16[128,640]{1,0:T(8,128)(2,1)S(1)}, u32[]{:S(2)}, u32[]{:S(2)}) %collective-permute-start.14) | collective-permute-done | bytes 163872 | tf_op jit(solution)/shard_map/ppermute | solution.py:73
  62.0 1.0 shard_map.208
  63.0 0.4 shard_map.209
  63.4 1.1 %collective-permute-done.16.refs_1_ = bf16[256,512]{1,0:T(8,128)(2,1)S(1)} collective-permute-done((bf16[256,512]{1,0:T(8,128)(2,1)S(1)}, bf16[256,512]{1,0:T(8,128)(2,1)S(1)}, u32[]{:S(2)}, u32[]{:S(2)}) %collective-permute-start.16) | collective-permute-done | bytes 262176 | tf_op jit(solution)/shard_map/ppermute | solution.py:73
  64.5 0.5 shard_map.210
  65.1 0.8 shard_map.214
  66.1 1.5 %collective-permute-start.27 = (bf16[80,3072]{1,0:T(8,128)(2,1)S(1)}, bf16[80,3072]{1,0:T(8,128)(2,1)S(1)}, u32[]{:S(2)}, u32[]{:S(2)}) collective-permute-start(bf16[80,3072]{1,0:T(8,128)(2,1)S(1)} %get-tuple-element.154), channel_id=1, source_target_pairs={{0,8},{8,0},{16,24},{24,16},{1,9},{9,1},{17,25},{25,17},{2,10},{10... | collective-permute-start | bytes 1474568 | tf_op jit(solution)/shard_map/ppermute | solution.py:73
  67.6 0.9 collective-permute-start.28
  68.5 1.1 collective-permute-start.29
  69.9 5.4 %collective-permute-done.17.b = bf16[128,640]{1,0:T(8,128)(2,1)S(1)} collective-permute-done((bf16[128,640]{1,0:T(8,128)(2,1)S(1)}, bf16[128,640]{1,0:T(8,128)(2,1)S(1)}, u32[]{:S(2)}, u32[]{:S(2)}) %collective-permute-start.17) | collective-permute-done | bytes 163872 | tf_op jit(solution)/shard_map/ppermute | solution.py:73
  75.3 1.4 %collective-permute-start.18 = (bf16[128,640]{1,0:T(8,128)(2,1)S(1)}, bf16[128,640]{1,0:T(8,128)(2,1)S(1)}, u32[]{:S(2)}, u32[]{:S(2)}) collective-permute-start(bf16[128,640]{1,0:T(8,128)(2,1)S(1)} %shard_map.211.refs_0_), channel_id=1, source_target_pairs={{0,2},{1,3},{2,0},{3,1},{4,6},{5,7},{6,4},{7,5},{8,10},{9,11},{10,... | collective-permute-start | bytes 491528 | tf_op jit(solution)/shard_map/ppermute | solution.py:73
  76.8 1.6 %collective-permute-start.21 = (bf16[80,1152]{1,0:T(8,128)(2,1)S(1)}, bf16[80,1152]{1,0:T(8,128)(2,1)S(1)}, u32[]{:S(2)}, u32[]{:S(2)}) collective-permute-start(bf16[80,1152]{1,0:T(8,128)(2,1)S(1)} %get-tuple-element.147), channel_id=1, source_target_pairs={{0,8},{8,0},{16,24},{24,16},{1,9},{9,1},{17,25},{25,17},{2,10},{10... | collective-permute-start | bytes 552968 | tf_op jit(solution)/shard_map/ppermute | solution.py:73
  78.4 1.8 %collective-permute-done.27.refs_1_ = bf16[80,3072]{1,0:T(8,128)(2,1)S(1)} collective-permute-done((bf16[80,3072]{1,0:T(8,128)(2,1)S(1)}, bf16[80,3072]{1,0:T(8,128)(2,1)S(1)}, u32[]{:S(2)}, u32[]{:S(2)}) %collective-permute-start.27) | collective-permute-done | bytes 491552 | tf_op jit(solution)/shard_map/ppermute | solution.py:73
  80.2 1.4 %collective-permute-start.22 = (bf16[80,1152]{1,0:T(8,128)(2,1)S(1)}, bf16[80,1152]{1,0:T(8,128)(2,1)S(1)}, u32[]{:S(2)}, u32[]{:S(2)}) collective-permute-start(bf16[80,1152]{1,0:T(8,128)(2,1)S(1)} %get-tuple-element.148), channel_id=1, source_target_pairs={{0,16},{8,24},{16,0},{24,8},{1,17},{9,25},{17,1},{25,9},{2,18},{10... | collective-permute-start | bytes 552968 | tf_op jit(solution)/shard_map/ppermute | solution.py:73
  81.6 10.1 %collective-permute-done.28.refs_2_ = bf16[80,3072]{1,0:T(8,128)(2,1)S(1)} collective-permute-done((bf16[80,3072]{1,0:T(8,128)(2,1)S(1)}, bf16[80,3072]{1,0:T(8,128)(2,1)S(1)}, u32[]{:S(2)}, u32[]{:S(2)}) %collective-permute-start.28) | collective-permute-done | bytes 491552 | tf_op jit(solution)/shard_map/ppermute | solution.py:73
  91.7 0.7 collective-permute-start.23
  92.9 1.8 %collective-permute-start.30 = (bf16[80,1536]{1,0:T(8,128)(2,1)S(1)}, bf16[80,1536]{1,0:T(8,128)(2,1)S(1)}, u32[]{:S(2)}, u32[]{:S(2)}) collective-permute-start(bf16[80,1536]{1,0:T(8,128)(2,1)S(1)} %get-tuple-element.158), channel_id=1, source_target_pairs={{0,1},{1,0},{2,3},{3,2},{4,5},{5,4},{6,7},{7,6},{8,9},{9,8},{10,11... | collective-permute-start | bytes 737288 | tf_op jit(solution)/shard_map/ppermute | solution.py:73
  95.3 4.0 %collective-permute-done.22.refs_2_ = bf16[80,1152]{1,0:T(8,128)(2,1)S(1)} collective-permute-done((bf16[80,1152]{1,0:T(8,128)(2,1)S(1)}, bf16[80,1152]{1,0:T(8,128)(2,1)S(1)}, u32[]{:S(2)}, u32[]{:S(2)}) %collective-permute-start.22) | collective-permute-done | bytes 184352 | tf_op jit(solution)/shard_map/ppermute | solution.py:73
  99.3 0.7 shard_map.216
  100.0 2.5 %collective-permute-start.26 = (bf16[80,640]{1,0:T(8,128)(2,1)S(1)}, bf16[80,640]{1,0:T(8,128)(2,1)S(1)}, u32[]{:S(2)}, u32[]{:S(2)}) collective-permute-start(bf16[80,640]{1,0:T(8,128)(2,1)S(1)} %get-tuple-element.151.refs_0_), channel_id=1, source_target_pairs={{0,3},{1,2},{2,1},{3,0},{4,7},{5,6},{6,5},{7,4},{8,11},{9,10},{10,... | collective-permute-start | bytes 307208 | tf_op jit(solution)/shard_map/ppermute | solution.py:73
  102.5 1.9 %collective-permute-start.24 = (bf16[80,640]{1,0:T(8,128)(2,1)S(1)}, bf16[80,640]{1,0:T(8,128)(2,1)S(1)}, u32[]{:S(2)}, u32[]{:S(2)}) collective-permute-start(bf16[80,640]{1,0:T(8,128)(2,1)S(1)} %get-tuple-element.151.refs_0_), channel_id=1, source_target_pairs={{0,1},{1,0},{2,3},{3,2},{4,5},{5,4},{6,7},{7,6},{8,9},{9,8},{10,11... | collective-permute-start | bytes 307208 | tf_op jit(solution)/shard_map/ppermute | solution.py:73
  104.4 0.8 shard_map.204
  105.1 0.8 shard_map.219
  106.0 4.9 %collective-permute-done.19.b = bf16[128,640]{1,0:T(8,128)(2,1)S(1)} collective-permute-done((bf16[128,640]{1,0:T(8,128)(2,1)S(1)}, bf16[128,640]{1,0:T(8,128)(2,1)S(1)}, u32[]{:S(2)}, u32[]{:S(2)}) %collective-permute-start.19) | collective-permute-done | bytes 163872 | tf_op jit(solution)/shard_map/ppermute | solution.py:73
  110.9 0.8 shard_map.213
  112.0 0.7 shard_map.217
  (65 shorter events, 3.3 us)
Async XLA Ops:
  0.6 4.5 %copy-start.8 = (f32[4,640]{1,0:T(4,128)S(1)}, f32[4,640]{1,0:T(4,128)}, u32[]{:S(2)}) copy-start(f32[4,640]{1,0:T(4,128)} %gains.5) | copy-start | bytes 30724
  0.7 4.5 %copy-start.9 = (f32[2,256]{1,0:T(2,128)S(1)}, f32[2,256]{1,0:T(2,128)}, u32[]{:S(2)}) copy-start(f32[2,256]{1,0:T(2,128)} %hgains.7) | copy-start | bytes 6148
  0.7 4.5 %copy-start.4 = (bf16[640,512]{1,0:T(8,128)(2,1)S(1)}, bf16[640,512]{1,0:T(8,128)(2,1)}, u32[]{:S(2)}) copy-start(bf16[640,512]{1,0:T(8,128)(2,1)} %wkv.3) | copy-start | bytes 1966084
  0.7 4.5 %copy-start.11 = (s32[4]{0:T(128)S(1)}, s32[4]{0:T(128)}, u32[]{:S(2)}) copy-start(s32[4]{0:T(128)} %refs_0_.3) | copy-start | bytes 52
  0.7 4.5 %copy-start.10 = (s32[1,512]{1,0:T(1,128)S(1)}, s32[1,512]{1,0:T(1,128)}, u32[]{:S(2)}) copy-start(s32[1,512]{1,0:T(1,128)} %pos.1) | copy-start | bytes 6148
  0.7 4.5 %copy-start.3 = (bf16[1,2,128,640]{3,2,1,0:T(8,128)(2,1)S(1)}, bf16[1,2,128,640]{3,2,1,0:T(8,128)(2,1)}, u32[]{:S(2)}) copy-start(bf16[1,2,128,640]{3,2,1,0:T(8,128)(2,1)} %param.12) | copy-start | bytes 983044
  0.7 13.3 %copy-start.6 = (bf16[640,256]{1,0:T(8,128)(2,1)S(1)}, bf16[640,256]{1,0:T(8,128)(2,1)}, u32[]{:S(2)}) copy-start(bf16[640,256]{1,0:T(8,128)(2,1)} %wq.3) | copy-start | bytes 983044
  0.7 13.7 %copy-start.5 = (bf16[256,640]{1,0:T(8,128)(2,1)S(1)}, bf16[256,640]{1,0:T(8,128)(2,1)}, u32[]{:S(2)}) copy-start(bf16[256,640]{1,0:T(8,128)(2,1)} %refs_0_.5) | copy-start | bytes 983044
  1.9 8.6 %collective-permute-start.1 = (bf16[80,1152]{1,0:T(8,128)(2,1)S(1)}, bf16[80,1152]{1,0:T(8,128)(2,1)S(1)}, u32[]{:S(2)}, u32[]{:S(2)}) collective-permute-start(bf16[80,1152]{1,0:T(8,128)(2,1)S(1)} %get-tuple-element.88), channel_id=1, source_target_pairs={{0,1},{1,0},{2,3},{3,2},{4,5},{5,4},{6,7},{7,6},{8,9},{9,8},{10,11... | collective-permute-start | bytes 552968 | tf_op jit(solution)/shard_map/ppermute | solution.py:73
  5.1 12.8 %collective-permute-start = (bf16[320,512]{1,0:T(8,128)(2,1)S(1)}, bf16[320,512]{1,0:T(8,128)(2,1)S(1)}, u32[]{:S(2)}, u32[]{:S(2)}) collective-permute-start(bf16[320,512]{1,0:T(8,128)(2,1)S(1)} %get-tuple-element.87), channel_id=1, source_target_pairs={{0,1},{1,0},{2,3},{3,2},{4,5},{5,4},{6,7},{7,6},{8,9},{9,8},{10,11... | collective-permute-start | bytes 983048 | tf_op jit(solution)/shard_map/ppermute | solution.py:73
  6.6 7.8 %collective-permute-start.8 = (bf16[256,512]{1,0:T(8,128)(2,1)S(1)}, bf16[256,512]{1,0:T(8,128)(2,1)S(1)}, u32[]{:S(2)}, u32[]{:S(2)}) collective-permute-start(bf16[256,512]{1,0:T(8,128)(2,1)S(1)} %get-tuple-element.100.refs_5_.refs_3_), channel_id=1, source_target_pairs={{0,4},{4,0},{1,5},{5,1},{2,6},{6,2},{3,7},{7,3},{8,12},{12,8},{9,1... | collective-permute-start | bytes 786440 | tf_op jit(solution)/shard_map/ppermute | solution.py:73
  10.5 8.3 %collective-permute-start.4 = (bf16[80,1152]{1,0:T(8,128)(2,1)S(1)}, bf16[80,1152]{1,0:T(8,128)(2,1)S(1)}, u32[]{:S(2)}, u32[]{:S(2)}) collective-permute-start(bf16[80,1152]{1,0:T(8,128)(2,1)S(1)} %collective-permute-done.1.refs_0_), channel_id=1, source_target_pairs={{0,24},{8,16},{16,8},{24,0},{1,25},{9,17},{17,9},{25,1},{2,26},{10... | collective-permute-start | bytes 552968 | tf_op jit(solution)/shard_map/ppermute | solution.py:73
  13.4 6.9 %collective-permute-start.3 = (bf16[80,1152]{1,0:T(8,128)(2,1)S(1)}, bf16[80,1152]{1,0:T(8,128)(2,1)S(1)}, u32[]{:S(2)}, u32[]{:S(2)}) collective-permute-start(bf16[80,1152]{1,0:T(8,128)(2,1)S(1)} %collective-permute-done.1.refs_0_), channel_id=1, source_target_pairs={{0,16},{8,24},{16,0},{24,8},{1,17},{9,25},{17,1},{25,9},{2,18},{10... | collective-permute-start | bytes 552968 | tf_op jit(solution)/shard_map/ppermute | solution.py:73
  13.9 6.4 %collective-permute-start.2 = (bf16[80,1152]{1,0:T(8,128)(2,1)S(1)}, bf16[80,1152]{1,0:T(8,128)(2,1)S(1)}, u32[]{:S(2)}, u32[]{:S(2)}) collective-permute-start(bf16[80,1152]{1,0:T(8,128)(2,1)S(1)} %collective-permute-done.1.refs_0_), channel_id=1, source_target_pairs={{0,8},{8,0},{16,24},{24,16},{1,9},{9,1},{17,25},{25,17},{2,10},{10... | collective-permute-start | bytes 552968 | tf_op jit(solution)/shard_map/ppermute | solution.py:73
  15.8 15.9 %copy-start = (bf16[640,512]{1,0:T(8,128)(2,1)S(1)}, bf16[640,512]{1,0:T(8,128)(2,1)}, u32[]{:S(2)}) copy-start(bf16[640,512]{1,0:T(8,128)(2,1)} %refs_5_.1) | copy-start | bytes 1966084
  15.8 15.9 %copy-start.1 = (bf16[640,512]{1,0:T(8,128)(2,1)S(1)}, bf16[640,512]{1,0:T(8,128)(2,1)}, u32[]{:S(2)}) copy-start(bf16[640,512]{1,0:T(8,128)(2,1)} %refs_6_.1) | copy-start | bytes 1966084
  15.8 15.9 %copy-start.2 = (bf16[512,640]{1,0:T(8,128)(2,1)S(1)}, bf16[512,640]{1,0:T(8,128)(2,1)}, u32[]{:S(2)}) copy-start(bf16[512,640]{1,0:T(8,128)(2,1)} %refs_7_.1) | copy-start | bytes 1966084
  15.8 5.4 %collective-permute-start.9 = (bf16[128,640]{1,0:T(8,128)(2,1)S(1)}, bf16[128,640]{1,0:T(8,128)(2,1)S(1)}, u32[]{:S(2)}, u32[]{:S(2)}) collective-permute-start(bf16[128,640]{1,0:T(8,128)(2,1)S(1)} %get-tuple-element.102), channel_id=1, source_target_pairs={{0,1},{1,0},{2,3},{3,2},{4,5},{5,4},{6,7},{7,6},{8,9},{9,8},{10,11... | collective-permute-start | bytes 491528 | tf_op jit(solution)/shard_map/ppermute | solution.py:73
  17.9 6.4 %collective-permute-start.5 = (bf16[320,512]{1,0:T(8,128)(2,1)S(1)}, bf16[320,512]{1,0:T(8,128)(2,1)S(1)}, u32[]{:S(2)}, u32[]{:S(2)}) collective-permute-start(bf16[320,512]{1,0:T(8,128)(2,1)S(1)} %collective-permute-done.refs_0_), channel_id=1, source_target_pairs={{0,4},{4,0},{1,5},{5,1},{2,6},{6,2},{3,7},{7,3},{8,12},{12,8},{9,1... | collective-permute-start | bytes 983048 | tf_op jit(solution)/shard_map/ppermute | solution.py:73
  20.4 3.9 %collective-permute-start.6 = (bf16[320,512]{1,0:T(8,128)(2,1)S(1)}, bf16[320,512]{1,0:T(8,128)(2,1)S(1)}, u32[]{:S(2)}, u32[]{:S(2)}) collective-permute-start(bf16[320,512]{1,0:T(8,128)(2,1)S(1)} %get-tuple-element.89.refs_1_), channel_id=1, source_target_pairs={{0,4},{4,0},{1,5},{5,1},{2,6},{6,2},{3,7},{7,3},{8,12},{12,8},{9,1... | collective-permute-start | bytes 983048 | tf_op jit(solution)/shard_map/ppermute | solution.py:73
  20.5 3.8 %collective-permute-start.7 = (bf16[256,640]{1,0:T(8,128)(2,1)S(1)}, bf16[256,640]{1,0:T(8,128)(2,1)S(1)}, u32[]{:S(2)}, u32[]{:S(2)}) collective-permute-start(bf16[256,640]{1,0:T(8,128)(2,1)S(1)} %get-tuple-element.90.refs_2_), channel_id=1, source_target_pairs={{0,4},{4,0},{1,5},{5,1},{2,6},{6,2},{3,7},{7,3},{8,12},{12,8},{9,1... | collective-permute-start | bytes 983048 | tf_op jit(solution)/shard_map/ppermute | solution.py:73
  21.2 10.5 %collective-permute-start.10 = (bf16[128,640]{1,0:T(8,128)(2,1)S(1)}, bf16[128,640]{1,0:T(8,128)(2,1)S(1)}, u32[]{:S(2)}, u32[]{:S(2)}) collective-permute-start(bf16[128,640]{1,0:T(8,128)(2,1)S(1)} %shard_map.200.refs_8_), channel_id=1, source_target_pairs={{0,2},{1,3},{2,0},{3,1},{4,6},{5,7},{6,4},{7,5},{8,10},{9,11},{10,... | collective-permute-start | bytes 491528 | tf_op jit(solution)/shard_map/ppermute | solution.py:73
  31.7 10.8 %copy-start.7 = (bf16[1,2,128,640]{3,2,1,0:T(8,128)(2,1)S(1)}, bf16[1,2,128,640]{3,2,1,0:T(8,128)(2,1)}, u32[]{:S(2)}) copy-start(bf16[1,2,128,640]{3,2,1,0:T(8,128)(2,1)} %param.23) | copy-start | bytes 983044
  32.9 9.7 %collective-permute-start.11 = (bf16[128,640]{1,0:T(8,128)(2,1)S(1)}, bf16[128,640]{1,0:T(8,128)(2,1)S(1)}, u32[]{:S(2)}, u32[]{:S(2)}) collective-permute-start(bf16[128,640]{1,0:T(8,128)(2,1)S(1)} %get-tuple-element.108.refs_11_), channel_id=1, source_target_pairs={{0,2},{1,3},{2,0},{3,1},{4,6},{5,7},{6,4},{7,5},{8,10},{9,11},{10,... | collective-permute-start | bytes 491528 | tf_op jit(solution)/shard_map/ppermute | solution.py:73
  45.8 10.0 %collective-permute-start.15 = (bf16[320,3072]{1,0:T(8,128)(2,1)S(1)}, bf16[320,3072]{1,0:T(8,128)(2,1)S(1)}, u32[]{:S(2)}, u32[]{:S(2)}) collective-permute-start(bf16[320,3072]{1,0:T(8,128)(2,1)S(1)} %get-tuple-element.123), channel_id=1, source_target_pairs={{0,4},{4,0},{1,5},{5,1},{2,6},{6,2},{3,7},{7,3},{8,12},{12,8},{9,1... | collective-permute-start | bytes 5898248 | tf_op jit(solution)/shard_map/ppermute | solution.py:73
  45.9 9.4 %collective-permute-start.13 = (bf16[128,640]{1,0:T(8,128)(2,1)S(1)}, bf16[128,640]{1,0:T(8,128)(2,1)S(1)}, u32[]{:S(2)}, u32[]{:S(2)}) collective-permute-start(bf16[128,640]{1,0:T(8,128)(2,1)S(1)} %get-tuple-element.112.refs_0_), channel_id=1, source_target_pairs={{0,2},{1,3},{2,0},{3,1},{4,6},{5,7},{6,4},{7,5},{8,10},{9,11},{10,... | collective-permute-start | bytes 491528 | tf_op jit(solution)/shard_map/ppermute | solution.py:73
  55.7 6.2 %collective-permute-start.14 = (bf16[128,640]{1,0:T(8,128)(2,1)S(1)}, bf16[128,640]{1,0:T(8,128)(2,1)S(1)}, u32[]{:S(2)}, u32[]{:S(2)}) collective-permute-start(bf16[128,640]{1,0:T(8,128)(2,1)S(1)} %get-tuple-element.122.refs_5_.da), channel_id=1, source_target_pairs={{0,1},{1,0},{2,3},{3,2},{4,5},{5,4},{6,7},{7,6},{8,9},{9,8},{10,11... | collective-permute-start | bytes 491528 | tf_op jit(solution)/shard_map/ppermute | solution.py:73
  62.9 1.6 %collective-permute-start.16 = (bf16[256,512]{1,0:T(8,128)(2,1)S(1)}, bf16[256,512]{1,0:T(8,128)(2,1)S(1)}, u32[]{:S(2)}, u32[]{:S(2)}) collective-permute-start(bf16[256,512]{1,0:T(8,128)(2,1)S(1)} %get-tuple-element.133), channel_id=1, source_target_pairs={{0,4},{4,0},{1,5},{5,1},{2,6},{6,2},{3,7},{7,3},{8,12},{12,8},{9,1... | collective-permute-start | bytes 786440 | tf_op jit(solution)/shard_map/ppermute | solution.py:73
  65.9 10.7 %collective-permute-start.20 = (bf16[320,1152]{1,0:T(8,128)(2,1)S(1)}, bf16[320,1152]{1,0:T(8,128)(2,1)S(1)}, u32[]{:S(2)}, u32[]{:S(2)}) collective-permute-start(bf16[320,1152]{1,0:T(8,128)(2,1)S(1)} %get-tuple-element.145), channel_id=1, source_target_pairs={{0,4},{4,0},{1,5},{5,1},{2,6},{6,2},{3,7},{7,3},{8,12},{12,8},{9,1... | collective-permute-start | bytes 2211848 | tf_op jit(solution)/shard_map/ppermute | solution.py:73
  66.1 14.1 %collective-permute-start.27 = (bf16[80,3072]{1,0:T(8,128)(2,1)S(1)}, bf16[80,3072]{1,0:T(8,128)(2,1)S(1)}, u32[]{:S(2)}, u32[]{:S(2)}) collective-permute-start(bf16[80,3072]{1,0:T(8,128)(2,1)S(1)} %get-tuple-element.154), channel_id=1, source_target_pairs={{0,8},{8,0},{16,24},{24,16},{1,9},{9,1},{17,25},{25,17},{2,10},{10... | collective-permute-start | bytes 1474568 | tf_op jit(solution)/shard_map/ppermute | solution.py:73
  67.6 24.0 %collective-permute-start.28 = (bf16[80,3072]{1,0:T(8,128)(2,1)S(1)}, bf16[80,3072]{1,0:T(8,128)(2,1)S(1)}, u32[]{:S(2)}, u32[]{:S(2)}) collective-permute-start(bf16[80,3072]{1,0:T(8,128)(2,1)S(1)} %get-tuple-element.155), channel_id=1, source_target_pairs={{0,16},{8,24},{16,0},{24,8},{1,17},{9,25},{17,1},{25,9},{2,18},{10... | collective-permute-start | bytes 1474568 | tf_op jit(solution)/shard_map/ppermute | solution.py:73
  68.5 23.8 %collective-permute-start.29 = (bf16[80,3072]{1,0:T(8,128)(2,1)S(1)}, bf16[80,3072]{1,0:T(8,128)(2,1)S(1)}, u32[]{:S(2)}, u32[]{:S(2)}) collective-permute-start(bf16[80,3072]{1,0:T(8,128)(2,1)S(1)} %get-tuple-element.156), channel_id=1, source_target_pairs={{0,24},{8,16},{16,8},{24,0},{1,25},{9,17},{17,9},{25,1},{2,26},{10... | collective-permute-start | bytes 1474568 | tf_op jit(solution)/shard_map/ppermute | solution.py:73
  69.6 5.6 %collective-permute-start.17 = (bf16[128,640]{1,0:T(8,128)(2,1)S(1)}, bf16[128,640]{1,0:T(8,128)(2,1)S(1)}, u32[]{:S(2)}, u32[]{:S(2)}) collective-permute-start(bf16[128,640]{1,0:T(8,128)(2,1)S(1)} %get-tuple-element.135.send), channel_id=1, source_target_pairs={{0,1},{1,0},{2,3},{3,2},{4,5},{5,4},{6,7},{7,6},{8,9},{9,8},{10,11... | collective-permute-start | bytes 491528 | tf_op jit(solution)/shard_map/ppermute | solution.py:73
  75.3 17.6 %collective-permute-start.18 = (bf16[128,640]{1,0:T(8,128)(2,1)S(1)}, bf16[128,640]{1,0:T(8,128)(2,1)S(1)}, u32[]{:S(2)}, u32[]{:S(2)}) collective-permute-start(bf16[128,640]{1,0:T(8,128)(2,1)S(1)} %shard_map.211.refs_0_), channel_id=1, source_target_pairs={{0,2},{1,3},{2,0},{3,1},{4,6},{5,7},{6,4},{7,5},{8,10},{9,11},{10,... | collective-permute-start | bytes 491528 | tf_op jit(solution)/shard_map/ppermute | solution.py:73
  76.8 18.1 %collective-permute-start.21 = (bf16[80,1152]{1,0:T(8,128)(2,1)S(1)}, bf16[80,1152]{1,0:T(8,128)(2,1)S(1)}, u32[]{:S(2)}, u32[]{:S(2)}) collective-permute-start(bf16[80,1152]{1,0:T(8,128)(2,1)S(1)} %get-tuple-element.147), channel_id=1, source_target_pairs={{0,8},{8,0},{16,24},{24,16},{1,9},{9,1},{17,25},{25,17},{2,10},{10... | collective-permute-start | bytes 552968 | tf_op jit(solution)/shard_map/ppermute | solution.py:73
  80.2 19.1 %collective-permute-start.22 = (bf16[80,1152]{1,0:T(8,128)(2,1)S(1)}, bf16[80,1152]{1,0:T(8,128)(2,1)S(1)}, u32[]{:S(2)}, u32[]{:S(2)}) collective-permute-start(bf16[80,1152]{1,0:T(8,128)(2,1)S(1)} %get-tuple-element.148), channel_id=1, source_target_pairs={{0,16},{8,24},{16,0},{24,8},{1,17},{9,25},{17,1},{25,9},{2,18},{10... | collective-permute-start | bytes 552968 | tf_op jit(solution)/shard_map/ppermute | solution.py:73
  91.7 7.6 %collective-permute-start.23 = (bf16[80,1152]{1,0:T(8,128)(2,1)S(1)}, bf16[80,1152]{1,0:T(8,128)(2,1)S(1)}, u32[]{:S(2)}, u32[]{:S(2)}) collective-permute-start(bf16[80,1152]{1,0:T(8,128)(2,1)S(1)} %get-tuple-element.149), channel_id=1, source_target_pairs={{0,24},{8,16},{16,8},{24,0},{1,25},{9,17},{17,9},{25,1},{2,26},{10... | collective-permute-start | bytes 552968 | tf_op jit(solution)/shard_map/ppermute | solution.py:73
  92.4 10.1 %collective-permute-start.12 = (bf16[128,640]{1,0:T(8,128)(2,1)S(1)}, bf16[128,640]{1,0:T(8,128)(2,1)S(1)}, u32[]{:S(2)}, u32[]{:S(2)}) collective-permute-start(bf16[128,640]{1,0:T(8,128)(2,1)S(1)} %get-tuple-element.109.a), channel_id=1, source_target_pairs={{0,1},{1,0},{2,3},{3,2},{4,5},{5,4},{6,7},{7,6},{8,9},{9,8},{10,11... | collective-permute-start | bytes 491528 | tf_op jit(solution)/shard_map/ppermute | solution.py:73
  92.9 12.2 %collective-permute-start.30 = (bf16[80,1536]{1,0:T(8,128)(2,1)S(1)}, bf16[80,1536]{1,0:T(8,128)(2,1)S(1)}, u32[]{:S(2)}, u32[]{:S(2)}) collective-permute-start(bf16[80,1536]{1,0:T(8,128)(2,1)S(1)} %get-tuple-element.158), channel_id=1, source_target_pairs={{0,1},{1,0},{2,3},{3,2},{4,5},{5,4},{6,7},{7,6},{8,9},{9,8},{10,11... | collective-permute-start | bytes 737288 | tf_op jit(solution)/shard_map/ppermute | solution.py:73
  95.0 15.9 %collective-permute-start.19 = (bf16[128,640]{1,0:T(8,128)(2,1)S(1)}, bf16[128,640]{1,0:T(8,128)(2,1)S(1)}, u32[]{:S(2)}, u32[]{:S(2)}) collective-permute-start(bf16[128,640]{1,0:T(8,128)(2,1)S(1)} %shard_map.212.a), channel_id=1, source_target_pairs={{0,1},{1,0},{2,3},{3,2},{4,5},{5,4},{6,7},{7,6},{8,9},{9,8},{10,11... | collective-permute-start | bytes 491528 | tf_op jit(solution)/shard_map/ppermute | solution.py:73
  100.0 11.7 %collective-permute-start.26 = (bf16[80,640]{1,0:T(8,128)(2,1)S(1)}, bf16[80,640]{1,0:T(8,128)(2,1)S(1)}, u32[]{:S(2)}, u32[]{:S(2)}) collective-permute-start(bf16[80,640]{1,0:T(8,128)(2,1)S(1)} %get-tuple-element.151.refs_0_), channel_id=1, source_target_pairs={{0,3},{1,2},{2,1},{3,0},{4,7},{5,6},{6,5},{7,4},{8,11},{9,10},{10,... | collective-permute-start | bytes 307208 | tf_op jit(solution)/shard_map/ppermute | solution.py:73
  102.5 9.2 %collective-permute-start.25 = (bf16[80,640]{1,0:T(8,128)(2,1)S(1)}, bf16[80,640]{1,0:T(8,128)(2,1)S(1)}, u32[]{:S(2)}, u32[]{:S(2)}) collective-permute-start(bf16[80,640]{1,0:T(8,128)(2,1)S(1)} %get-tuple-element.151.refs_0_), channel_id=1, source_target_pairs={{0,2},{1,3},{2,0},{3,1},{4,6},{5,7},{6,4},{7,5},{8,10},{9,11},{10,... | collective-permute-start | bytes 307208 | tf_op jit(solution)/shard_map/ppermute | solution.py:73
  102.5 9.5 %collective-permute-start.24 = (bf16[80,640]{1,0:T(8,128)(2,1)S(1)}, bf16[80,640]{1,0:T(8,128)(2,1)S(1)}, u32[]{:S(2)}, u32[]{:S(2)}) collective-permute-start(bf16[80,640]{1,0:T(8,128)(2,1)S(1)} %get-tuple-element.151.refs_0_), channel_id=1, source_target_pairs={{0,1},{1,0},{2,3},{3,2},{4,5},{5,4},{6,7},{7,6},{8,9},{9,8},{10,11... | collective-permute-start | bytes 307208 | tf_op jit(solution)/shard_map/ppermute | solution.py:73
where the time goes:
time: 113 us
  waiting for transfers between devices  65.6 us (58%)
  starting transfers between devices  28.7 us (25%)
  Pallas kernels  17.4 us (15%)
    ppermute x31, waiting for transfers between devices, swap(): return lax.ppermute(x, axis, [(i, i ^ k) for i in range(size)])  65.6 us
    ppermute x31, starting transfers between devices, swap(): return lax.ppermute(x, axis, [(i, i ^ k) for i in range(size)])  28.7 us
    pallas_call x25, Pallas kernels, kernel_call(): pl.pallas_call(body, out_shape=[jax.ShapeDtypeStruct(s, d) for s, d in ou...  16.2 us
  transfers between devices with their start and end apart: 31, of which 15 were waited for; matrix products, arithmetic and copies ran while one was open for 0% of the time, Pallas kernels for 8%

commit v1 on v0

--- a/solution.py
+++ b/solution.py
@@ -2,6 +2,7 @@
 
 import jax
 import jax.numpy as jnp
+import numpy as np
 from jax import lax
 from jax.experimental import pallas as pl
 from jax.experimental.pallas import tpu as pltpu
@@ -52,19 +53,24 @@
     return lax.dot_general(left, right, (((1,), (1,)), ((), ())), preferred_element_type=f32)
 
 
-def kernel_call(body, args, outs, scratch=(), tables=0, flops=0):
+def kernel_call(body, args, outs, scratch=(), tables=0, in_hbm=0):
     moved = sum(a.size * a.dtype.itemsize for a in args)
     moved += sum(functools.reduce(lambda m, n: m * n, s, 1) * jnp.dtype(d).itemsize for s, d in outs)
-    work = sum(functools.reduce(lambda m, n: m * n, s.shape, 1) * jnp.dtype(s.dtype).itemsize for s in scratch)
+    work = sum(
+        functools.reduce(lambda m, n: m * n, s.shape, 1) * jnp.dtype(s.dtype).itemsize
+        for s in scratch
+        if s.dtype in (f32, bf16)
+    )
     limit = min(60 << 20, (8 << 20) + 2 * (moved + work))
     return pl.pallas_call(
         body,
         out_shape=[jax.ShapeDtypeStruct(s, d) for s, d in outs],
         in_specs=[pl.BlockSpec(memory_space=pltpu.SMEM)] * tables
-        + [pl.BlockSpec(memory_space=pltpu.VMEM)] * (len(args) - tables),
+        + [pl.BlockSpec(memory_space=pltpu.VMEM)] * (len(args) - tables - in_hbm)
+        + [pl.BlockSpec(memory_space=pltpu.HBM)] * in_hbm,
         out_specs=[pl.BlockSpec(memory_space=pltpu.VMEM)] * len(outs),
         scratch_shapes=list(scratch),
-        cost_estimate=pl.CostEstimate(flops=flops, bytes_accessed=moved, transcendentals=0),
+        cost_estimate=pl.CostEstimate(flops=0, bytes_accessed=moved, transcendentals=0),
         compiler_params=pltpu.CompilerParams(vmem_limit_bytes=limit),
     )(*args)
 
@@ -114,7 +120,7 @@
 
     hidden = hidden_in.reshape(rows, width)
     cot = out_cotangent.reshape(rows, width)
-    freq = (rope_base ** (-(jnp.arange(half, dtype=f32) * 2.0 / head_dim))).reshape(1, half)
+    freq = jnp.asarray(rope_base ** (-np.arange(half) * 2.0 / head_dim), f32).reshape(1, half)
 
     def part(k):
         return slice(k * share, (k + 1) * share)
@@ -153,60 +159,25 @@
     down_piece = ff // (2 * n_batch)
     piece_rows = max(up_piece, down_piece)
 
-    def pack_body(gate, up, down, gate_o, piece_o, sem):
+    def pre_body(*refs):
+        sources, (gate, up, down) = refs[:7], refs[7:10]
+        normed_o, kv_o, unit_o, scale_o, cos_o, sin_o, idx_o, start_o, gate_o, piece_o = refs[10:20]
+        col_pos, col_idx, sem = refs[20:23]
+        table, hid, pos, gains, hgains, freqs, wkv = refs[23:]
+        loads = [pltpu.make_async_copy(a, b, sem.at[i]) for i, (a, b) in enumerate(zip(sources, refs[23:]))]
+        moves = [
+            pltpu.make_async_copy(up.at[own_piece(width), :], piece_o.at[:up_piece, :ff], sem.at[7]),
+            pltpu.make_async_copy(down.at[own_piece(ff), :], piece_o.at[:down_piece, ff:], sem.at[8]),
+            pltpu.make_async_copy(gate.at[own_half(width), :], gate_o, sem.at[9]),
+        ]
+        for move in loads + moves:
+            move.start()
         if up_piece < piece_rows:
             piece_o[up_piece:, :ff] = jnp.zeros((piece_rows - up_piece, ff), bf16)
         if down_piece < piece_rows:
             piece_o[down_piece:, ff:] = jnp.zeros((piece_rows - down_piece, width), bf16)
-        moves = [
-            pltpu.make_async_copy(up.at[own_piece(width), :], piece_o.at[:up_piece, :ff], sem.at[0]),
-            pltpu.make_async_copy(down.at[own_piece(ff), :], piece_o.at[:down_piece, ff:], sem.at[1]),
-            pltpu.make_async_copy(gate.at[own_half(width), :], gate_o, sem.at[2]),
-        ]
-        for move in moves:
-            move.start()
-        for move in moves:
-            move.wait()
-
-    gate_pack, piece_pack = pl.pallas_call(
-        pack_body,
-        out_shape=[jax.ShapeDtypeStruct((width // 2, ff), bf16), jax.ShapeDtypeStruct((piece_rows, ff + width), bf16)],
-        in_specs=[pl.BlockSpec(memory_space=pltpu.HBM)] * 3,
-        out_specs=[pl.BlockSpec(memory_space=pltpu.VMEM)] * 2,
-        scratch_shapes=[pltpu.SemaphoreType.DMA((3,))],
-        name="pack",
-        compiler_params=pltpu.CompilerParams(vmem_limit_bytes=16 << 20),
-    )(*(pltpu.with_memory_space_constraint(w, pltpu.HBM) for w in (gate_weight, up_weight, down_weight)))
-    gate_near = neighbour(gate_pack)
-    piece_near = neighbour(piece_pack)
-    pieces = [piece_near] + [swap(piece_near, "batch", n_batch, k) for k in range(1, n_batch)]
-
-    def stack_body(*refs):
-        up_o, down_o = refs[n_batch:]
-        for k in range(n_batch):
-            b = lax.axis_index("batch") ^ k
-            up_o[pl.ds(pl.multiple_of(b * up_piece, up_piece), up_piece), :] = refs[k][:up_piece, :ff]
-            down_o[pl.ds(pl.multiple_of(b * down_piece, down_piece), down_piece), :] = refs[k][
-                :down_piece, ff:
-            ]
-
-    up_near, down_near = kernel_call(stack_body, tuple(pieces), [((width // 2, ff), bf16), ((ff // 2, width), bf16)])
-
-    def whole_body(*refs):
-        for mine, far, whole in zip(refs[:3], refs[3:6], refs[6:]):
-            length = mine.shape[0]
-            for k, ref in enumerate((mine, far)):
-                place = ((lax.axis_index("ctx") & 1) ^ k) * length
-                whole[pl.ds(pl.multiple_of(place, length), length), :] = ref[...]
-
-    halves = (gate_near, up_near, down_near)
-    near_weights = kernel_call(
-        whole_body,
-        halves + tuple(other_core(h) for h in halves),
-        [((width, ff), bf16), ((width, ff), bf16), ((ff, width), bf16)],
-    )
-
-    def pre_body(table, hid, pos, gains, hgains, freqs, wkv, normed_o, kv_o, unit_o, scale_o, cos_o, sin_o, idx_o, start_o, col_pos, col_idx):
+        for load in loads:
+            load.wait()
         eye = lax.broadcasted_iota(jnp.int32, (block_len, block_len), 0) == lax.broadcasted_iota(
             jnp.int32, (block_len, block_len), 1
         )
@@ -235,10 +206,16 @@
         scale_o[...] = scale
         kv_o[:, :head_dim] = rotate(unit * hgains[1:2, :], cos_o[...], sin_o[...]).astype(bf16)
         kv_o[:, head_dim:] = kv[:, head_dim:].astype(bf16)
-
-    normed, kv_mine, unit_k, scale_k, cosine, sine, idx, start = kernel_call(
+        for move in moves:
+            move.wait()
+
+    sources = (block_table, hidden, positions, norm_gains, head_norm_gains, freq, key_value_weight)
+    normed, kv_mine, unit_k, scale_k, cosine, sine, idx, start, gate_pack, piece_pack = kernel_call(
         pre_body,
-        (block_table, hidden, positions, norm_gains, head_norm_gains, freq, key_value_weight),
+        tuple(
+            pltpu.with_memory_space_constraint(x, pltpu.HBM)
+            for x in (*sources, gate_weight, up_weight, down_weight)
+        ),
         [
             ((rows, width), bf16),
             ((rows, 2 * head_dim), bf16),
@@ -248,9 +225,42 @@
             ((rows, half), f32),
             ((rows, 1), f32),
             ((rows, 1), f32),
+            ((width // 2, ff), bf16),
+            ((piece_rows, ff + width), bf16),
         ],
-        scratch=[pltpu.VMEM((rows, 1), f32), pltpu.VMEM((rows, 1), f32)],
-        tables=1,
+        scratch=[pltpu.VMEM((rows, 1), f32), pltpu.VMEM((rows, 1), f32), pltpu.SemaphoreType.DMA((10,))]
+        + [pltpu.SMEM(block_table.shape, block_table.dtype)]
+        + [pltpu.VMEM(x.shape, x.dtype) for x in sources[1:]],
+        in_hbm=10,
+    )
+
+    gate_near = neighbour(gate_pack)
+    piece_near = neighbour(piece_pack)
+    pieces = [piece_near] + [swap(piece_near, "batch", n_batch, k) for k in range(1, n_batch)]
+
+    def stack_body(*refs):
+        up_o, down_o = refs[n_batch:]
+        for k in range(n_batch):
+            b = lax.axis_index("batch") ^ k
+            up_o[pl.ds(pl.multiple_of(b * up_piece, up_piece), up_piece), :] = refs[k][:up_piece, :ff]
+            down_o[pl.ds(pl.multiple_of(b * down_piece, down_piece), down_piece), :] = refs[k][
+                :down_piece, ff:
+            ]
+
+    up_near, down_near = kernel_call(stack_body, tuple(pieces), [((width // 2, ff), bf16), ((ff // 2, width), bf16)])
+
+    def whole_body(*refs):
+        for mine, far, whole in zip(refs[:3], refs[3:6], refs[6:]):
+            length = mine.shape[0]
+            for k, ref in enumerate((mine, far)):
+                place = ((lax.axis_index("ctx") & 1) ^ k) * length
+                whole[pl.ds(pl.multiple_of(place, length), length), :] = ref[...]
+
+    halves = (gate_near, up_near, down_near)
+    near_weights = kernel_call(
+        whole_body,
+        halves + tuple(other_core(h) for h in halves),
+        [((width, ff), bf16), ((width, ff), bf16), ((ff, width), bf16)],
     )
 
     if paired:
@@ -347,7 +357,9 @@
         hid, gains = refs[:2]
         groups = ff_groups(refs[2:8])
         attn = summed(refs[8 : 8 + n_terms])
-        unit_o, scale_o, mixed_o, x_o, act_o, gate_o, up_o, send_o = refs[8 + n_terms :]
+        unit_o, scale_o, mixed_o, x_o = refs[8 + n_terms : 12 + n_terms]
+        act_o = refs[12 + n_terms : 14 + n_terms]
+        gate_o, up_o, send_o = refs[14 + n_terms :]
         scale = rms_scale(attn)
         unit = attn * scale
         mixed = hid[own_rows(0), :].astype(f32) + unit * gains[1:2, :]
@@ -357,7 +369,7 @@
         x = (mixed * rms_scale(mixed) * gains[2:3, :]).astype(bf16)
         x_o[...] = x
         total = None
-        for wg, wu, wd, cols in groups:
+        for k, (wg, wu, wd, cols) in enumerate(groups):
             gate = product(x, wg)
             up = product(x, wu)
             gate_o[:, cols] = gate
@@ -366,10 +378,10 @@
             act = (0.5 * gate * (1.0 + jnp.tanh(inner)) * up).astype(bf16)
             term = product(act, wd)
             total = term if total is None else total + term
-            act_o[:, cols] = act
+            act_o[k][...] = act
         send_o[...] = total.astype(bf16)
 
-    unit_a, scale_a, mixed, ff_in, activated, gate, up, ff_send = kernel_call(
+    unit_a, scale_a, mixed, ff_in, act_mine, act_send, gate, up, ff_send = kernel_call(
         feed_body,
         (hidden, norm_gains, *weights, *attn_terms),
         [
@@ -377,13 +389,15 @@
             ((share, 1), f32),
             ((share, width), f32),
             ((share, width), bf16),
-            ((share, 2 * ff), bf16),
+            ((share, ff), bf16),
+            ((share, ff), bf16),
             ((share, 2 * ff), f32),
             ((share, 2 * ff), f32),
             ((share, width), bf16),
         ],
     )
     ff_terms = exchanged(ff_send)
+    act_near = neighbour(act_send)
 
     def slope_body(gate_r, up_r, gelu_o, slope_o):
         v = gate_r[...]
@@ -434,6 +448,7 @@
     )
     dffin_terms = exchanged(dff_send)
     hidden_near = neighbour(hidden_mine)
+    d_ff_near = neighbour(d_ff_out)
 
     def arrange(acc, outs):
         if not paired:
@@ -448,40 +463,53 @@
                     pl.ds(pl.multiple_of(first, out_rows), out_rows), :
                 ].astype(bf16)
 
-    def grad_call(body, args, columns):
-        if paired:
-            outs = [((n_batch * out_rows, columns), bf16)] * 2
-        else:
-            outs = [((width, columns), f32)]
-        return kernel_call(body, args, outs, scratch=[pltpu.VMEM((width, columns), f32)])
-
-    def reduce_grads(grads):
+    def grad_call(fill, args, *columns):
+        count = 2 if paired else 1
+
+        def body(*refs):
+            accs = refs[len(args) + count * len(columns) :]
+            fill(*refs[: len(args)], *accs)
+            for k, acc in enumerate(accs):
+                at = len(args) + count * k
+                arrange(acc, refs[at : at + count])
+
+        outs = []
+        for c in columns:
+            outs += [((n_batch * out_rows, c), bf16)] * 2 if paired else [((width, c), f32)]
+        terms = kernel_call(body, args, outs, scratch=[pltpu.VMEM((width, c), f32) for c in columns])
+        return [terms[count * k : count * (k + 1)] for k in range(len(columns))]
+
+    def reduce_grads(*grads):
         if not paired:
-            return [lax.psum_scatter(grads[0], ("batch", "ctx"), scatter_dimension=0, tiled=True)]
-        keep, send = grads
-        columns = keep.shape[1]
-        got = other_core(send)
-
-        def add_body(a, b, *outs):
-            total = a[...].astype(f32) + b[...].astype(f32)
-            for k in range(n_batch):
-                outs[k][...] = total[k * out_rows : (k + 1) * out_rows].astype(outs[k].dtype)
+            sums = [
+                lax.psum_scatter(g[0], ("batch", "ctx"), scatter_dimension=0, tiled=True) for g in grads
+            ]
+            return [jnp.concatenate(sums, axis=1)]
+        columns = sum(g[0].shape[1] for g in grads)
+        pairs = [x for keep, send in grads for x in (keep, other_core(send))]
+
+        def add_body(*refs):
+            at = 0
+            for a, b in zip(refs[: len(pairs) : 2], refs[1 : len(pairs) : 2]):
+                total = a[...].astype(f32) + b[...].astype(f32)
+                cols = slice(at, at + total.shape[1])
+                at = cols.stop
+                for k, out in enumerate(refs[len(pairs) :]):
+                    out[:, cols] = total[k * out_rows : (k + 1) * out_rows].astype(out.dtype)
 
         parts = kernel_call(
-            add_body, (keep, got), [((out_rows, columns), f32)] + [((out_rows, columns), bf16)] * (n_batch - 1)
+            add_body, tuple(pairs), [((out_rows, columns), f32)] + [((out_rows, columns), bf16)] * (n_batch - 1)
         )
         return [parts[0]] + [swap(parts[k], "batch", n_batch, k) for k in range(1, n_batch)]
 
-    def ff_grad_body(x, d_out, act, dgate, dup, *refs):
-        acc = refs[-1]
-        for at, left, right in ((0, x, dgate), (1, x, dup), (2, d_out, act)):
-            total = lead_product(left[...], right[...])
-            acc[:, at * ff : (at + 1) * ff] = total[:, :ff]
-            acc[:, (3 + at) * ff : (4 + at) * ff] = total[:, ff:]
-        arrange(acc, refs[:-1])
-
-    ff_grads = grad_call(ff_grad_body, (ff_in, d_ff_out, activated, d_gate, d_up), 6 * ff)
-    mid_terms = reduce_grads(ff_grads)
+    def ff_grad_fill(x, dgate, dup, near_acc, own_acc):
+        for at, right in enumerate((dgate, dup)):
+            total = lead_product(x[...], right[...])
+            own_acc[:, at * ff : (at + 1) * ff] = total[:, :ff]
+            near_acc[:, at * ff : (at + 1) * ff] = total[:, ff:]
+
+    near_grads, own_grads = grad_call(ff_grad_fill, (ff_in, d_gate, d_up), 2 * ff, 2 * ff)
+    mid_terms = reduce_grads(near_grads)
 
     def mix_back_body(gains, mixed_r, unit_r, scale_r, cot_r, *refs):
         d_in = summed(refs[:n_terms])
@@ -498,7 +526,7 @@
 
     d_mixed, dattn_mine, gain_f, gain_a = kernel_call(
         mix_back_body,
-        (norm_gains, mixed, unit_a, scale_a, cot, dffin_terms[0], *(after(t, ff_grads[0]) for t in dffin_terms[1:])),
+        (norm_gains, mixed, unit_a, scale_a, cot, dffin_terms[0], *(after(t, near_grads[0]) for t in dffin_terms[1:])),
         [((share, width), f32), ((share, width), bf16), ((1, width), f32), ((1, width), f32)],
     )
     d_attn = (dattn_mine, after(neighbour(dattn_mine), mid_terms[0]))
@@ -590,33 +618,41 @@
     dn_terms = exchanged(meet(dn_mine, neighbour(dn_send)))
 
     def mid_body(*refs):
-        count = len(mid_terms)
-        total = summed(refs[:count])
-        refs[count][...] = total[:, : 3 * ff]
-        refs[count + 1][...] = total[:, 3 * ff :].astype(bf16)
-
-    mid_mine, mid_send = kernel_call(
-        mid_body, tuple(mid_terms), [((out_rows, 3 * ff), f32), ((out_rows, 3 * ff), bf16)]
-    )
-
-    def ff_out_body(mine, near, *outs):
-        for k in range(3):
-            cols = slice(k * ff, (k + 1) * ff)
-            outs[k][...] = mine[:, cols] + near[:, cols].astype(f32)
-
-    gate_grad, up_grad, down_grad = kernel_call(
-        ff_out_body, (mid_mine, neighbour(mid_send)), [((out_rows, ff), f32)] * 3
+        refs[-1][...] = summed(refs[:-1]).astype(bf16)
+
+    (mid_send,) = kernel_call(mid_body, tuple(mid_terms), [((out_rows, 2 * ff), bf16)])
+    mid_near = neighbour(mid_send)
+
+    def down_grad_fill(dff, dff_near, act, act_r, acc):
+        acc[...] = lead_product(joined((dff, dff_near)), joined((act, act_r)))
+
+    def out_grad_fill(da, da_near, ctx_r, acc):
+        acc[...] = lead_product(joined((da, da_near)), ctx_r[...])
+
+    side_terms = reduce_grads(
+        own_grads,
+        *grad_call(down_grad_fill, (d_ff_out, d_ff_near, act_mine, act_near), ff),
+        *grad_call(out_grad_fill, (*d_attn, context), q_width),
+    )
+
+    def side_body(*refs):
+        total = summed(refs[: len(side_terms)])
+        near, gate_o, up_o, down_o, out_o = refs[len(side_terms) :]
+        gate_o[...] = total[:, :ff] + near[:, :ff].astype(f32)
+        up_o[...] = total[:, ff : 2 * ff] + near[:, ff:].astype(f32)
+        down_o[...] = total[:, 2 * ff : 3 * ff]
+        out_o[...] = total[:, 3 * ff :]
+
+    gate_grad, up_grad, down_grad, out_grad = kernel_call(
+        side_body, (*side_terms, mid_near), [((out_rows, ff), f32)] * 3 + [((out_rows, q_width), f32)]
     )
 
     lanes = 128
     kv_at = q_width
     gain_at = q_width + 2 * head_dim
-    out_at = gain_at + lanes
-
-    def last_grad_body(nrm, draw, dkv, hid, g_o, g_f, g_a, g_q, g_k, mine, send, ctx_r, da, da_near, *refs):
-        acc = refs[-1]
+
+    def last_grad_fill(nrm, draw, dkv, hid, g_o, g_f, g_a, g_q, g_k, mine, send, acc):
         acc[:, :kv_at] = lead_product(nrm[...], draw[...])
-        acc[:, out_at:] = lead_product(joined((da, da_near)), ctx_r[...])
         acc[:, kv_at:gain_at] = lead_product(nrm[...], dkv[...])
         g_in = jnp.zeros((1, width), f32)
         for k, terms in enumerate((mine, send)):
@@ -626,19 +662,18 @@
         packed = jnp.where(line == 0, g_in, 0.0)
         for at, row in enumerate((g_a, g_f, g_o), 1):
             packed = jnp.where(line == at, row[...], packed)
-        acc[:, gain_at:out_at] = packed.T
+        acc[:, gain_at:] = packed.T
         line = lax.broadcasted_iota(jnp.int32, (lanes, head_dim), 0)
         packed = jnp.where(line == 4, g_q[...], jnp.where(line == 5, g_k[...], 0.0)).T
         for d in range(shards):
             at = slice(d * out_rows, d * out_rows + head_rows)
-            acc[at, gain_at:out_at] = acc[at, gain_at:out_at] + packed[d * head_rows : (d + 1) * head_rows]
-        arrange(acc, refs[:-1])
+            acc[at, gain_at:] = acc[at, gain_at:] + packed[d * head_rows : (d + 1) * head_rows]
 
     last_terms = reduce_grads(
-        grad_call(
-            last_grad_body,
-            (normed, d_query_raw, d_kv_raw, hidden, gain_o, gain_f, gain_a, gain_q, gain_k, dn_mine, dn_send, context, *d_attn),
-            out_at + q_width,
+        *grad_call(
+            last_grad_fill,
+            (normed, d_query_raw, d_kv_raw, hidden, gain_o, gain_f, gain_a, gain_q, gain_k, dn_mine, dn_send),
+            gain_at + lanes,
         ),
     )
 
@@ -646,13 +681,10 @@
         count = len(last_terms)
         total = summed(refs[:count])
         refs[count][...] = total[:, :kv_at]
-        refs[count + 1][...] = total[:, kv_at:out_at].astype(bf16)
-        refs[count + 2][...] = total[:, out_at:]
-
-    query_grad, kv_mine_sum, out_grad = kernel_call(
-        last_body,
-        tuple(last_terms),
-        [((out_rows, q_width), f32), ((out_rows, 2 * head_dim + lanes), bf16), ((out_rows, q_width), f32)],
+        refs[count + 1][...] = total[:, kv_at:].astype(bf16)
+
+    query_grad, kv_mine_sum = kernel_call(
+        last_body, tuple(last_terms), [((out_rows, q_width), f32), ((out_rows, 2 * head_dim + lanes), bf16)]
     )
     kv_sums = [kv_mine_sum] + [swap(kv_mine_sum, "tp", n_tp, k) for k in range(1, n_tp)]
 

time: 113 us -> 117 us (1.035)
  starting transfers between devices: 28.7 us -> 31.8 us
  local copies, waits for them, and re-layouts: 0.06 us -> 1.39 us
    ppermute x31 -> x39, starting transfers between devices: 28.7 us -> 31.8 us  [swap(): return lax.ppermute(x, axis, [(i, i ^ k) for i in range(size)])]
    unnamed x24 -> x22, local copies, waits for them, and re-layouts: 0.06 us -> 1.39 us
    pallas_call x1 -> x0, Pallas kernels: 1.2 us -> none  [on_device(): pl.pallas_call(pack_body, out_shape=[jax.ShapeDtypeStruct((width // 2, ff...]
    pallas_call x25 -> x28, Pallas kernels: 16.2 us -> 16.9 us  [kernel_call(): pl.pallas_call(body, out_shape=[jax.ShapeDtypeStruct(s, d) for s, d in ou...]
    ppermute x31 -> x39, waiting for transfers between devices: 65.6 us -> 65.9 us  [swap(): return lax.ppermute(x, axis, [(i, i ^ k) for i in range(size)])]
  transfers between devices with their start and end apart: 31 -> 39, of which waited for: 15 -> 17; matrix products, arithmetic and copies ran while one was open for 0% -> 0% of each run, Pallas kernels for 8% -> 8%
where the time goes in v1:
time: 117 us
  waiting for transfers between devices  65.9 us (56%)
  starting transfers between devices  31.8 us (27%)
  Pallas kernels  16.9 us (14%)
  local copies, waits for them, and re-layouts  1.39 us (1%)
    ppermute x39, waiting for transfers between devices, swap(): return lax.ppermute(x, axis, [(i, i ^ k) for i in range(size)])  65.9 us
    ppermute x39, starting transfers between devices, swap(): return lax.ppermute(x, axis, [(i, i ^ k) for i in range(size)])  31.8 us
    pallas_call x28, Pallas kernels, kernel_call(): pl.pallas_call(body, out_shape=[jax.ShapeDtypeStruct(s, d) for s, d in ou...  16.9 us
  transfers between devices with their start and end apart: 39, of which 17 were waited for; matrix products, arithmetic and copies ran while one was open for 0% of the time, Pallas kernels for 8%

profile of v1, /device:TPU:0, one launch (start us, length us, event | category | flops | bytes accessed | tf_op | source)
XLA Modules:
  0.0 117.0 jit_solution(4869926394112162474)
XLA Ops:
  0.7 2.3 %shard_map.204 = (bf16[256,640]{1,0:T(8,128)(2,1)S(1)}, bf16[256,512]{1,0:T(8,128)(2,1)S(1)}, f32[256,256]{1,0:T(8,128)S(1)}, f32[256,1]{1,0:T(8,128)S(1)}, f32[...) custom-call(s32[4]{0:T(128)} %refs_0_.5, ...), custom_call_target="tpu_custom_call" | custom-call | bytes 4593168 | tf_op jit(solution)/shard_map/pallas_call | solution.py:65
  2.9 3.1 %collective-permute-start.1 = (bf16[80,1152]{1,0:T(8,128)(2,1)S(1)}, bf16[80,1152]{1,0:T(8,128)(2,1)S(1)}, u32[]{:S(2)}, u32[]{:S(2)}) collective-permute-start(bf16[80,1152]{1,0:T(8,128)(2,1)S(1)} %get-tuple-element.97), channel_id=1, source_target_pairs={{0,1},{1,0},{2,3},{3,2},{4,5},{5,4},{6,7},{7,6},{8,9},{9,8},{10,11... | collective-permute-start | bytes 552968 | tf_op jit(solution)/shard_map/ppermute | solution.py:79
  6.2 5.4 %collective-permute-done.1.refs_0_ = bf16[80,1152]{1,0:T(8,128)(2,1)S(1)} collective-permute-done((bf16[80,1152]{1,0:T(8,128)(2,1)S(1)}, bf16[80,1152]{1,0:T(8,128)(2,1)S(1)}, u32[]{:S(2)}, u32[]{:S(2)}) %collective-permute-start.1) | collective-permute-done | bytes 184352 | tf_op jit(solution)/shard_map/ppermute | solution.py:79
  11.6 2.9 %collective-permute-start.4 = (bf16[80,1152]{1,0:T(8,128)(2,1)S(1)}, bf16[80,1152]{1,0:T(8,128)(2,1)S(1)}, u32[]{:S(2)}, u32[]{:S(2)}) collective-permute-start(bf16[80,1152]{1,0:T(8,128)(2,1)S(1)} %collective-permute-done.1.refs_0_), channel_id=1, source_target_pairs={{0,24},{8,16},{16,8},{24,0},{1,25},{9,17},{17,9},{25,1},{2,26},{10... | collective-permute-start | bytes 552968 | tf_op jit(solution)/shard_map/ppermute | solution.py:79
  15.1 0.7 copy-done.9
  16.1 0.6 copy-done.5
  16.8 1.3 %shard_map.208 = (f32[1,256,512]{2,1,0:T(8,128)S(1)}, bf16[256,256]{1,0:T(8,128)(2,1)S(1)}, f32[128,640]{1,0:T(8,128)S(1)}, bf16[128,640]{1,0:T(8,128)(2,1)S(1)}) custom-call(s32[4]{0:T(128)S(1)} %copy-done.10, bf16[256,256]{1,0:T(8,128)(2,1)S(1)} %get-tuple-element.106.refs_1_.refs_2_, f32[256,1]{1,0:T(8,128)S(1)} %get-tuple-element.107.refs_2_, ...), custom_call_target="tpu_custom_call" | custom-call | bytes 2131984 | tf_op jit(solution)/shard_map/pallas_call | solution.py:65
  18.1 2.1 %collective-permute-start.9 = (bf16[128,640]{1,0:T(8,128)(2,1)S(1)}, bf16[128,640]{1,0:T(8,128)(2,1)S(1)}, u32[]{:S(2)}, u32[]{:S(2)}) collective-permute-start(bf16[128,640]{1,0:T(8,128)(2,1)S(1)} %get-tuple-element.111), channel_id=1, source_target_pairs={{0,1},{1,0},{2,3},{3,2},{4,5},{5,4},{6,7},{7,6},{8,9},{9,8},{10,11... | collective-permute-start | bytes 491528 | tf_op jit(solution)/shard_map/ppermute | solution.py:79
  20.2 1.1 collective-permute-done.3.refs_2_
  22.0 1.5 %collective-permute-done.9.b = bf16[128,640]{1,0:T(8,128)(2,1)S(1)} collective-permute-done((bf16[128,640]{1,0:T(8,128)(2,1)S(1)}, bf16[128,640]{1,0:T(8,128)(2,1)S(1)}, u32[]{:S(2)}, u32[]{:S(2)}) %collective-permute-start.9) | collective-permute-done | bytes 163872 | tf_op jit(solution)/shard_map/ppermute | solution.py:79
  23.6 3.1 %collective-permute-start.10 = (bf16[128,640]{1,0:T(8,128)(2,1)S(1)}, bf16[128,640]{1,0:T(8,128)(2,1)S(1)}, u32[]{:S(2)}, u32[]{:S(2)}) collective-permute-start(bf16[128,640]{1,0:T(8,128)(2,1)S(1)} %shard_map.209.refs_8_), channel_id=1, source_target_pairs={{0,2},{1,3},{2,0},{3,1},{4,6},{5,7},{6,4},{7,5},{8,10},{9,11},{10,... | collective-permute-start | bytes 491528 | tf_op jit(solution)/shard_map/ppermute | solution.py:79
  26.9 5.9 %collective-permute-done.10.refs_9_ = bf16[128,640]{1,0:T(8,128)(2,1)S(1)} collective-permute-done((bf16[128,640]{1,0:T(8,128)(2,1)S(1)}, bf16[128,640]{1,0:T(8,128)(2,1)S(1)}, u32[]{:S(2)}, u32[]{:S(2)}) %collective-permute-start.10) | collective-permute-done | bytes 163872 | tf_op jit(solution)/shard_map/ppermute | solution.py:79
  32.8 1.1 shard_map.210
  34.7 8.8 %collective-permute-done.11.refs_12_ = bf16[128,640]{1,0:T(8,128)(2,1)S(1)} collective-permute-done((bf16[128,640]{1,0:T(8,128)(2,1)S(1)}, bf16[128,640]{1,0:T(8,128)(2,1)S(1)}, u32[]{:S(2)}, u32[]{:S(2)}) %collective-permute-start.11) | collective-permute-done | bytes 163872 | tf_op jit(solution)/shard_map/ppermute | solution.py:79
  43.5 1.7 %shard_map.212 = (bf16[128,640]{1,0:T(8,128)(2,1)S(1)}, f32[1,640]{1,0:T(1,128)S(1)}, bf16[128,640]{1,0:T(8,128)(2,1)S(1)}, bf16[128,1024]{1,0:T(8,128)(2,1)S(1)...) custom-call(f32[4,640]{1,0:T(4,128)S(1)} %copy-done.8, f32[128,640]{1,0:T(8,128)S(1)} %get-tuple-element.112.refs_1_.mixed_r, ...), custom_call_target="tpu_custom_call" | custom-call | bytes 6992384 | tf_op jit(solution)/shard_map/pallas_call | solution.py:65
  45.1 1.0 shard_map.214
  46.3 9.7 %collective-permute-done.13.refs_1_ = bf16[128,640]{1,0:T(8,128)(2,1)S(1)} collective-permute-done((bf16[128,640]{1,0:T(8,128)(2,1)S(1)}, bf16[128,640]{1,0:T(8,128)(2,1)S(1)}, u32[]{:S(2)}, u32[]{:S(2)}) %collective-permute-start.13) | collective-permute-done | bytes 163872 | tf_op jit(solution)/shard_map/ppermute | solution.py:79
  56.7 6.0 %collective-permute-done.14.refs_6_.refs_1_ = bf16[128,640]{1,0:T(8,128)(2,1)S(1)} collective-permute-done((bf16[128,640]{1,0:T(8,128)(2,1)S(1)}, bf16[128,640]{1,0:T(8,128)(2,1)S(1)}, u32[]{:S(2)}, u32[]{:S(2)}) %collective-permute-start.14) | collective-permute-done | bytes 163872 | tf_op jit(solution)/shard_map/ppermute | solution.py:79
  62.7 1.0 shard_map.217
  65.3 0.5 shard_map.219
  65.8 0.7 shard_map.223
  66.7 1.4 %collective-permute-start.29 = (bf16[128,512]{1,0:T(8,128)(2,1)S(1)}, bf16[128,512]{1,0:T(8,128)(2,1)S(1)}, u32[]{:S(2)}, u32[]{:S(2)}) collective-permute-start(bf16[128,512]{1,0:T(8,128)(2,1)S(1)} %get-tuple-element.163), channel_id=1, source_target_pairs={{0,1},{1,0},{2,3},{3,2},{4,5},{5,4},{6,7},{7,6},{8,9},{9,8},{10,11... | collective-permute-start | bytes 393224 | tf_op jit(solution)/shard_map/ppermute | solution.py:79
  68.1 5.1 %collective-permute-done.29.refs_3_ = bf16[128,512]{1,0:T(8,128)(2,1)S(1)} collective-permute-done((bf16[128,512]{1,0:T(8,128)(2,1)S(1)}, bf16[128,512]{1,0:T(8,128)(2,1)S(1)}, u32[]{:S(2)}, u32[]{:S(2)}) %collective-permute-start.29) | collective-permute-done | bytes 131104 | tf_op jit(solution)/shard_map/ppermute | solution.py:79
  73.7 0.8 collective-permute-start.12
  74.5 1.3 %collective-permute-start.17 = (bf16[128,640]{1,0:T(8,128)(2,1)S(1)}, bf16[128,640]{1,0:T(8,128)(2,1)S(1)}, u32[]{:S(2)}, u32[]{:S(2)}) collective-permute-start(bf16[128,640]{1,0:T(8,128)(2,1)S(1)} %get-tuple-element.142.refs_10_), channel_id=1, source_target_pairs={{0,1},{1,0},{2,3},{3,2},{4,5},{5,4},{6,7},{7,6},{8,9},{9,8},{10,11... | collective-permute-start | bytes 491528 | tf_op jit(solution)/shard_map/ppermute | solution.py:79
  76.2 4.7 %collective-permute-done.12.b = bf16[128,640]{1,0:T(8,128)(2,1)S(1)} collective-permute-done((bf16[128,640]{1,0:T(8,128)(2,1)S(1)}, bf16[128,640]{1,0:T(8,128)(2,1)S(1)}, u32[]{:S(2)}, u32[]{:S(2)}) %collective-permute-start.12) | collective-permute-done | bytes 163872 | tf_op jit(solution)/shard_map/ppermute | solution.py:79
  80.9 1.5 %collective-permute-start.35 = (bf16[80,1024]{1,0:T(8,128)(2,1)S(1)}, bf16[80,1024]{1,0:T(8,128)(2,1)S(1)}, u32[]{:S(2)}, u32[]{:S(2)}) collective-permute-start(bf16[80,1024]{1,0:T(8,128)(2,1)S(1)} %get-tuple-element.173), channel_id=1, source_target_pairs={{0,8},{8,0},{16,24},{24,16},{1,9},{9,1},{17,25},{25,17},{2,10},{10... | collective-permute-start | bytes 491528 | tf_op jit(solution)/shard_map/ppermute | solution.py:79
  82.4 1.5 %collective-permute-done.17.b = bf16[128,640]{1,0:T(8,128)(2,1)S(1)} collective-permute-done((bf16[128,640]{1,0:T(8,128)(2,1)S(1)}, bf16[128,640]{1,0:T(8,128)(2,1)S(1)}, u32[]{:S(2)}, u32[]{:S(2)}) %collective-permute-start.17) | collective-permute-done | bytes 163872 | tf_op jit(solution)/shard_map/ppermute | solution.py:79
  83.9 0.5 collective-permute-start.37
  84.4 1.7 %collective-permute-start.18 = (bf16[128,640]{1,0:T(8,128)(2,1)S(1)}, bf16[128,640]{1,0:T(8,128)(2,1)S(1)}, u32[]{:S(2)}, u32[]{:S(2)}) collective-permute-start(bf16[128,640]{1,0:T(8,128)(2,1)S(1)} %shard_map.220.refs_0_), channel_id=1, source_target_pairs={{0,2},{1,3},{2,0},{3,1},{4,6},{5,7},{6,4},{7,5},{8,10},{9,11},{10,... | collective-permute-start | bytes 491528 | tf_op jit(solution)/shard_map/ppermute | solution.py:79
  86.3 1.6 %collective-permute-start.21 = (bf16[80,896]{1,0:T(8,128)(2,1)S(1)}, bf16[80,896]{1,0:T(8,128)(2,1)S(1)}, u32[]{:S(2)}, u32[]{:S(2)}) collective-permute-start(bf16[80,896]{1,0:T(8,128)(2,1)S(1)} %get-tuple-element.153), channel_id=1, source_target_pairs={{0,8},{8,0},{16,24},{24,16},{1,9},{9,1},{17,25},{25,17},{2,10},{10... | collective-permute-start | bytes 430088 | tf_op jit(solution)/shard_map/ppermute | solution.py:79
  88.0 1.4 %collective-permute-start.22 = (bf16[80,896]{1,0:T(8,128)(2,1)S(1)}, bf16[80,896]{1,0:T(8,128)(2,1)S(1)}, u32[]{:S(2)}, u32[]{:S(2)}) collective-permute-start(bf16[80,896]{1,0:T(8,128)(2,1)S(1)} %get-tuple-element.154), channel_id=1, source_target_pairs={{0,16},{8,24},{16,0},{24,8},{1,17},{9,25},{17,1},{25,9},{2,18},{10... | collective-permute-start | bytes 430088 | tf_op jit(solution)/shard_map/ppermute | solution.py:79
  89.6 3.3 %collective-permute-done.36.refs_2_ = bf16[80,1024]{1,0:T(8,128)(2,1)S(1)} collective-permute-done((bf16[80,1024]{1,0:T(8,128)(2,1)S(1)}, bf16[80,1024]{1,0:T(8,128)(2,1)S(1)}, u32[]{:S(2)}, u32[]{:S(2)}) %collective-permute-start.36) | collective-permute-done | bytes 163872 | tf_op jit(solution)/shard_map/ppermute | solution.py:79
  93.2 1.5 %collective-permute-done.18.refs_1_ = bf16[128,640]{1,0:T(8,128)(2,1)S(1)} collective-permute-done((bf16[128,640]{1,0:T(8,128)(2,1)S(1)}, bf16[128,640]{1,0:T(8,128)(2,1)S(1)}, u32[]{:S(2)}, u32[]{:S(2)}) %collective-permute-start.18) | collective-permute-done | bytes 163872 | tf_op jit(solution)/shard_map/ppermute | solution.py:79
  94.7 2.0 %collective-permute-start.23 = (bf16[80,896]{1,0:T(8,128)(2,1)S(1)}, bf16[80,896]{1,0:T(8,128)(2,1)S(1)}, u32[]{:S(2)}, u32[]{:S(2)}) collective-permute-start(bf16[80,896]{1,0:T(8,128)(2,1)S(1)} %get-tuple-element.155), channel_id=1, source_target_pairs={{0,24},{8,16},{16,8},{24,0},{1,25},{9,17},{17,9},{25,1},{2,26},{10... | collective-permute-start | bytes 430088 | tf_op jit(solution)/shard_map/ppermute | solution.py:79
  96.7 0.9 collective-permute-start.34
  98.0 6.5 %collective-permute-done.23.refs_3_ = bf16[80,896]{1,0:T(8,128)(2,1)S(1)} collective-permute-done((bf16[80,896]{1,0:T(8,128)(2,1)S(1)}, bf16[80,896]{1,0:T(8,128)(2,1)S(1)}, u32[]{:S(2)}, u32[]{:S(2)}) %collective-permute-start.23) | collective-permute-done | bytes 143392 | tf_op jit(solution)/shard_map/ppermute | solution.py:79
  104.5 1.0 collective-permute-start.19
  105.5 0.7 shard_map.225
  106.2 2.5 %collective-permute-start.26 = (bf16[80,640]{1,0:T(8,128)(2,1)S(1)}, bf16[80,640]{1,0:T(8,128)(2,1)S(1)}, u32[]{:S(2)}, u32[]{:S(2)}) collective-permute-start(bf16[80,640]{1,0:T(8,128)(2,1)S(1)} %get-tuple-element.157.refs_0_), channel_id=1, source_target_pairs={{0,3},{1,2},{2,1},{3,0},{4,7},{5,6},{6,5},{7,4},{8,11},{9,10},{10,... | collective-permute-start | bytes 307208 | tf_op jit(solution)/shard_map/ppermute | solution.py:79
  108.7 1.9 %collective-permute-done.33.refs_2_ = bf16[80,1792]{1,0:T(8,128)(2,1)S(1)} collective-permute-done((bf16[80,1792]{1,0:T(8,128)(2,1)S(1)}, bf16[80,1792]{1,0:T(8,128)(2,1)S(1)}, u32[]{:S(2)}, u32[]{:S(2)}) %collective-permute-start.33) | collective-permute-done | bytes 286752 | tf_op jit(solution)/shard_map/ppermute | solution.py:79
  110.7 0.7 collective-permute-start.24
  111.3 0.8 shard_map.213
  112.1 0.9 shard_map.231
  113.0 0.8 shard_map.222
  113.7 1.5 %collective-permute-done.25.refs_2_ = bf16[80,640]{1,0:T(8,128)(2,1)S(1)} collective-permute-done((bf16[80,640]{1,0:T(8,128)(2,1)S(1)}, bf16[80,640]{1,0:T(8,128)(2,1)S(1)}, u32[]{:S(2)}, u32[]{:S(2)}) %collective-permute-start.25) | collective-permute-done | bytes 102432 | tf_op jit(solution)/shard_map/ppermute | solution.py:79
  115.3 1.0 collective-permute-done.24.refs_1_
  116.2 0.7 shard_map.226
  (80 shorter events, 7.3 us)
Async XLA Ops:
  0.6 14.4 %copy-start.6 = (bf16[640,256]{1,0:T(8,128)(2,1)S(1)}, bf16[640,256]{1,0:T(8,128)(2,1)}, u32[]{:S(2)}) copy-start(bf16[640,256]{1,0:T(8,128)(2,1)} %wq.3) | copy-start | bytes 983044
  2.9 8.6 %collective-permute-start.1 = (bf16[80,1152]{1,0:T(8,128)(2,1)S(1)}, bf16[80,1152]{1,0:T(8,128)(2,1)S(1)}, u32[]{:S(2)}, u32[]{:S(2)}) collective-permute-start(bf16[80,1152]{1,0:T(8,128)(2,1)S(1)} %get-tuple-element.97), channel_id=1, source_target_pairs={{0,1},{1,0},{2,3},{3,2},{4,5},{5,4},{6,7},{7,6},{8,9},{9,8},{10,11... | collective-permute-start | bytes 552968 | tf_op jit(solution)/shard_map/ppermute | solution.py:79
  6.1 14.2 %collective-permute-start = (bf16[320,512]{1,0:T(8,128)(2,1)S(1)}, bf16[320,512]{1,0:T(8,128)(2,1)S(1)}, u32[]{:S(2)}, u32[]{:S(2)}) collective-permute-start(bf16[320,512]{1,0:T(8,128)(2,1)S(1)} %get-tuple-element.96), channel_id=1, source_target_pairs={{0,1},{1,0},{2,3},{3,2},{4,5},{5,4},{6,7},{7,6},{8,9},{9,8},{10,11... | collective-permute-start | bytes 983048 | tf_op jit(solution)/shard_map/ppermute | solution.py:79
  6.1 10.0 %collective-permute-start.8 = (bf16[256,512]{1,0:T(8,128)(2,1)S(1)}, bf16[256,512]{1,0:T(8,128)(2,1)S(1)}, u32[]{:S(2)}, u32[]{:S(2)}) collective-permute-start(bf16[256,512]{1,0:T(8,128)(2,1)S(1)} %get-tuple-element.109.refs_5_.refs_3_), channel_id=1, source_target_pairs={{0,4},{4,0},{1,5},{5,1},{2,6},{6,2},{3,7},{7,3},{8,12},{12,8},{9,1... | collective-permute-start | bytes 786440 | tf_op jit(solution)/shard_map/ppermute | solution.py:79
  11.6 8.7 %collective-permute-start.4 = (bf16[80,1152]{1,0:T(8,128)(2,1)S(1)}, bf16[80,1152]{1,0:T(8,128)(2,1)S(1)}, u32[]{:S(2)}, u32[]{:S(2)}) collective-permute-start(bf16[80,1152]{1,0:T(8,128)(2,1)S(1)} %collective-permute-done.1.refs_0_), channel_id=1, source_target_pairs={{0,24},{8,16},{16,8},{24,0},{1,25},{9,17},{17,9},{25,1},{2,26},{10... | collective-permute-start | bytes 552968 | tf_op jit(solution)/shard_map/ppermute | solution.py:79
  14.4 6.9 %collective-permute-start.3 = (bf16[80,1152]{1,0:T(8,128)(2,1)S(1)}, bf16[80,1152]{1,0:T(8,128)(2,1)S(1)}, u32[]{:S(2)}, u32[]{:S(2)}) collective-permute-start(bf16[80,1152]{1,0:T(8,128)(2,1)S(1)} %collective-permute-done.1.refs_0_), channel_id=1, source_target_pairs={{0,16},{8,24},{16,0},{24,8},{1,17},{9,25},{17,1},{25,9},{2,18},{10... | collective-permute-start | bytes 552968 | tf_op jit(solution)/shard_map/ppermute | solution.py:79
  15.0 6.4 %collective-permute-start.2 = (bf16[80,1152]{1,0:T(8,128)(2,1)S(1)}, bf16[80,1152]{1,0:T(8,128)(2,1)S(1)}, u32[]{:S(2)}, u32[]{:S(2)}) collective-permute-start(bf16[80,1152]{1,0:T(8,128)(2,1)S(1)} %collective-permute-done.1.refs_0_), channel_id=1, source_target_pairs={{0,8},{8,0},{16,24},{24,16},{1,9},{9,1},{17,25},{25,17},{2,10},{10... | collective-permute-start | bytes 552968 | tf_op jit(solution)/shard_map/ppermute | solution.py:79
  15.7 1.0 copy-start.5
  18.1 5.4 %collective-permute-start.9 = (bf16[128,640]{1,0:T(8,128)(2,1)S(1)}, bf16[128,640]{1,0:T(8,128)(2,1)S(1)}, u32[]{:S(2)}, u32[]{:S(2)}) collective-permute-start(bf16[128,640]{1,0:T(8,128)(2,1)S(1)} %get-tuple-element.111), channel_id=1, source_target_pairs={{0,1},{1,0},{2,3},{3,2},{4,5},{5,4},{6,7},{7,6},{8,9},{9,8},{10,11... | collective-permute-start | bytes 491528 | tf_op jit(solution)/shard_map/ppermute | solution.py:79
  20.2 6.5 %collective-permute-start.5 = (bf16[320,512]{1,0:T(8,128)(2,1)S(1)}, bf16[320,512]{1,0:T(8,128)(2,1)S(1)}, u32[]{:S(2)}, u32[]{:S(2)}) collective-permute-start(bf16[320,512]{1,0:T(8,128)(2,1)S(1)} %collective-permute-done.refs_0_), channel_id=1, source_target_pairs={{0,4},{4,0},{1,5},{5,1},{2,6},{6,2},{3,7},{7,3},{8,12},{12,8},{9,1... | collective-permute-start | bytes 983048 | tf_op jit(solution)/shard_map/ppermute | solution.py:79
  21.4 5.3 %collective-permute-start.6 = (bf16[320,512]{1,0:T(8,128)(2,1)S(1)}, bf16[320,512]{1,0:T(8,128)(2,1)S(1)}, u32[]{:S(2)}, u32[]{:S(2)}) collective-permute-start(bf16[320,512]{1,0:T(8,128)(2,1)S(1)} %get-tuple-element.98.refs_1_), channel_id=1, source_target_pairs={{0,4},{4,0},{1,5},{5,1},{2,6},{6,2},{3,7},{7,3},{8,12},{12,8},{9,1... | collective-permute-start | bytes 983048 | tf_op jit(solution)/shard_map/ppermute | solution.py:79
  21.5 5.2 %collective-permute-start.7 = (bf16[256,640]{1,0:T(8,128)(2,1)S(1)}, bf16[256,640]{1,0:T(8,128)(2,1)S(1)}, u32[]{:S(2)}, u32[]{:S(2)}) collective-permute-start(bf16[256,640]{1,0:T(8,128)(2,1)S(1)} %get-tuple-element.99.refs_2_), channel_id=1, source_target_pairs={{0,4},{4,0},{1,5},{5,1},{2,6},{6,2},{3,7},{7,3},{8,12},{12,8},{9,1... | collective-permute-start | bytes 983048 | tf_op jit(solution)/shard_map/ppermute | solution.py:79
  23.5 9.2 %copy-start.3 = (bf16[1,2,128,640]{3,2,1,0:T(8,128)(2,1)S(1)}, bf16[1,2,128,640]{3,2,1,0:T(8,128)(2,1)}, u32[]{:S(2)}) copy-start(bf16[1,2,128,640]{3,2,1,0:T(8,128)(2,1)} %param.13) | copy-start | bytes 983044
  23.5 9.2 %copy-start.8 = (f32[4,640]{1,0:T(4,128)S(1)}, f32[4,640]{1,0:T(4,128)}, u32[]{:S(2)}) copy-start(f32[4,640]{1,0:T(4,128)} %gains.3) | copy-start | bytes 30724
  23.6 9.2 %copy-start = (bf16[640,512]{1,0:T(8,128)(2,1)S(1)}, bf16[640,512]{1,0:T(8,128)(2,1)}, u32[]{:S(2)}) copy-start(bf16[640,512]{1,0:T(8,128)(2,1)} %refs_5_.1) | copy-start | bytes 1966084
  23.6 9.2 %copy-start.1 = (bf16[640,512]{1,0:T(8,128)(2,1)S(1)}, bf16[640,512]{1,0:T(8,128)(2,1)}, u32[]{:S(2)}) copy-start(bf16[640,512]{1,0:T(8,128)(2,1)} %refs_6_.3) | copy-start | bytes 1966084
  23.6 9.2 %copy-start.2 = (bf16[512,640]{1,0:T(8,128)(2,1)S(1)}, bf16[512,640]{1,0:T(8,128)(2,1)}, u32[]{:S(2)}) copy-start(bf16[512,640]{1,0:T(8,128)(2,1)} %refs_7_.3) | copy-start | bytes 1966084
  23.6 9.1 %collective-permute-start.10 = (bf16[128,640]{1,0:T(8,128)(2,1)S(1)}, bf16[128,640]{1,0:T(8,128)(2,1)S(1)}, u32[]{:S(2)}, u32[]{:S(2)}) collective-permute-start(bf16[128,640]{1,0:T(8,128)(2,1)S(1)} %shard_map.209.refs_8_), channel_id=1, source_target_pairs={{0,2},{1,3},{2,0},{3,1},{4,6},{5,7},{6,4},{7,5},{8,10},{9,11},{10,... | collective-permute-start | bytes 491528 | tf_op jit(solution)/shard_map/ppermute | solution.py:79
  33.9 9.6 %collective-permute-start.11 = (bf16[128,640]{1,0:T(8,128)(2,1)S(1)}, bf16[128,640]{1,0:T(8,128)(2,1)S(1)}, u32[]{:S(2)}, u32[]{:S(2)}) collective-permute-start(bf16[128,640]{1,0:T(8,128)(2,1)S(1)} %get-tuple-element.117.refs_11_), channel_id=1, source_target_pairs={{0,2},{1,3},{2,0},{3,1},{4,6},{5,7},{6,4},{7,5},{8,10},{9,11},{10,... | collective-permute-start | bytes 491528 | tf_op jit(solution)/shard_map/ppermute | solution.py:79
  34.2 9.2 %copy-start.7 = (bf16[1,2,128,640]{3,2,1,0:T(8,128)(2,1)S(1)}, bf16[1,2,128,640]{3,2,1,0:T(8,128)(2,1)}, u32[]{:S(2)}) copy-start(bf16[1,2,128,640]{3,2,1,0:T(8,128)(2,1)} %param.24) | copy-start | bytes 983044
  46.2 10.3 %collective-permute-start.15 = (bf16[320,1024]{1,0:T(8,128)(2,1)S(1)}, bf16[320,1024]{1,0:T(8,128)(2,1)S(1)}, u32[]{:S(2)}, u32[]{:S(2)}) collective-permute-start(bf16[320,1024]{1,0:T(8,128)(2,1)S(1)} %get-tuple-element.130), channel_id=1, source_target_pairs={{0,4},{4,0},{1,5},{5,1},{2,6},{6,2},{3,7},{7,3},{8,12},{12,8},{9,1... | collective-permute-start | bytes 1966088 | tf_op jit(solution)/shard_map/ppermute | solution.py:79
  46.2 9.8 %collective-permute-start.13 = (bf16[128,640]{1,0:T(8,128)(2,1)S(1)}, bf16[128,640]{1,0:T(8,128)(2,1)S(1)}, u32[]{:S(2)}, u32[]{:S(2)}) collective-permute-start(bf16[128,640]{1,0:T(8,128)(2,1)S(1)} %get-tuple-element.121.refs_0_), channel_id=1, source_target_pairs={{0,2},{1,3},{2,0},{3,1},{4,6},{5,7},{6,4},{7,5},{8,10},{9,11},{10,... | collective-permute-start | bytes 491528 | tf_op jit(solution)/shard_map/ppermute | solution.py:79
  56.4 6.2 %collective-permute-start.14 = (bf16[128,640]{1,0:T(8,128)(2,1)S(1)}, bf16[128,640]{1,0:T(8,128)(2,1)S(1)}, u32[]{:S(2)}, u32[]{:S(2)}) collective-permute-start(bf16[128,640]{1,0:T(8,128)(2,1)S(1)} %get-tuple-element.129.refs_5_.refs_0_), channel_id=1, source_target_pairs={{0,1},{1,0},{2,3},{3,2},{4,5},{5,4},{6,7},{7,6},{8,9},{9,8},{10,11... | collective-permute-start | bytes 491528 | tf_op jit(solution)/shard_map/ppermute | solution.py:79
  63.6 1.6 %copy-start.4 = (bf16[640,512]{1,0:T(8,128)(2,1)S(1)}, bf16[640,512]{1,0:T(8,128)(2,1)}, u32[]{:S(2)}) copy-start(bf16[640,512]{1,0:T(8,128)(2,1)} %wkv.1) | copy-start | bytes 1966084
  63.7 1.6 %collective-permute-start.16 = (bf16[256,512]{1,0:T(8,128)(2,1)S(1)}, bf16[256,512]{1,0:T(8,128)(2,1)S(1)}, u32[]{:S(2)}, u32[]{:S(2)}) collective-permute-start(bf16[256,512]{1,0:T(8,128)(2,1)S(1)} %get-tuple-element.140), channel_id=1, source_target_pairs={{0,4},{4,0},{1,5},{5,1},{2,6},{6,2},{3,7},{7,3},{8,12},{12,8},{9,1... | collective-permute-start | bytes 786440 | tf_op jit(solution)/shard_map/ppermute | solution.py:79
  63.7 18.6 %collective-permute-start.27 = (bf16[320,1024]{1,0:T(8,128)(2,1)S(1)}, bf16[320,1024]{1,0:T(8,128)(2,1)S(1)}, u32[]{:S(2)}, u32[]{:S(2)}) collective-permute-start(bf16[320,1024]{1,0:T(8,128)(2,1)S(1)} %get-tuple-element.160), channel_id=1, source_target_pairs={{0,4},{4,0},{1,5},{5,1},{2,6},{6,2},{3,7},{7,3},{8,12},{12,8},{9,1... | collective-permute-start | bytes 1966088 | tf_op jit(solution)/shard_map/ppermute | solution.py:79
  64.2 9.0 %collective-permute-start.28 = (bf16[128,640]{1,0:T(8,128)(2,1)S(1)}, bf16[128,640]{1,0:T(8,128)(2,1)S(1)}, u32[]{:S(2)}, u32[]{:S(2)}) collective-permute-start(bf16[128,640]{1,0:T(8,128)(2,1)S(1)} %get-tuple-element.161.refs_0_), channel_id=1, source_target_pairs={{0,1},{1,0},{2,3},{3,2},{4,5},{5,4},{6,7},{7,6},{8,9},{9,8},{10,11... | collective-permute-start | bytes 491528 | tf_op jit(solution)/shard_map/ppermute | solution.py:79
  66.5 17.9 %collective-permute-start.20 = (bf16[320,896]{1,0:T(8,128)(2,1)S(1)}, bf16[320,896]{1,0:T(8,128)(2,1)S(1)}, u32[]{:S(2)}, u32[]{:S(2)}) collective-permute-start(bf16[320,896]{1,0:T(8,128)(2,1)S(1)} %get-tuple-element.151), channel_id=1, source_target_pairs={{0,4},{4,0},{1,5},{5,1},{2,6},{6,2},{3,7},{7,3},{8,12},{12,8},{9,1... | collective-permute-start | bytes 1720328 | tf_op jit(solution)/shard_map/ppermute | solution.py:79
  66.7 6.5 %collective-permute-start.29 = (bf16[128,512]{1,0:T(8,128)(2,1)S(1)}, bf16[128,512]{1,0:T(8,128)(2,1)S(1)}, u32[]{:S(2)}, u32[]{:S(2)}) collective-permute-start(bf16[128,512]{1,0:T(8,128)(2,1)S(1)} %get-tuple-element.163), channel_id=1, source_target_pairs={{0,1},{1,0},{2,3},{3,2},{4,5},{5,4},{6,7},{7,6},{8,9},{9,8},{10,11... | collective-permute-start | bytes 393224 | tf_op jit(solution)/shard_map/ppermute | solution.py:79
  73.7 7.2 %collective-permute-start.30 = (bf16[320,512]{1,0:T(8,128)(2,1)S(1)}, bf16[320,512]{1,0:T(8,128)(2,1)S(1)}, u32[]{:S(2)}, u32[]{:S(2)}) collective-permute-start(bf16[320,512]{1,0:T(8,128)(2,1)S(1)} %get-tuple-element.165), channel_id=1, source_target_pairs={{0,4},{4,0},{1,5},{5,1},{2,6},{6,2},{3,7},{7,3},{8,12},{12,8},{9,1... | collective-permute-start | bytes 983048 | tf_op jit(solution)/shard_map/ppermute | solution.py:79
  73.7 7.1 %collective-permute-start.12 = (bf16[128,640]{1,0:T(8,128)(2,1)S(1)}, bf16[128,640]{1,0:T(8,128)(2,1)S(1)}, u32[]{:S(2)}, u32[]{:S(2)}) collective-permute-start(bf16[128,640]{1,0:T(8,128)(2,1)S(1)} %get-tuple-element.118.a), channel_id=1, source_target_pairs={{0,1},{1,0},{2,3},{3,2},{4,5},{5,4},{6,7},{7,6},{8,9},{9,8},{10,11... | collective-permute-start | bytes 491528 | tf_op jit(solution)/shard_map/ppermute | solution.py:79
  74.5 9.4 %collective-permute-start.17 = (bf16[128,640]{1,0:T(8,128)(2,1)S(1)}, bf16[128,640]{1,0:T(8,128)(2,1)S(1)}, u32[]{:S(2)}, u32[]{:S(2)}) collective-permute-start(bf16[128,640]{1,0:T(8,128)(2,1)S(1)} %get-tuple-element.142.refs_10_), channel_id=1, source_target_pairs={{0,1},{1,0},{2,3},{3,2},{4,5},{5,4},{6,7},{7,6},{8,9},{9,8},{10,11... | collective-permute-start | bytes 491528 | tf_op jit(solution)/shard_map/ppermute | solution.py:79
  80.9 5.4 %collective-permute-start.31 = (bf16[320,256]{1,0:T(8,128)(2,1)S(1)}, bf16[320,256]{1,0:T(8,128)(2,1)S(1)}, u32[]{:S(2)}, u32[]{:S(2)}) collective-permute-start(bf16[320,256]{1,0:T(8,128)(2,1)S(1)} %get-tuple-element.168), channel_id=1, source_target_pairs={{0,4},{4,0},{1,5},{5,1},{2,6},{6,2},{3,7},{7,3},{8,12},{12,8},{9,1... | collective-permute-start | bytes 491528 | tf_op jit(solution)/shard_map/ppermute | solution.py:79
  80.9 7.1 %collective-permute-start.35 = (bf16[80,1024]{1,0:T(8,128)(2,1)S(1)}, bf16[80,1024]{1,0:T(8,128)(2,1)S(1)}, u32[]{:S(2)}, u32[]{:S(2)}) collective-permute-start(bf16[80,1024]{1,0:T(8,128)(2,1)S(1)} %get-tuple-element.173), channel_id=1, source_target_pairs={{0,8},{8,0},{16,24},{24,16},{1,9},{9,1},{17,25},{25,17},{2,10},{10... | collective-permute-start | bytes 491528 | tf_op jit(solution)/shard_map/ppermute | solution.py:79
  82.4 10.6 %collective-permute-start.36 = (bf16[80,1024]{1,0:T(8,128)(2,1)S(1)}, bf16[80,1024]{1,0:T(8,128)(2,1)S(1)}, u32[]{:S(2)}, u32[]{:S(2)}) collective-permute-start(bf16[80,1024]{1,0:T(8,128)(2,1)S(1)} %get-tuple-element.174), channel_id=1, source_target_pairs={{0,16},{8,24},{16,0},{24,8},{1,17},{9,25},{17,1},{25,9},{2,18},{10... | collective-permute-start | bytes 491528 | tf_op jit(solution)/shard_map/ppermute | solution.py:79
  83.9 9.3 %collective-permute-start.37 = (bf16[80,1024]{1,0:T(8,128)(2,1)S(1)}, bf16[80,1024]{1,0:T(8,128)(2,1)S(1)}, u32[]{:S(2)}, u32[]{:S(2)}) collective-permute-start(bf16[80,1024]{1,0:T(8,128)(2,1)S(1)} %get-tuple-element.175), channel_id=1, source_target_pairs={{0,24},{8,16},{16,8},{24,0},{1,25},{9,17},{17,9},{25,1},{2,26},{10... | collective-permute-start | bytes 491528 | tf_op jit(solution)/shard_map/ppermute | solution.py:79
  84.4 10.2 %collective-permute-start.18 = (bf16[128,640]{1,0:T(8,128)(2,1)S(1)}, bf16[128,640]{1,0:T(8,128)(2,1)S(1)}, u32[]{:S(2)}, u32[]{:S(2)}) collective-permute-start(bf16[128,640]{1,0:T(8,128)(2,1)S(1)} %shard_map.220.refs_0_), channel_id=1, source_target_pairs={{0,2},{1,3},{2,0},{3,1},{4,6},{5,7},{6,4},{7,5},{8,10},{9,11},{10,... | collective-permute-start | bytes 491528 | tf_op jit(solution)/shard_map/ppermute | solution.py:79
  86.3 10.4 %collective-permute-start.21 = (bf16[80,896]{1,0:T(8,128)(2,1)S(1)}, bf16[80,896]{1,0:T(8,128)(2,1)S(1)}, u32[]{:S(2)}, u32[]{:S(2)}) collective-permute-start(bf16[80,896]{1,0:T(8,128)(2,1)S(1)} %get-tuple-element.153), channel_id=1, source_target_pairs={{0,8},{8,0},{16,24},{24,16},{1,9},{9,1},{17,25},{25,17},{2,10},{10... | collective-permute-start | bytes 430088 | tf_op jit(solution)/shard_map/ppermute | solution.py:79
  88.0 9.7 %collective-permute-start.22 = (bf16[80,896]{1,0:T(8,128)(2,1)S(1)}, bf16[80,896]{1,0:T(8,128)(2,1)S(1)}, u32[]{:S(2)}, u32[]{:S(2)}) collective-permute-start(bf16[80,896]{1,0:T(8,128)(2,1)S(1)} %get-tuple-element.154), channel_id=1, source_target_pairs={{0,16},{8,24},{16,0},{24,8},{1,17},{9,25},{17,1},{25,9},{2,18},{10... | collective-permute-start | bytes 430088 | tf_op jit(solution)/shard_map/ppermute | solution.py:79
  93.0 15.7 %collective-permute-start.32 = (bf16[80,1792]{1,0:T(8,128)(2,1)S(1)}, bf16[80,1792]{1,0:T(8,128)(2,1)S(1)}, u32[]{:S(2)}, u32[]{:S(2)}) collective-permute-start(bf16[80,1792]{1,0:T(8,128)(2,1)S(1)} %get-tuple-element.170), channel_id=1, source_target_pairs={{0,8},{8,0},{16,24},{24,16},{1,9},{9,1},{17,25},{25,17},{2,10},{10... | collective-permute-start | bytes 860168 | tf_op jit(solution)/shard_map/ppermute | solution.py:79
  93.2 17.5 %collective-permute-start.33 = (bf16[80,1792]{1,0:T(8,128)(2,1)S(1)}, bf16[80,1792]{1,0:T(8,128)(2,1)S(1)}, u32[]{:S(2)}, u32[]{:S(2)}) collective-permute-start(bf16[80,1792]{1,0:T(8,128)(2,1)S(1)} %get-tuple-element.171), channel_id=1, source_target_pairs={{0,16},{8,24},{16,0},{24,8},{1,17},{9,25},{17,1},{25,9},{2,18},{10... | collective-permute-start | bytes 860168 | tf_op jit(solution)/shard_map/ppermute | solution.py:79
  94.7 9.8 %collective-permute-start.23 = (bf16[80,896]{1,0:T(8,128)(2,1)S(1)}, bf16[80,896]{1,0:T(8,128)(2,1)S(1)}, u32[]{:S(2)}, u32[]{:S(2)}) collective-permute-start(bf16[80,896]{1,0:T(8,128)(2,1)S(1)} %get-tuple-element.155), channel_id=1, source_target_pairs={{0,24},{8,16},{16,8},{24,0},{1,25},{9,17},{17,9},{25,1},{2,26},{10... | collective-permute-start | bytes 430088 | tf_op jit(solution)/shard_map/ppermute | solution.py:79
  96.7 15.4 %collective-permute-start.34 = (bf16[80,1792]{1,0:T(8,128)(2,1)S(1)}, bf16[80,1792]{1,0:T(8,128)(2,1)S(1)}, u32[]{:S(2)}, u32[]{:S(2)}) collective-permute-start(bf16[80,1792]{1,0:T(8,128)(2,1)S(1)} %get-tuple-element.172), channel_id=1, source_target_pairs={{0,24},{8,16},{16,8},{24,0},{1,25},{9,17},{17,9},{25,1},{2,26},{10... | collective-permute-start | bytes 860168 | tf_op jit(solution)/shard_map/ppermute | solution.py:79
  97.7 8.5 %collective-permute-start.38 = (bf16[80,1024]{1,0:T(8,128)(2,1)S(1)}, bf16[80,1024]{1,0:T(8,128)(2,1)S(1)}, u32[]{:S(2)}, u32[]{:S(2)}) collective-permute-start(bf16[80,1024]{1,0:T(8,128)(2,1)S(1)} %shard_map.230), channel_id=1, source_target_pairs={{0,1},{1,0},{2,3},{3,2},{4,5},{5,4},{6,7},{7,6},{8,9},{9,8},{10,11... | collective-permute-start | bytes 491528 | tf_op jit(solution)/shard_map/ppermute | solution.py:79
  104.5 8.5 %collective-permute-start.19 = (bf16[128,640]{1,0:T(8,128)(2,1)S(1)}, bf16[128,640]{1,0:T(8,128)(2,1)S(1)}, u32[]{:S(2)}, u32[]{:S(2)}) collective-permute-start(bf16[128,640]{1,0:T(8,128)(2,1)S(1)} %shard_map.221.a), channel_id=1, source_target_pairs={{0,1},{1,0},{2,3},{3,2},{4,5},{5,4},{6,7},{7,6},{8,9},{9,8},{10,11... | collective-permute-start | bytes 491528 | tf_op jit(solution)/shard_map/ppermute | solution.py:79
  106.2 7.5 %collective-permute-start.26 = (bf16[80,640]{1,0:T(8,128)(2,1)S(1)}, bf16[80,640]{1,0:T(8,128)(2,1)S(1)}, u32[]{:S(2)}, u32[]{:S(2)}) collective-permute-start(bf16[80,640]{1,0:T(8,128)(2,1)S(1)} %get-tuple-element.157.refs_0_), channel_id=1, source_target_pairs={{0,3},{1,2},{2,1},{3,0},{4,7},{5,6},{6,5},{7,4},{8,11},{9,10},{10,... | collective-permute-start | bytes 307208 | tf_op jit(solution)/shard_map/ppermute | solution.py:79
  108.7 6.6 %collective-permute-start.25 = (bf16[80,640]{1,0:T(8,128)(2,1)S(1)}, bf16[80,640]{1,0:T(8,128)(2,1)S(1)}, u32[]{:S(2)}, u32[]{:S(2)}) collective-permute-start(bf16[80,640]{1,0:T(8,128)(2,1)S(1)} %get-tuple-element.157.refs_0_), channel_id=1, source_target_pairs={{0,2},{1,3},{2,0},{3,1},{4,6},{5,7},{6,4},{7,5},{8,10},{9,11},{10,... | collective-permute-start | bytes 307208 | tf_op jit(solution)/shard_map/ppermute | solution.py:79
  110.7 5.6 %collective-permute-start.24 = (bf16[80,640]{1,0:T(8,128)(2,1)S(1)}, bf16[80,640]{1,0:T(8,128)(2,1)S(1)}, u32[]{:S(2)}, u32[]{:S(2)}) collective-permute-start(bf16[80,640]{1,0:T(8,128)(2,1)S(1)} %get-tuple-element.157.refs_0_), channel_id=1, source_target_pairs={{0,1},{1,0},{2,3},{3,2},{4,5},{5,4},{6,7},{7,6},{8,9},{9,8},{10,11... | collective-permute-start | bytes 307208 | tf_op jit(solution)/shard_map/ppermute | solution.py:79
  (2 other events, 1.4 us)

commit v2 on v1

--- a/solution.py
+++ b/solution.py
@@ -110,6 +110,8 @@
     seq = positions.shape[1]
     root = head_dim ** (-0.5)
     share = rows // 2
+    streams = 2
+    piece = share // streams
     unit_len = min(share, block_len)
     peers = tuple(range(2, n_tp, 2))
     copies = n_tp // 2
@@ -128,6 +130,10 @@
     def own_rows(k):
         return pl.ds(pl.multiple_of(((lax.axis_index("tp") & 1) ^ k) * share, share), share)
 
+    def own_stream(k):
+        place = (lax.axis_index("tp") & 1) * share + k * piece
+        return pl.ds(pl.multiple_of(place, piece), piece)
+
     def neighbour(x):
         return swap(x, "tp", n_tp, 1)
 
@@ -160,15 +166,17 @@
     piece_rows = max(up_piece, down_piece)
 
     def pre_body(*refs):
-        sources, (gate, up, down) = refs[:7], refs[7:10]
-        normed_o, kv_o, unit_o, scale_o, cos_o, sin_o, idx_o, start_o, gate_o, piece_o = refs[10:20]
-        col_pos, col_idx, sem = refs[20:23]
-        table, hid, pos, gains, hgains, freqs, wkv = refs[23:]
-        loads = [pltpu.make_async_copy(a, b, sem.at[i]) for i, (a, b) in enumerate(zip(sources, refs[23:]))]
+        sources, (gate, up, down, wq, wo) = refs[:7], refs[7:12]
+        normed_o, kv_o, unit_o, scale_o, cos_o, sin_o, idx_o, start_o, gate_o, piece_o, wq_o, wo_o = refs[12:24]
+        col_pos, col_idx, sem = refs[24:27]
+        table, hid, pos, gains, hgains, freqs, wkv = refs[27:]
+        loads = [pltpu.make_async_copy(a, b, sem.at[i]) for i, (a, b) in enumerate(zip(sources, refs[27:]))]
         moves = [
             pltpu.make_async_copy(up.at[own_piece(width), :], piece_o.at[:up_piece, :ff], sem.at[7]),
             pltpu.make_async_copy(down.at[own_piece(ff), :], piece_o.at[:down_piece, ff:], sem.at[8]),
             pltpu.make_async_copy(gate.at[own_half(width), :], gate_o, sem.at[9]),
+            pltpu.make_async_copy(wq, wq_o, sem.at[10]),
+            pltpu.make_async_copy(wo, wo_o, sem.at[11]),
         ]
         for move in loads + moves:
             move.start()
@@ -210,11 +218,11 @@
             move.wait()
 
     sources = (block_table, hidden, positions, norm_gains, head_norm_gains, freq, key_value_weight)
-    normed, kv_mine, unit_k, scale_k, cosine, sine, idx, start, gate_pack, piece_pack = kernel_call(
+    normed, kv_mine, unit_k, scale_k, cosine, sine, idx, start, gate_pack, piece_pack, wq_near, wo_near = kernel_call(
         pre_body,
         tuple(
             pltpu.with_memory_space_constraint(x, pltpu.HBM)
-            for x in (*sources, gate_weight, up_weight, down_weight)
+            for x in (*sources, gate_weight, up_weight, down_weight, query_weight, output_weight)
         ),
         [
             ((rows, width), bf16),
@@ -227,11 +235,13 @@
             ((rows, 1), f32),
             ((width // 2, ff), bf16),
             ((piece_rows, ff + width), bf16),
+            (query_weight.shape, bf16),
+            (output_weight.shape, bf16),
         ],
-        scratch=[pltpu.VMEM((rows, 1), f32), pltpu.VMEM((rows, 1), f32), pltpu.SemaphoreType.DMA((10,))]
+        scratch=[pltpu.VMEM((rows, 1), f32), pltpu.VMEM((rows, 1), f32), pltpu.SemaphoreType.DMA((12,))]
         + [pltpu.SMEM(block_table.shape, block_table.dtype)]
         + [pltpu.VMEM(x.shape, x.dtype) for x in sources[1:]],
-        in_hbm=10,
+        in_hbm=12,
     )
 
     gate_near = neighbour(gate_pack)
@@ -280,7 +290,7 @@
 
     queries, unit_q, scale_q = kernel_call(
         query_body,
-        (normed, query_weight, head_norm_gains, cosine, sine),
+        (normed, wq_near, head_norm_gains, cosine, sine),
         [((rows, q_width), bf16), ((rows, q_width), f32), ((rows, heads), f32)],
     )
 
@@ -326,7 +336,7 @@
 
     probs, context, attn_mine, attn_send = kernel_call(
         attend_body,
-        (block_table, queries, idx, start, output_weight, *kvs),
+        (block_table, queries, idx, start, wo_near, *kvs),
         [
             ((heads, rows, seq), f32),
             ((rows, q_width), bf16),
@@ -353,51 +363,63 @@
             (refs[3][...], refs[4][...], refs[5][...], slice(ff, 2 * ff)),
         ]
 
-    def feed_body(*refs):
-        hid, gains = refs[:2]
-        groups = ff_groups(refs[2:8])
-        attn = summed(refs[8 : 8 + n_terms])
-        unit_o, scale_o, mixed_o, x_o = refs[8 + n_terms : 12 + n_terms]
-        act_o = refs[12 + n_terms : 14 + n_terms]
-        gate_o, up_o, send_o = refs[14 + n_terms :]
-        scale = rms_scale(attn)
-        unit = attn * scale
-        mixed = hid[own_rows(0), :].astype(f32) + unit * gains[1:2, :]
-        unit_o[...] = unit
-        scale_o[...] = scale
-        mixed_o[...] = mixed
-        x = (mixed * rms_scale(mixed) * gains[2:3, :]).astype(bf16)
-        x_o[...] = x
-        total = None
-        for k, (wg, wu, wd, cols) in enumerate(groups):
-            gate = product(x, wg)
-            up = product(x, wu)
-            gate_o[:, cols] = gate
-            up_o[:, cols] = up
-            inner = gelu_coef * (gate + 0.044715 * gate * gate * gate)
-            act = (0.5 * gate * (1.0 + jnp.tanh(inner)) * up).astype(bf16)
-            term = product(act, wd)
-            total = term if total is None else total + term
-            act_o[k][...] = act
-        send_o[...] = total.astype(bf16)
-
-    unit_a, scale_a, mixed, ff_in, act_mine, act_send, gate, up, ff_send = kernel_call(
-        feed_body,
-        (hidden, norm_gains, *weights, *attn_terms),
-        [
-            ((share, width), f32),
-            ((share, 1), f32),
-            ((share, width), f32),
-            ((share, width), bf16),
-            ((share, ff), bf16),
-            ((share, ff), bf16),
-            ((share, 2 * ff), f32),
-            ((share, 2 * ff), f32),
-            ((share, width), bf16),
-        ],
-    )
-    ff_terms = exchanged(ff_send)
-    act_near = neighbour(act_send)
+    def with_earlier(value, earlier, out):
+        for k, ref in enumerate(earlier):
+            out[k * piece : (k + 1) * piece, :] = ref[...]
+        out[len(earlier) * piece :, :] = value
+
+    def feed(k, earlier):
+        rows_k = slice(k * piece, (k + 1) * piece)
+        full = (k + 1) * piece
+
+        def feed_body(*refs):
+            hid, gains = refs[:2]
+            groups = ff_groups(refs[2:8])
+            terms = refs[8 : 8 + n_terms]
+            before = refs[8 + n_terms : 8 + n_terms + len(earlier)]
+            unit_o, scale_o, mixed_o, x_o, act_o, near_o, gate_o, up_o, send_o = refs[8 + n_terms + len(earlier) :]
+            attn = terms[0][rows_k, :].astype(f32)
+            for r in terms[1:]:
+                attn = attn + r[rows_k, :].astype(f32)
+            scale = rms_scale(attn)
+            unit = attn * scale
+            mixed = hid[own_stream(k), :].astype(f32) + unit * gains[1:2, :]
+            unit_o[...] = unit
+            scale_o[...] = scale
+            mixed_o[...] = mixed
+            x = (mixed * rms_scale(mixed) * gains[2:3, :]).astype(bf16)
+            x_o[...] = x
+            total = None
+            for at, (wg, wu, wd, cols) in enumerate(groups):
+                gate = product(x, wg)
+                up = product(x, wu)
+                gate_o[:, cols] = gate
+                up_o[:, cols] = up
+                inner = gelu_coef * (gate + 0.044715 * gate * gate * gate)
+                act = (0.5 * gate * (1.0 + jnp.tanh(inner)) * up).astype(bf16)
+                term = product(act, wd)
+                total = term if total is None else total + term
+                if at == 0:
+                    act_o[...] = act
+                else:
+                    with_earlier(act, before, near_o)
+            send_o[...] = total.astype(bf16)
+
+        return kernel_call(
+            feed_body,
+            (hidden, norm_gains, *weights, *attn_terms, *earlier),
+            [
+                ((piece, width), f32),
+                ((piece, 1), f32),
+                ((piece, width), f32),
+                ((piece, width), bf16),
+                ((piece, ff), bf16),
+                ((full, ff), bf16),
+                ((piece, 2 * ff), f32),
+                ((piece, 2 * ff), f32),
+                ((piece, width), bf16),
+            ],
+        )
 
     def slope_body(gate_r, up_r, gelu_o, slope_o):
         v = gate_r[...]
@@ -409,44 +431,67 @@
         )
         slope_o[...] = slope * up_r[...]
 
-    gelu, up_slope = kernel_call(slope_body, (gate, up), [((share, 2 * ff), f32), ((share, 2 * ff), f32)])
-
-    def back_body(*refs):
-        gains, mixed_r, cot_r, gelu_r, slope_r = refs[:5]
-        groups = ff_groups(refs[5:11])
-        ff_out = summed(refs[11 : 11 + n_terms])
-        hidden_o, gain_o, dout_o, dgate_o, dup_o, send_o = refs[11 + n_terms :]
-        scale = rms_scale(ff_out)
-        unit = ff_out * scale
-        hidden_o[...] = (mixed_r[...] + unit * gains[3:4, :]).astype(bf16)
-        grad = cot_r[own_rows(0), :].astype(f32)
-        gain_o[...] = jnp.sum(grad * unit, axis=0, keepdims=True) * (1.0 / copies)
-        d_out = rms_back(grad, unit, scale, gains[3:4, :]).astype(bf16)
-        dout_o[...] = d_out
-        total = None
-        for wg, wu, wd, cols in groups:
-            d_act = back_product(d_out, wd)
-            d_gate = (d_act * slope_r[:, cols]).astype(bf16)
-            d_up = (d_act * gelu_r[:, cols]).astype(bf16)
-            term = back_product(d_gate, wg) + back_product(d_up, wu)
-            total = term if total is None else total + term
-            dgate_o[:, cols] = d_gate
-            dup_o[:, cols] = d_up
-        send_o[...] = total.astype(bf16)
-
-    hidden_mine, gain_o, d_ff_out, d_gate, d_up, dff_send = kernel_call(
-        back_body,
-        (norm_gains, mixed, cot, gelu, up_slope, *weights, *ff_terms),
-        [
-            ((share, width), bf16),
-            ((1, width), f32),
-            ((share, width), bf16),
-            ((share, 2 * ff), bf16),
-            ((share, 2 * ff), bf16),
-            ((share, width), bf16),
-        ],
-    )
-    dffin_terms = exchanged(dff_send)
+    fed, ff_terms, slopes = [], [], []
+    act_send = []
+    for k in range(streams):
+        fed.append(feed(k, act_send))
+        act_send = [fed[k][5]]
+        ff_terms.append(exchanged(fed[k][8]))
+        slopes.append(kernel_call(slope_body, tuple(fed[k][6:8]), [((piece, 2 * ff), f32)] * 2))
+    act_near = neighbour(act_send[0])
+    act_mine = [f[4] for f in fed]
+    ff_in = [f[3] for f in fed]
+
+    def feed_back(k, earlier):
+        full = (k + 1) * piece
+
+        def back_body(*refs):
+            gains, mixed_r, cot_r, gelu_r, slope_r = refs[:5]
+            groups = ff_groups(refs[5:11])
+            ff_out = summed(refs[11 : 11 + n_terms])
+            before = refs[11 + n_terms : 11 + n_terms + len(earlier)]
+            hidden_o, gain_o, dout_o, dgate_o, dup_o, send_o = refs[11 + n_terms + len(earlier) :]
+            scale = rms_scale(ff_out)
+            unit = ff_out * scale
+            with_earlier((mixed_r[...] + unit * gains[3:4, :]).astype(bf16), before[:1], hidden_o)
+            grad = cot_r[own_stream(k), :].astype(f32)
+            gain_o[...] = jnp.sum(grad * unit, axis=0, keepdims=True) * (1.0 / copies)
+            d_out = rms_back(grad, unit, scale, gains[3:4, :]).astype(bf16)
+            with_earlier(d_out, before[1:], dout_o)
+            total = None
+            for wg, wu, wd, cols in groups:
+                d_act = back_product(d_out, wd)
+                d_gate = (d_act * slope_r[:, cols]).astype(bf16)
+                d_up = (d_act * gelu_r[:, cols]).astype(bf16)
+                term = back_product(d_gate, wg) + back_product(d_up, wu)
+                total = term if total is None else total + term
+                dgate_o[:, cols] = d_gate
+                dup_o[:, cols] = d_up
+            send_o[...] = total.astype(bf16)
+
+        return kernel_call(
+            back_body,
+            (norm_gains, fed[k][2], cot, *slopes[k], *weights, *ff_terms[k], *earlier),
+            [
+                ((full, width), bf16),
+                ((1, width), f32),
+                ((full, width), bf16),
+                ((piece, 2 * ff), bf16),
+                ((piece, 2 * ff), bf16),
+                ((piece, width), bf16),
+            ],
+        )
+
+    backed, dffin_terms = [], []
+    earlier = ()
+    for k in range(streams):
+        backed.append(feed_back(k, earlier))
+        earlier = (backed[k][0], backed[k][2])
+        dffin_terms.append(exchanged(backed[k][5]))
+    hidden_mine, d_ff_out = earlier
+    gain_o = [r[1] for r in backed]
+    d_gate = [r[3] for r in backed]
+    d_up = [r[4] for r in backed]
     hidden_near = neighbour(hidden_mine)
     d_ff_near = neighbour(d_ff_out)
 
@@ -502,41 +547,56 @@
         )
         return [parts[0]] + [swap(parts[k], "batch", n_batch, k) for k in range(1, n_batch)]
 
-    def ff_grad_fill(x, dgate, dup, near_acc, own_acc):
-        for at, right in enumerate((dgate, dup)):
-            total = lead_product(x[...], right[...])
+    def ff_grad_fill(*refs):
+        x, d_gate_v, d_up_v = (joined(refs[k * streams : (k + 1) * streams]) for k in range(3))
+        near_acc, own_acc = refs[3 * streams :]
+        for at, right in enumerate((d_gate_v, d_up_v)):
+            total = lead_product(x, right)
             own_acc[:, at * ff : (at + 1) * ff] = total[:, :ff]
             near_acc[:, at * ff : (at + 1) * ff] = total[:, ff:]
 
-    near_grads, own_grads = grad_call(ff_grad_fill, (ff_in, d_gate, d_up), 2 * ff, 2 * ff)
+    near_grads, own_grads = grad_call(ff_grad_fill, (*ff_in, *d_gate, *d_up), 2 * ff, 2 * ff)
     mid_terms = reduce_grads(near_grads)
 
-    def mix_back_body(gains, mixed_r, unit_r, scale_r, cot_r, *refs):
-        d_in = summed(refs[:n_terms])
-        dmixed_o, dattn_o, gain_f_o, gain_a_o = refs[n_terms:]
-        mixed_v = mixed_r[...]
-        scale = rms_scale(mixed_v)
-        unit_f = mixed_v * scale
-        gain_f_o[...] = jnp.sum(d_in * unit_f, axis=0, keepdims=True) * (1.0 / copies)
-        d_mix = cot_r[own_rows(0), :].astype(f32) + rms_back(d_in, unit_f, scale, gains[2:3, :])
-        dmixed_o[...] = d_mix
-        unit = unit_r[...]
-        gain_a_o[...] = jnp.sum(d_mix * unit, axis=0, keepdims=True) * (1.0 / copies)
-        dattn_o[...] = rms_back(d_mix, unit, scale_r[...], gains[1:2, :]).astype(bf16)
-
-    d_mixed, dattn_mine, gain_f, gain_a = kernel_call(
-        mix_back_body,
-        (norm_gains, mixed, unit_a, scale_a, cot, dffin_terms[0], *(after(t, near_grads[0]) for t in dffin_terms[1:])),
-        [((share, width), f32), ((share, width), bf16), ((1, width), f32), ((1, width), f32)],
-    )
-    d_attn = (dattn_mine, after(neighbour(dattn_mine), mid_terms[0]))
+    def mix_back(k):
+        def mix_back_body(gains, mixed_r, unit_r, scale_r, cot_r, *refs):
+            d_in = summed(refs[:n_terms])
+            dmixed_o, dattn_o, gain_f_o, gain_a_o = refs[n_terms:]
+            mixed_v = mixed_r[...]
+            scale = rms_scale(mixed_v)
+            unit_f = mixed_v * scale
+            gain_f_o[...] = jnp.sum(d_in * unit_f, axis=0, keepdims=True) * (1.0 / copies)
+            d_mix = cot_r[own_stream(k), :].astype(f32) + rms_back(d_in, unit_f, scale, gains[2:3, :])
+            dmixed_o[...] = d_mix
+            unit = unit_r[...]
+            gain_a_o[...] = jnp.sum(d_mix * unit, axis=0, keepdims=True) * (1.0 / copies)
+            dattn_o[...] = rms_back(d_mix, unit, scale_r[...], gains[1:2, :]).astype(bf16)
+
+        terms = dffin_terms[k]
+        if k == streams - 1:
+            terms = [terms[0]] + [after(t, near_grads[0]) for t in terms[1:]]
+        unit_a, scale_a, mixed = fed[k][:3]
+        return kernel_call(
+            mix_back_body,
+            (norm_gains, mixed, unit_a, scale_a, cot, *terms),
+            [((piece, width), f32), ((piece, width), bf16), ((1, width), f32), ((1, width), f32)],
+        )
+
+    mix_backs = [mix_back(k) for k in range(streams)]
+    d_mixed = [m[0] for m in mix_backs]
+    gain_f = [m[2] for m in mix_backs]
+    gain_a = [m[3] for m in mix_backs]
+    near_parts = [neighbour(m[1]) for m in mix_backs]
+    near_parts[-1] = after(near_parts[-1], mid_terms[0])
+    d_attn = (*(m[1] for m in mix_backs), *near_parts)
 
     def attend_back_body(*refs):
         wo, probs_r, q = refs[:3]
         kv = refs[3 : 3 + len(kvs)]
-        d_out = joined(refs[3 + len(kvs) : 5 + len(kvs)])
-        dq_o = refs[5 + len(kvs)]
-        dkv_o = refs[6 + len(kvs) :]
+        at = 3 + len(kvs) + len(d_attn)
+        d_out = joined(refs[3 + len(kvs) : at])
+        dq_o = refs[at]
+        dkv_o = refs[at + 1 :]
         d_context = back_product(d_out, wo[...]).astype(bf16)
         length = seq // len(kvs)
         for h in range(heads):
@@ -567,7 +627,7 @@
     else:
         dkv_outs = [((seq, 2 * head_dim), f32)]
     attended_back = kernel_call(
-        attend_back_body, (output_weight, probs, queries, *kvs, *d_attn), [((rows, q_width), f32)] + dkv_outs
+        attend_back_body, (wo_near, probs, queries, *kvs, *d_attn), [((rows, q_width), f32)] + dkv_outs
     )
     d_q = attended_back[0]
     if paired:
@@ -588,7 +648,7 @@
 
     d_query_raw, dn_query, gain_q = kernel_call(
         query_back_body,
-        (d_q, unit_q, scale_q, cosine, sine, head_norm_gains, query_weight),
+        (d_q, unit_q, scale_q, cosine, sine, head_norm_gains, wq_near),
         [((rows, q_width), bf16), ((rows, width), f32), ((1, head_dim), f32)],
     )
 
@@ -623,15 +683,15 @@
     (mid_send,) = kernel_call(mid_body, tuple(mid_terms), [((out_rows, 2 * ff), bf16)])
     mid_near = neighbour(mid_send)
 
-    def down_grad_fill(dff, dff_near, act, act_r, acc):
-        acc[...] = lead_product(joined((dff, dff_near)), joined((act, act_r)))
-
-    def out_grad_fill(da, da_near, ctx_r, acc):
-        acc[...] = lead_product(joined((da, da_near)), ctx_r[...])
+    def down_grad_fill(*refs):
+        refs[-1][...] = lead_product(joined(refs[:2]), joined(refs[2:-1]))
+
+    def out_grad_fill(*refs):
+        refs[-1][...] = lead_product(joined(refs[:-2]), refs[-2][...])
 
     side_terms = reduce_grads(
         own_grads,
-        *grad_call(down_grad_fill, (d_ff_out, d_ff_near, act_mine, act_near), ff),
+        *grad_call(down_grad_fill, (d_ff_out, d_ff_near, *act_mine, act_near), ff),
         *grad_call(out_grad_fill, (*d_attn, context), q_width),
     )
 
@@ -651,7 +711,9 @@
     kv_at = q_width
     gain_at = q_width + 2 * head_dim
 
-    def last_grad_fill(nrm, draw, dkv, hid, g_o, g_f, g_a, g_q, g_k, mine, send, acc):
+    def last_grad_fill(nrm, draw, dkv, hid, g_q, g_k, mine, send, *refs):
+        acc = refs[-1]
+        g_o, g_f, g_a = (summed(refs[k * streams : (k + 1) * streams]) for k in range(3))
         acc[:, :kv_at] = lead_product(nrm[...], draw[...])
         acc[:, kv_at:gain_at] = lead_product(nrm[...], dkv[...])
         g_in = jnp.zeros((1, width), f32)
@@ -661,7 +723,7 @@
         line = lax.broadcasted_iota(jnp.int32, (lanes, width), 0)
         packed = jnp.where(line == 0, g_in, 0.0)
         for at, row in enumerate((g_a, g_f, g_o), 1):
-            packed = jnp.where(line == at, row[...], packed)
+            packed = jnp.where(line == at, row, packed)
         acc[:, gain_at:] = packed.T
         line = lax.broadcasted_iota(jnp.int32, (lanes, head_dim), 0)
         packed = jnp.where(line == 4, g_q[...], jnp.where(line == 5, g_k[...], 0.0)).T
@@ -672,7 +734,7 @@
     last_terms = reduce_grads(
         *grad_call(
             last_grad_fill,
-            (normed, d_query_raw, d_kv_raw, hidden, gain_o, gain_f, gain_a, gain_q, gain_k, dn_mine, dn_send),
+            (normed, d_query_raw, d_kv_raw, hidden, gain_q, gain_k, dn_mine, dn_send, *gain_o, *gain_f, *gain_a),
             gain_at + lanes,
         ),
     )
@@ -701,13 +763,14 @@
         kv_body, tuple(kv_sums), [((out_rows, 2 * head_dim), f32), ((4, out_rows), f32), ((2, head_rows), f32)]
     )
 
-    def input_back_body(hid, gains, dmix, *refs):
-        d_normed = summed(refs[:n_terms])
+    def input_back_body(hid, gains, *refs):
+        d_mix = joined(refs[:streams])
+        d_normed = summed(refs[streams:-1])
         x = hid[own_rows(0), :].astype(f32)
         scale = rms_scale(x)
-        refs[n_terms][...] = (dmix[...] + rms_back(d_normed, x * scale, scale, gains[0:1, :])).astype(bf16)
-
-    (input_mine,) = kernel_call(input_back_body, (hidden, norm_gains, d_mixed, *dn_terms), [((share, width), bf16)])
+        refs[-1][...] = (d_mix + rms_back(d_normed, x * scale, scale, gains[0:1, :])).astype(bf16)
+
+    (input_mine,) = kernel_call(input_back_body, (hidden, norm_gains, *d_mixed, *dn_terms), [((share, width), bf16)])
 
     def place_body(a, b, o):
         o[own_rows(0), :] = a[...]

time: 117 us -> 118 us (level)
  waiting for transfers between devices: 65.9 us -> 54.9 us
  starting transfers between devices: 31.8 us -> 41.1 us
  Pallas kernels: 16.9 us -> 19.7 us
    ppermute x39 -> x42, waiting for transfers between devices: 65.9 us -> 54.9 us  [swap(): return lax.ppermute(x, axis, [(i, i ^ k) for i in range(size)])]
    ppermute x39 -> x42, starting transfers between devices: 31.8 us -> 41.1 us  [swap(): return lax.ppermute(x, axis, [(i, i ^ k) for i in range(size)])]
    pallas_call x28 -> x32, Pallas kernels: 16.9 us -> 19.7 us  [kernel_call(): pl.pallas_call(body, out_shape=[jax.ShapeDtypeStruct(s, d) for s, d in ou...]
  transfers between devices with their start and end apart: 39 -> 42, of which waited for: 17 -> 19; matrix products, arithmetic and copies ran while one was open for 0% -> 0% of each run, Pallas kernels for 8% -> 10%
where the time goes in v2:
time: 118 us
  waiting for transfers between devices  54.9 us (47%)
  starting transfers between devices  41.1 us (35%)
  Pallas kernels  19.7 us (17%)
  local copies, waits for them, and re-layouts  1.37 us (1%)
    ppermute x42, waiting for transfers between devices, swap(): return lax.ppermute(x, axis, [(i, i ^ k) for i in range(size)])  54.9 us
    ppermute x42, starting transfers between devices, swap(): return lax.ppermute(x, axis, [(i, i ^ k) for i in range(size)])  41.1 us
    pallas_call x32, Pallas kernels, kernel_call(): pl.pallas_call(body, out_shape=[jax.ShapeDtypeStruct(s, d) for s, d in ou...  19.7 us
  transfers between devices with their start and end apart: 42, of which 19 were waited for; matrix products, arithmetic and copies ran while one was open for 0% of the time, Pallas kernels for 10%

profile of v2, /device:TPU:0, one launch (start us, length us, event | category | flops | bytes accessed | tf_op | source)
XLA Modules:
  0.0 118.1 jit_solution(1814371466616396382)
XLA Ops:
  0.6 2.3 %shard_map.204 = (bf16[256,640]{1,0:T(8,128)(2,1)S(1)}, bf16[256,512]{1,0:T(8,128)(2,1)S(1)}, f32[256,256]{1,0:T(8,128)S(1)}, f32[256,1]{1,0:T(8,128)S(1)}, f32[...) custom-call(s32[4]{0:T(128)} %refs_0_.5, ...), custom_call_target="tpu_custom_call" | custom-call | bytes 5903888 | tf_op jit(solution)/shard_map/pallas_call | solution.py:65
  2.9 3.1 %collective-permute-start.1 = (bf16[80,1152]{1,0:T(8,128)(2,1)S(1)}, bf16[80,1152]{1,0:T(8,128)(2,1)S(1)}, u32[]{:S(2)}, u32[]{:S(2)}) collective-permute-start(bf16[80,1152]{1,0:T(8,128)(2,1)S(1)} %get-tuple-element.120), channel_id=1, source_target_pairs={{0,1},{1,0},{2,3},{3,2},{4,5},{5,4},{6,7},{7,6},{8,9},{9,8},{10,11... | collective-permute-start | bytes 552968 | tf_op jit(solution)/shard_map/ppermute | solution.py:79
  6.1 5.4 %collective-permute-done.1.refs_0_ = bf16[80,1152]{1,0:T(8,128)(2,1)S(1)} collective-permute-done((bf16[80,1152]{1,0:T(8,128)(2,1)S(1)}, bf16[80,1152]{1,0:T(8,128)(2,1)S(1)}, u32[]{:S(2)}, u32[]{:S(2)}) %collective-permute-start.1) | collective-permute-done | bytes 184352 | tf_op jit(solution)/shard_map/ppermute | solution.py:79
  11.5 1.9 %collective-permute-start.2 = (bf16[80,1152]{1,0:T(8,128)(2,1)S(1)}, bf16[80,1152]{1,0:T(8,128)(2,1)S(1)}, u32[]{:S(2)}, u32[]{:S(2)}) collective-permute-start(bf16[80,1152]{1,0:T(8,128)(2,1)S(1)} %collective-permute-done.1.refs_0_), channel_id=1, source_target_pairs={{0,8},{8,0},{16,24},{24,16},{1,9},{9,1},{17,25},{25,17},{2,10},{10... | collective-permute-start | bytes 552968 | tf_op jit(solution)/shard_map/ppermute | solution.py:79
  13.5 1.5 %collective-permute-start.3 = (bf16[80,1152]{1,0:T(8,128)(2,1)S(1)}, bf16[80,1152]{1,0:T(8,128)(2,1)S(1)}, u32[]{:S(2)}, u32[]{:S(2)}) collective-permute-start(bf16[80,1152]{1,0:T(8,128)(2,1)S(1)} %collective-permute-done.1.refs_0_), channel_id=1, source_target_pairs={{0,16},{8,24},{16,0},{24,8},{1,17},{9,25},{17,1},{25,9},{2,18},{10... | collective-permute-start | bytes 552968 | tf_op jit(solution)/shard_map/ppermute | solution.py:79
  16.7 1.3 %shard_map.208 = (f32[1,256,512]{2,1,0:T(8,128)S(1)}, bf16[256,256]{1,0:T(8,128)(2,1)S(1)}, f32[128,640]{1,0:T(8,128)S(1)}, bf16[128,640]{1,0:T(8,128)(2,1)S(1)}) custom-call(s32[4]{0:T(128)S(1)} %copy-done.8, bf16[256,256]{1,0:T(8,128)(2,1)S(1)} %get-tuple-element.130.refs_1_.refs_2_, f32[256,1]{1,0:T(8,128)S(1)} %get-tuple-element.131.refs_2_, ...), custom_call_target="tpu_custom_call" | custom-call | bytes 2131984 | tf_op jit(solution)/shard_map/pallas_call | solution.py:65
  18.1 2.1 %collective-permute-start.9 = (bf16[128,640]{1,0:T(8,128)(2,1)S(1)}, bf16[128,640]{1,0:T(8,128)(2,1)S(1)}, u32[]{:S(2)}, u32[]{:S(2)}) collective-permute-start(bf16[128,640]{1,0:T(8,128)(2,1)S(1)} %get-tuple-element.136), channel_id=1, source_target_pairs={{0,1},{1,0},{2,3},{3,2},{4,5},{5,4},{6,7},{7,6},{8,9},{9,8},{10,11... | collective-permute-start | bytes 491528 | tf_op jit(solution)/shard_map/ppermute | solution.py:79
  20.2 1.8 %collective-permute-done.3.refs_2_ = bf16[80,1152]{1,0:T(8,128)(2,1)S(1)} collective-permute-done((bf16[80,1152]{1,0:T(8,128)(2,1)S(1)}, bf16[80,1152]{1,0:T(8,128)(2,1)S(1)}, u32[]{:S(2)}, u32[]{:S(2)}) %collective-permute-start.3) | collective-permute-done | bytes 184352 | tf_op jit(solution)/shard_map/ppermute | solution.py:79
  22.6 0.9 collective-permute-done.9.b
  23.5 3.1 %collective-permute-start.10 = (bf16[128,640]{1,0:T(8,128)(2,1)S(1)}, bf16[128,640]{1,0:T(8,128)(2,1)S(1)}, u32[]{:S(2)}, u32[]{:S(2)}) collective-permute-start(bf16[128,640]{1,0:T(8,128)(2,1)S(1)} %shard_map.209.refs_8_), channel_id=1, source_target_pairs={{0,2},{1,3},{2,0},{3,1},{4,6},{5,7},{6,4},{7,5},{8,10},{9,11},{10,... | collective-permute-start | bytes 491528 | tf_op jit(solution)/shard_map/ppermute | solution.py:79
  26.8 6.5 %collective-permute-done.10.refs_9_ = bf16[128,640]{1,0:T(8,128)(2,1)S(1)} collective-permute-done((bf16[128,640]{1,0:T(8,128)(2,1)S(1)}, bf16[128,640]{1,0:T(8,128)(2,1)S(1)}, u32[]{:S(2)}, u32[]{:S(2)}) %collective-permute-start.10) | collective-permute-done | bytes 163872 | tf_op jit(solution)/shard_map/ppermute | solution.py:79
  33.3 1.1 shard_map.210
  34.5 1.1 shard_map.211
  35.6 3.0 %collective-permute-start.11 = (bf16[64,640]{1,0:T(8,128)(2,1)S(1)}, bf16[64,640]{1,0:T(8,128)(2,1)S(1)}, u32[]{:S(2)}, u32[]{:S(2)}) collective-permute-start(bf16[64,640]{1,0:T(8,128)(2,1)S(1)} %get-tuple-element.143.refs_11_), channel_id=1, source_target_pairs={{0,2},{1,3},{2,0},{3,1},{4,6},{5,7},{6,4},{7,5},{8,10},{9,11},{10,... | collective-permute-start | bytes 245768 | tf_op jit(solution)/shard_map/ppermute | solution.py:79
  39.0 2.7 %collective-permute-done.12.refs_12_ = bf16[64,640]{1,0:T(8,128)(2,1)S(1)} collective-permute-done((bf16[64,640]{1,0:T(8,128)(2,1)S(1)}, bf16[64,640]{1,0:T(8,128)(2,1)S(1)}, u32[]{:S(2)}, u32[]{:S(2)}) %collective-permute-start.12) | collective-permute-done | bytes 81952 | tf_op jit(solution)/shard_map/ppermute | solution.py:79
  41.6 1.6 %shard_map.214 = (bf16[64,640]{1,0:T(8,128)(2,1)S(1)}, f32[1,640]{1,0:T(1,128)S(1)}, bf16[64,640]{1,0:T(8,128)(2,1)S(1)}, bf16[64,1024]{1,0:T(8,128)(2,1)S(1)}, ...) custom-call(f32[4,640]{1,0:T(4,128)S(1)} %copy-done.6, f32[64,640]{1,0:T(8,128)S(1)} %get-tuple-element.144.refs_1_.mixed_r, ...), custom_call_target="tpu_custom_call" | custom-call | bytes 5632512 | tf_op jit(solution)/shard_map/pallas_call | solution.py:65
  43.4 1.6 %shard_map.215 = (bf16[128,640]{1,0:T(8,128)(2,1)S(1)}, f32[1,640]{1,0:T(1,128)S(1)}, bf16[128,640]{1,0:T(8,128)(2,1)S(1)}, bf16[64,1024]{1,0:T(8,128)(2,1)S(1)}...) custom-call(f32[4,640]{1,0:T(4,128)S(1)} %copy-done.6, f32[64,640]{1,0:T(8,128)S(1)} %get-tuple-element.138.refs_1_.mixed_r, ...), custom_call_target="tpu_custom_call" | custom-call | bytes 5960192 | tf_op jit(solution)/shard_map/pallas_call | solution.py:65
  45.0 1.0 shard_map.218
  46.8 2.3 %collective-permute-start.14 = (bf16[64,640]{1,0:T(8,128)(2,1)S(1)}, bf16[64,640]{1,0:T(8,128)(2,1)S(1)}, u32[]{:S(2)}, u32[]{:S(2)}) collective-permute-start(bf16[64,640]{1,0:T(8,128)(2,1)S(1)} %get-tuple-element.155.refs_0_), channel_id=1, source_target_pairs={{0,2},{1,3},{2,0},{3,1},{4,6},{5,7},{6,4},{7,5},{8,10},{9,11},{10,... | collective-permute-start | bytes 245768 | tf_op jit(solution)/shard_map/ppermute | solution.py:79
  49.1 6.8 %collective-permute-done.15.refs_1_ = bf16[64,640]{1,0:T(8,128)(2,1)S(1)} collective-permute-done((bf16[64,640]{1,0:T(8,128)(2,1)S(1)}, bf16[64,640]{1,0:T(8,128)(2,1)S(1)}, u32[]{:S(2)}, u32[]{:S(2)}) %collective-permute-start.15) | collective-permute-done | bytes 81952 | tf_op jit(solution)/shard_map/ppermute | solution.py:79
  56.3 0.9 collective-permute-done.14.refs_1_
  57.5 1.2 collective-permute-start.16
  58.9 2.6 %collective-permute-done.17.refs_8_.refs_3_ = bf16[64,640]{1,0:T(8,128)(2,1)S(1)} collective-permute-done((bf16[64,640]{1,0:T(8,128)(2,1)S(1)}, bf16[64,640]{1,0:T(8,128)(2,1)S(1)}, u32[]{:S(2)}, u32[]{:S(2)}) %collective-permute-start.17) | collective-permute-done | bytes 81952 | tf_op jit(solution)/shard_map/ppermute | solution.py:79
  61.4 0.9 collective-permute-done.16.refs_7_.refs_2_
  62.3 1.0 shard_map.221
  63.9 0.8 collective-permute-start.31
  66.5 1.2 %collective-permute-start.32 = (bf16[128,512]{1,0:T(8,128)(2,1)S(1)}, bf16[128,512]{1,0:T(8,128)(2,1)S(1)}, u32[]{:S(2)}, u32[]{:S(2)}) collective-permute-start(bf16[128,512]{1,0:T(8,128)(2,1)S(1)} %get-tuple-element.209), channel_id=1, source_target_pairs={{0,1},{1,0},{2,3},{3,2},{4,5},{5,4},{6,7},{7,6},{8,9},{9,8},{10,11... | collective-permute-start | bytes 393224 | tf_op jit(solution)/shard_map/ppermute | solution.py:79
  67.7 5.1 %collective-permute-done.32.refs_4_ = bf16[128,512]{1,0:T(8,128)(2,1)S(1)} collective-permute-done((bf16[128,512]{1,0:T(8,128)(2,1)S(1)}, bf16[128,512]{1,0:T(8,128)(2,1)S(1)}, u32[]{:S(2)}, u32[]{:S(2)}) %collective-permute-start.32) | collective-permute-done | bytes 131104 | tf_op jit(solution)/shard_map/ppermute | solution.py:79
  73.4 0.9 collective-permute-start.13
  74.3 1.2 %collective-permute-start.20 = (bf16[128,640]{1,0:T(8,128)(2,1)S(1)}, bf16[128,640]{1,0:T(8,128)(2,1)S(1)}, u32[]{:S(2)}, u32[]{:S(2)}) collective-permute-start(bf16[128,640]{1,0:T(8,128)(2,1)S(1)} %get-tuple-element.184.refs_7_), channel_id=1, source_target_pairs={{0,1},{1,0},{2,3},{3,2},{4,5},{5,4},{6,7},{7,6},{8,9},{9,8},{10,11... | collective-permute-start | bytes 491528 | tf_op jit(solution)/shard_map/ppermute | solution.py:79
  75.5 5.0 %collective-permute-done.13.b = bf16[128,640]{1,0:T(8,128)(2,1)S(1)} collective-permute-done((bf16[128,640]{1,0:T(8,128)(2,1)S(1)}, bf16[128,640]{1,0:T(8,128)(2,1)S(1)}, u32[]{:S(2)}, u32[]{:S(2)}) %collective-permute-start.13) | collective-permute-done | bytes 163872 | tf_op jit(solution)/shard_map/ppermute | solution.py:79
  80.5 1.3 %collective-permute-start.38 = (bf16[80,1024]{1,0:T(8,128)(2,1)S(1)}, bf16[80,1024]{1,0:T(8,128)(2,1)S(1)}, u32[]{:S(2)}, u32[]{:S(2)}) collective-permute-start(bf16[80,1024]{1,0:T(8,128)(2,1)S(1)} %get-tuple-element.219), channel_id=1, source_target_pairs={{0,8},{8,0},{16,24},{24,16},{1,9},{9,1},{17,25},{25,17},{2,10},{10... | collective-permute-start | bytes 491528 | tf_op jit(solution)/shard_map/ppermute | solution.py:79
  83.5 1.0 collective-permute-start.40
  84.6 0.8 collective-permute-start.21
  85.8 1.7 %collective-permute-start.24 = (bf16[80,896]{1,0:T(8,128)(2,1)S(1)}, bf16[80,896]{1,0:T(8,128)(2,1)S(1)}, u32[]{:S(2)}, u32[]{:S(2)}) collective-permute-start(bf16[80,896]{1,0:T(8,128)(2,1)S(1)} %get-tuple-element.198), channel_id=1, source_target_pairs={{0,8},{8,0},{16,24},{24,16},{1,9},{9,1},{17,25},{25,17},{2,10},{10... | collective-permute-start | bytes 430088 | tf_op jit(solution)/shard_map/ppermute | solution.py:79
  87.6 0.8 collective-permute-start.25
  88.6 4.3 %collective-permute-done.39.refs_2_ = bf16[80,1024]{1,0:T(8,128)(2,1)S(1)} collective-permute-done((bf16[80,1024]{1,0:T(8,128)(2,1)S(1)}, bf16[80,1024]{1,0:T(8,128)(2,1)S(1)}, u32[]{:S(2)}, u32[]{:S(2)}) %collective-permute-start.39) | collective-permute-done | bytes 163872 | tf_op jit(solution)/shard_map/ppermute | solution.py:79
  93.6 1.9 %collective-permute-start.36 = (bf16[80,1792]{1,0:T(8,128)(2,1)S(1)}, bf16[80,1792]{1,0:T(8,128)(2,1)S(1)}, u32[]{:S(2)}, u32[]{:S(2)}) collective-permute-start(bf16[80,1792]{1,0:T(8,128)(2,1)S(1)} %get-tuple-element.217), channel_id=1, source_target_pairs={{0,16},{8,24},{16,0},{24,8},{1,17},{9,25},{17,1},{25,9},{2,18},{10... | collective-permute-start | bytes 860168 | tf_op jit(solution)/shard_map/ppermute | solution.py:79
  95.6 0.8 collective-permute-start.26
  96.4 2.1 %collective-permute-start.37 = (bf16[80,1792]{1,0:T(8,128)(2,1)S(1)}, bf16[80,1792]{1,0:T(8,128)(2,1)S(1)}, u32[]{:S(2)}, u32[]{:S(2)}) collective-permute-start(bf16[80,1792]{1,0:T(8,128)(2,1)S(1)} %get-tuple-element.218), channel_id=1, source_target_pairs={{0,24},{8,16},{16,8},{24,0},{1,25},{9,17},{17,9},{25,1},{2,26},{10... | collective-permute-start | bytes 860168 | tf_op jit(solution)/shard_map/ppermute | solution.py:79
  99.6 6.3 %collective-permute-done.26.refs_3_ = bf16[80,896]{1,0:T(8,128)(2,1)S(1)} collective-permute-done((bf16[80,896]{1,0:T(8,128)(2,1)S(1)}, bf16[80,896]{1,0:T(8,128)(2,1)S(1)}, u32[]{:S(2)}, u32[]{:S(2)}) %collective-permute-start.26) | collective-permute-done | bytes 143392 | tf_op jit(solution)/shard_map/ppermute | solution.py:79
  107.2 1.3 %collective-permute-start.27 = (bf16[80,640]{1,0:T(8,128)(2,1)S(1)}, bf16[80,640]{1,0:T(8,128)(2,1)S(1)}, u32[]{:S(2)}, u32[]{:S(2)}) collective-permute-start(bf16[80,640]{1,0:T(8,128)(2,1)S(1)} %get-tuple-element.202.refs_0_), channel_id=1, source_target_pairs={{0,1},{1,0},{2,3},{3,2},{4,5},{5,4},{6,7},{7,6},{8,9},{9,8},{10,11... | collective-permute-start | bytes 307208 | tf_op jit(solution)/shard_map/ppermute | solution.py:79
  108.9 1.8 %collective-permute-done.36.refs_2_ = bf16[80,1792]{1,0:T(8,128)(2,1)S(1)} collective-permute-done((bf16[80,1792]{1,0:T(8,128)(2,1)S(1)}, bf16[80,1792]{1,0:T(8,128)(2,1)S(1)}, u32[]{:S(2)}, u32[]{:S(2)}) %collective-permute-start.36) | collective-permute-done | bytes 286752 | tf_op jit(solution)/shard_map/ppermute | solution.py:79
  110.8 1.3 %collective-permute-start.29 = (bf16[80,640]{1,0:T(8,128)(2,1)S(1)}, bf16[80,640]{1,0:T(8,128)(2,1)S(1)}, u32[]{:S(2)}, u32[]{:S(2)}) collective-permute-start(bf16[80,640]{1,0:T(8,128)(2,1)S(1)} %get-tuple-element.202.refs_0_), channel_id=1, source_target_pairs={{0,3},{1,2},{2,1},{3,0},{4,7},{5,6},{6,5},{7,4},{8,11},{9,10},{10,... | collective-permute-start | bytes 307208 | tf_op jit(solution)/shard_map/ppermute | solution.py:79
  112.8 0.9 shard_map.235
  113.7 0.8 shard_map.226
  114.4 0.8 collective-permute-done.28.refs_2_
  115.2 2.1 %collective-permute-done.29.refs_3_ = bf16[80,640]{1,0:T(8,128)(2,1)S(1)} collective-permute-done((bf16[80,640]{1,0:T(8,128)(2,1)S(1)}, bf16[80,640]{1,0:T(8,128)(2,1)S(1)}, u32[]{:S(2)}, u32[]{:S(2)}) %collective-permute-start.29) | collective-permute-done | bytes 102432 | tf_op jit(solution)/shard_map/ppermute | solution.py:79
  (86 shorter events, 15.2 us)
Async XLA Ops:
  2.9 8.6 %collective-permute-start.1 = (bf16[80,1152]{1,0:T(8,128)(2,1)S(1)}, bf16[80,1152]{1,0:T(8,128)(2,1)S(1)}, u32[]{:S(2)}, u32[]{:S(2)}) collective-permute-start(bf16[80,1152]{1,0:T(8,128)(2,1)S(1)} %get-tuple-element.120), channel_id=1, source_target_pairs={{0,1},{1,0},{2,3},{3,2},{4,5},{5,4},{6,7},{7,6},{8,9},{9,8},{10,11... | collective-permute-start | bytes 552968 | tf_op jit(solution)/shard_map/ppermute | solution.py:79
  6.0 14.1 %collective-permute-start = (bf16[320,512]{1,0:T(8,128)(2,1)S(1)}, bf16[320,512]{1,0:T(8,128)(2,1)S(1)}, u32[]{:S(2)}, u32[]{:S(2)}) collective-permute-start(bf16[320,512]{1,0:T(8,128)(2,1)S(1)} %get-tuple-element.119), channel_id=1, source_target_pairs={{0,1},{1,0},{2,3},{3,2},{4,5},{5,4},{6,7},{7,6},{8,9},{9,8},{10,11... | collective-permute-start | bytes 983048 | tf_op jit(solution)/shard_map/ppermute | solution.py:79
  6.1 10.0 %collective-permute-start.8 = (bf16[256,512]{1,0:T(8,128)(2,1)S(1)}, bf16[256,512]{1,0:T(8,128)(2,1)S(1)}, u32[]{:S(2)}, u32[]{:S(2)}) collective-permute-start(bf16[256,512]{1,0:T(8,128)(2,1)S(1)} %get-tuple-element.134.refs_5_.refs_3_), channel_id=1, source_target_pairs={{0,4},{4,0},{1,5},{5,1},{2,6},{6,2},{3,7},{7,3},{8,12},{12,8},{9,1... | collective-permute-start | bytes 786440 | tf_op jit(solution)/shard_map/ppermute | solution.py:79
  11.5 8.6 %collective-permute-start.2 = (bf16[80,1152]{1,0:T(8,128)(2,1)S(1)}, bf16[80,1152]{1,0:T(8,128)(2,1)S(1)}, u32[]{:S(2)}, u32[]{:S(2)}) collective-permute-start(bf16[80,1152]{1,0:T(8,128)(2,1)S(1)} %collective-permute-done.1.refs_0_), channel_id=1, source_target_pairs={{0,8},{8,0},{16,24},{24,16},{1,9},{9,1},{17,25},{25,17},{2,10},{10... | collective-permute-start | bytes 552968 | tf_op jit(solution)/shard_map/ppermute | solution.py:79
  13.5 8.5 %collective-permute-start.3 = (bf16[80,1152]{1,0:T(8,128)(2,1)S(1)}, bf16[80,1152]{1,0:T(8,128)(2,1)S(1)}, u32[]{:S(2)}, u32[]{:S(2)}) collective-permute-start(bf16[80,1152]{1,0:T(8,128)(2,1)S(1)} %collective-permute-done.1.refs_0_), channel_id=1, source_target_pairs={{0,16},{8,24},{16,0},{24,8},{1,17},{9,25},{17,1},{25,9},{2,18},{10... | collective-permute-start | bytes 552968 | tf_op jit(solution)/shard_map/ppermute | solution.py:79
  15.0 7.0 %collective-permute-start.4 = (bf16[80,1152]{1,0:T(8,128)(2,1)S(1)}, bf16[80,1152]{1,0:T(8,128)(2,1)S(1)}, u32[]{:S(2)}, u32[]{:S(2)}) collective-permute-start(bf16[80,1152]{1,0:T(8,128)(2,1)S(1)} %collective-permute-done.1.refs_0_), channel_id=1, source_target_pairs={{0,24},{8,16},{16,8},{24,0},{1,25},{9,17},{17,9},{25,1},{2,26},{10... | collective-permute-start | bytes 552968 | tf_op jit(solution)/shard_map/ppermute | solution.py:79
  18.1 5.4 %collective-permute-start.9 = (bf16[128,640]{1,0:T(8,128)(2,1)S(1)}, bf16[128,640]{1,0:T(8,128)(2,1)S(1)}, u32[]{:S(2)}, u32[]{:S(2)}) collective-permute-start(bf16[128,640]{1,0:T(8,128)(2,1)S(1)} %get-tuple-element.136), channel_id=1, source_target_pairs={{0,1},{1,0},{2,3},{3,2},{4,5},{5,4},{6,7},{7,6},{8,9},{9,8},{10,11... | collective-permute-start | bytes 491528 | tf_op jit(solution)/shard_map/ppermute | solution.py:79
  20.2 6.5 %collective-permute-start.5 = (bf16[320,512]{1,0:T(8,128)(2,1)S(1)}, bf16[320,512]{1,0:T(8,128)(2,1)S(1)}, u32[]{:S(2)}, u32[]{:S(2)}) collective-permute-start(bf16[320,512]{1,0:T(8,128)(2,1)S(1)} %collective-permute-done.refs_0_), channel_id=1, source_target_pairs={{0,4},{4,0},{1,5},{5,1},{2,6},{6,2},{3,7},{7,3},{8,12},{12,8},{9,1... | collective-permute-start | bytes 983048 | tf_op jit(solution)/shard_map/ppermute | solution.py:79
  22.0 4.6 %collective-permute-start.6 = (bf16[320,512]{1,0:T(8,128)(2,1)S(1)}, bf16[320,512]{1,0:T(8,128)(2,1)S(1)}, u32[]{:S(2)}, u32[]{:S(2)}) collective-permute-start(bf16[320,512]{1,0:T(8,128)(2,1)S(1)} %get-tuple-element.121.refs_1_), channel_id=1, source_target_pairs={{0,4},{4,0},{1,5},{5,1},{2,6},{6,2},{3,7},{7,3},{8,12},{12,8},{9,1... | collective-permute-start | bytes 983048 | tf_op jit(solution)/shard_map/ppermute | solution.py:79
  22.1 4.5 %collective-permute-start.7 = (bf16[256,640]{1,0:T(8,128)(2,1)S(1)}, bf16[256,640]{1,0:T(8,128)(2,1)S(1)}, u32[]{:S(2)}, u32[]{:S(2)}) collective-permute-start(bf16[256,640]{1,0:T(8,128)(2,1)S(1)} %get-tuple-element.122.refs_2_), channel_id=1, source_target_pairs={{0,4},{4,0},{1,5},{5,1},{2,6},{6,2},{3,7},{7,3},{8,12},{12,8},{9,1... | collective-permute-start | bytes 983048 | tf_op jit(solution)/shard_map/ppermute | solution.py:79
  23.5 9.9 %copy-start.3 = (bf16[1,2,128,640]{3,2,1,0:T(8,128)(2,1)S(1)}, bf16[1,2,128,640]{3,2,1,0:T(8,128)(2,1)}, u32[]{:S(2)}) copy-start(bf16[1,2,128,640]{3,2,1,0:T(8,128)(2,1)} %param.13) | copy-start | bytes 983044
  23.5 9.9 %copy-start.6 = (f32[4,640]{1,0:T(4,128)S(1)}, f32[4,640]{1,0:T(4,128)}, u32[]{:S(2)}) copy-start(f32[4,640]{1,0:T(4,128)} %gains.5) | copy-start | bytes 30724
  23.5 9.8 %copy-start = (bf16[640,512]{1,0:T(8,128)(2,1)S(1)}, bf16[640,512]{1,0:T(8,128)(2,1)}, u32[]{:S(2)}) copy-start(bf16[640,512]{1,0:T(8,128)(2,1)} %refs_5_.3) | copy-start | bytes 1966084
  23.5 9.8 %copy-start.1 = (bf16[640,512]{1,0:T(8,128)(2,1)S(1)}, bf16[640,512]{1,0:T(8,128)(2,1)}, u32[]{:S(2)}) copy-start(bf16[640,512]{1,0:T(8,128)(2,1)} %refs_6_.5) | copy-start | bytes 1966084
  23.5 9.8 %copy-start.2 = (bf16[512,640]{1,0:T(8,128)(2,1)S(1)}, bf16[512,640]{1,0:T(8,128)(2,1)}, u32[]{:S(2)}) copy-start(bf16[512,640]{1,0:T(8,128)(2,1)} %refs_7_.5) | copy-start | bytes 1966084
  23.5 9.8 %collective-permute-start.10 = (bf16[128,640]{1,0:T(8,128)(2,1)S(1)}, bf16[128,640]{1,0:T(8,128)(2,1)S(1)}, u32[]{:S(2)}, u32[]{:S(2)}) collective-permute-start(bf16[128,640]{1,0:T(8,128)(2,1)S(1)} %shard_map.209.refs_8_), channel_id=1, source_target_pairs={{0,2},{1,3},{2,0},{3,1},{4,6},{5,7},{6,4},{7,5},{8,10},{9,11},{10,... | collective-permute-start | bytes 491528 | tf_op jit(solution)/shard_map/ppermute | solution.py:79
  34.4 7.2 %collective-permute-start.12 = (bf16[64,640]{1,0:T(8,128)(2,1)S(1)}, bf16[64,640]{1,0:T(8,128)(2,1)S(1)}, u32[]{:S(2)}, u32[]{:S(2)}) collective-permute-start(bf16[64,640]{1,0:T(8,128)(2,1)S(1)} %get-tuple-element.149.refs_11_), channel_id=1, source_target_pairs={{0,2},{1,3},{2,0},{3,1},{4,6},{5,7},{6,4},{7,5},{8,10},{9,11},{10,... | collective-permute-start | bytes 245768 | tf_op jit(solution)/shard_map/ppermute | solution.py:79
  35.6 7.8 %collective-permute-start.11 = (bf16[64,640]{1,0:T(8,128)(2,1)S(1)}, bf16[64,640]{1,0:T(8,128)(2,1)S(1)}, u32[]{:S(2)}, u32[]{:S(2)}) collective-permute-start(bf16[64,640]{1,0:T(8,128)(2,1)S(1)} %get-tuple-element.143.refs_11_), channel_id=1, source_target_pairs={{0,2},{1,3},{2,0},{3,1},{4,6},{5,7},{6,4},{7,5},{8,10},{9,11},{10,... | collective-permute-start | bytes 245768 | tf_op jit(solution)/shard_map/ppermute | solution.py:79
  38.8 2.9 %copy-start.4 = (bf16[1,2,128,640]{3,2,1,0:T(8,128)(2,1)S(1)}, bf16[1,2,128,640]{3,2,1,0:T(8,128)(2,1)}, u32[]{:S(2)}) copy-start(bf16[1,2,128,640]{3,2,1,0:T(8,128)(2,1)} %param.24) | copy-start | bytes 983044
  46.0 12.7 %collective-permute-start.18 = (bf16[320,1024]{1,0:T(8,128)(2,1)S(1)}, bf16[320,1024]{1,0:T(8,128)(2,1)S(1)}, u32[]{:S(2)}, u32[]{:S(2)}) collective-permute-start(bf16[320,1024]{1,0:T(8,128)(2,1)S(1)} %get-tuple-element.172), channel_id=1, source_target_pairs={{0,4},{4,0},{1,5},{5,1},{2,6},{6,2},{3,7},{7,3},{8,12},{12,8},{9,1... | collective-permute-start | bytes 1966088 | tf_op jit(solution)/shard_map/ppermute | solution.py:79
  46.1 9.8 %collective-permute-start.15 = (bf16[64,640]{1,0:T(8,128)(2,1)S(1)}, bf16[64,640]{1,0:T(8,128)(2,1)S(1)}, u32[]{:S(2)}, u32[]{:S(2)}) collective-permute-start(bf16[64,640]{1,0:T(8,128)(2,1)S(1)} %get-tuple-element.159.refs_0_), channel_id=1, source_target_pairs={{0,2},{1,3},{2,0},{3,1},{4,6},{5,7},{6,4},{7,5},{8,10},{9,11},{10,... | collective-permute-start | bytes 245768 | tf_op jit(solution)/shard_map/ppermute | solution.py:79
  46.8 10.4 %collective-permute-start.14 = (bf16[64,640]{1,0:T(8,128)(2,1)S(1)}, bf16[64,640]{1,0:T(8,128)(2,1)S(1)}, u32[]{:S(2)}, u32[]{:S(2)}) collective-permute-start(bf16[64,640]{1,0:T(8,128)(2,1)S(1)} %get-tuple-element.155.refs_0_), channel_id=1, source_target_pairs={{0,2},{1,3},{2,0},{3,1},{4,6},{5,7},{6,4},{7,5},{8,10},{9,11},{10,... | collective-permute-start | bytes 245768 | tf_op jit(solution)/shard_map/ppermute | solution.py:79
  56.2 5.2 %collective-permute-start.17 = (bf16[64,640]{1,0:T(8,128)(2,1)S(1)}, bf16[64,640]{1,0:T(8,128)(2,1)S(1)}, u32[]{:S(2)}, u32[]{:S(2)}) collective-permute-start(bf16[64,640]{1,0:T(8,128)(2,1)S(1)} %get-tuple-element.171.refs_6_.refs_1_), channel_id=1, source_target_pairs={{0,1},{1,0},{2,3},{3,2},{4,5},{5,4},{6,7},{7,6},{8,9},{9,8},{10,11... | collective-permute-start | bytes 245768 | tf_op jit(solution)/shard_map/ppermute | solution.py:79
  57.5 4.8 %collective-permute-start.16 = (bf16[64,640]{1,0:T(8,128)(2,1)S(1)}, bf16[64,640]{1,0:T(8,128)(2,1)S(1)}, u32[]{:S(2)}, u32[]{:S(2)}) collective-permute-start(bf16[64,640]{1,0:T(8,128)(2,1)S(1)} %get-tuple-element.170.refs_5_.refs_0_), channel_id=1, source_target_pairs={{0,1},{1,0},{2,3},{3,2},{4,5},{5,4},{6,7},{7,6},{8,9},{9,8},{10,11... | collective-permute-start | bytes 245768 | tf_op jit(solution)/shard_map/ppermute | solution.py:79
  63.3 1.8 %collective-permute-start.19 = (bf16[256,512]{1,0:T(8,128)(2,1)S(1)}, bf16[256,512]{1,0:T(8,128)(2,1)S(1)}, u32[]{:S(2)}, u32[]{:S(2)}) collective-permute-start(bf16[256,512]{1,0:T(8,128)(2,1)S(1)} %get-tuple-element.182), channel_id=1, source_target_pairs={{0,4},{4,0},{1,5},{5,1},{2,6},{6,2},{3,7},{7,3},{8,12},{12,8},{9,1... | collective-permute-start | bytes 786440 | tf_op jit(solution)/shard_map/ppermute | solution.py:79
  63.4 18.8 %collective-permute-start.30 = (bf16[320,1024]{1,0:T(8,128)(2,1)S(1)}, bf16[320,1024]{1,0:T(8,128)(2,1)S(1)}, u32[]{:S(2)}, u32[]{:S(2)}) collective-permute-start(bf16[320,1024]{1,0:T(8,128)(2,1)S(1)} %get-tuple-element.205), channel_id=1, source_target_pairs={{0,4},{4,0},{1,5},{5,1},{2,6},{6,2},{3,7},{7,3},{8,12},{12,8},{9,1... | collective-permute-start | bytes 1966088 | tf_op jit(solution)/shard_map/ppermute | solution.py:79
  63.9 9.0 %collective-permute-start.31 = (bf16[128,640]{1,0:T(8,128)(2,1)S(1)}, bf16[128,640]{1,0:T(8,128)(2,1)S(1)}, u32[]{:S(2)}, u32[]{:S(2)}) collective-permute-start(bf16[128,640]{1,0:T(8,128)(2,1)S(1)} %get-tuple-element.206.refs_0_), channel_id=1, source_target_pairs={{0,1},{1,0},{2,3},{3,2},{4,5},{5,4},{6,7},{7,6},{8,9},{9,8},{10,11... | collective-permute-start | bytes 491528 | tf_op jit(solution)/shard_map/ppermute | solution.py:79
  66.4 18.2 %collective-permute-start.23 = (bf16[320,896]{1,0:T(8,128)(2,1)S(1)}, bf16[320,896]{1,0:T(8,128)(2,1)S(1)}, u32[]{:S(2)}, u32[]{:S(2)}) collective-permute-start(bf16[320,896]{1,0:T(8,128)(2,1)S(1)} %get-tuple-element.196), channel_id=1, source_target_pairs={{0,4},{4,0},{1,5},{5,1},{2,6},{6,2},{3,7},{7,3},{8,12},{12,8},{9,1... | collective-permute-start | bytes 1720328 | tf_op jit(solution)/shard_map/ppermute | solution.py:79
  66.5 6.4 %collective-permute-start.32 = (bf16[128,512]{1,0:T(8,128)(2,1)S(1)}, bf16[128,512]{1,0:T(8,128)(2,1)S(1)}, u32[]{:S(2)}, u32[]{:S(2)}) collective-permute-start(bf16[128,512]{1,0:T(8,128)(2,1)S(1)} %get-tuple-element.209), channel_id=1, source_target_pairs={{0,1},{1,0},{2,3},{3,2},{4,5},{5,4},{6,7},{7,6},{8,9},{9,8},{10,11... | collective-permute-start | bytes 393224 | tf_op jit(solution)/shard_map/ppermute | solution.py:79
  73.3 8.8 %collective-permute-start.33 = (bf16[320,512]{1,0:T(8,128)(2,1)S(1)}, bf16[320,512]{1,0:T(8,128)(2,1)S(1)}, u32[]{:S(2)}, u32[]{:S(2)}) collective-permute-start(bf16[320,512]{1,0:T(8,128)(2,1)S(1)} %get-tuple-element.211), channel_id=1, source_target_pairs={{0,4},{4,0},{1,5},{5,1},{2,6},{6,2},{3,7},{7,3},{8,12},{12,8},{9,1... | collective-permute-start | bytes 983048 | tf_op jit(solution)/shard_map/ppermute | solution.py:79
  73.4 7.1 %collective-permute-start.13 = (bf16[128,640]{1,0:T(8,128)(2,1)S(1)}, bf16[128,640]{1,0:T(8,128)(2,1)S(1)}, u32[]{:S(2)}, u32[]{:S(2)}) collective-permute-start(bf16[128,640]{1,0:T(8,128)(2,1)S(1)} %get-tuple-element.152.a), channel_id=1, source_target_pairs={{0,1},{1,0},{2,3},{3,2},{4,5},{5,4},{6,7},{7,6},{8,9},{9,8},{10,11... | collective-permute-start | bytes 491528 | tf_op jit(solution)/shard_map/ppermute | solution.py:79
  74.3 9.2 %collective-permute-start.20 = (bf16[128,640]{1,0:T(8,128)(2,1)S(1)}, bf16[128,640]{1,0:T(8,128)(2,1)S(1)}, u32[]{:S(2)}, u32[]{:S(2)}) collective-permute-start(bf16[128,640]{1,0:T(8,128)(2,1)S(1)} %get-tuple-element.184.refs_7_), channel_id=1, source_target_pairs={{0,1},{1,0},{2,3},{3,2},{4,5},{5,4},{6,7},{7,6},{8,9},{9,8},{10,11... | collective-permute-start | bytes 491528 | tf_op jit(solution)/shard_map/ppermute | solution.py:79
  80.5 5.3 %collective-permute-start.38 = (bf16[80,1024]{1,0:T(8,128)(2,1)S(1)}, bf16[80,1024]{1,0:T(8,128)(2,1)S(1)}, u32[]{:S(2)}, u32[]{:S(2)}) collective-permute-start(bf16[80,1024]{1,0:T(8,128)(2,1)S(1)} %get-tuple-element.219), channel_id=1, source_target_pairs={{0,8},{8,0},{16,24},{24,16},{1,9},{9,1},{17,25},{25,17},{2,10},{10... | collective-permute-start | bytes 491528 | tf_op jit(solution)/shard_map/ppermute | solution.py:79
  82.1 5.4 %collective-permute-start.34 = (bf16[320,256]{1,0:T(8,128)(2,1)S(1)}, bf16[320,256]{1,0:T(8,128)(2,1)S(1)}, u32[]{:S(2)}, u32[]{:S(2)}) collective-permute-start(bf16[320,256]{1,0:T(8,128)(2,1)S(1)} %get-tuple-element.214), channel_id=1, source_target_pairs={{0,4},{4,0},{1,5},{5,1},{2,6},{6,2},{3,7},{7,3},{8,12},{12,8},{9,1... | collective-permute-start | bytes 491528 | tf_op jit(solution)/shard_map/ppermute | solution.py:79
  82.2 10.6 %collective-permute-start.39 = (bf16[80,1024]{1,0:T(8,128)(2,1)S(1)}, bf16[80,1024]{1,0:T(8,128)(2,1)S(1)}, u32[]{:S(2)}, u32[]{:S(2)}) collective-permute-start(bf16[80,1024]{1,0:T(8,128)(2,1)S(1)} %get-tuple-element.220), channel_id=1, source_target_pairs={{0,16},{8,24},{16,0},{24,8},{1,17},{9,25},{17,1},{25,9},{2,18},{10... | collective-permute-start | bytes 491528 | tf_op jit(solution)/shard_map/ppermute | solution.py:79
  83.5 10.1 %collective-permute-start.40 = (bf16[80,1024]{1,0:T(8,128)(2,1)S(1)}, bf16[80,1024]{1,0:T(8,128)(2,1)S(1)}, u32[]{:S(2)}, u32[]{:S(2)}) collective-permute-start(bf16[80,1024]{1,0:T(8,128)(2,1)S(1)} %get-tuple-element.221), channel_id=1, source_target_pairs={{0,24},{8,16},{16,8},{24,0},{1,25},{9,17},{17,9},{25,1},{2,26},{10... | collective-permute-start | bytes 491528 | tf_op jit(solution)/shard_map/ppermute | solution.py:79
  84.6 11.0 %collective-permute-start.21 = (bf16[128,640]{1,0:T(8,128)(2,1)S(1)}, bf16[128,640]{1,0:T(8,128)(2,1)S(1)}, u32[]{:S(2)}, u32[]{:S(2)}) collective-permute-start(bf16[128,640]{1,0:T(8,128)(2,1)S(1)} %shard_map.224.refs_2_), channel_id=1, source_target_pairs={{0,2},{1,3},{2,0},{3,1},{4,6},{5,7},{6,4},{7,5},{8,10},{9,11},{10,... | collective-permute-start | bytes 491528 | tf_op jit(solution)/shard_map/ppermute | solution.py:79
  85.8 10.5 %collective-permute-start.24 = (bf16[80,896]{1,0:T(8,128)(2,1)S(1)}, bf16[80,896]{1,0:T(8,128)(2,1)S(1)}, u32[]{:S(2)}, u32[]{:S(2)}) collective-permute-start(bf16[80,896]{1,0:T(8,128)(2,1)S(1)} %get-tuple-element.198), channel_id=1, source_target_pairs={{0,8},{8,0},{16,24},{24,16},{1,9},{9,1},{17,25},{25,17},{2,10},{10... | collective-permute-start | bytes 430088 | tf_op jit(solution)/shard_map/ppermute | solution.py:79
  87.6 11.0 %collective-permute-start.25 = (bf16[80,896]{1,0:T(8,128)(2,1)S(1)}, bf16[80,896]{1,0:T(8,128)(2,1)S(1)}, u32[]{:S(2)}, u32[]{:S(2)}) collective-permute-start(bf16[80,896]{1,0:T(8,128)(2,1)S(1)} %get-tuple-element.199), channel_id=1, source_target_pairs={{0,16},{8,24},{16,0},{24,8},{1,17},{9,25},{17,1},{25,9},{2,18},{10... | collective-permute-start | bytes 430088 | tf_op jit(solution)/shard_map/ppermute | solution.py:79
  92.9 15.7 %collective-permute-start.35 = (bf16[80,1792]{1,0:T(8,128)(2,1)S(1)}, bf16[80,1792]{1,0:T(8,128)(2,1)S(1)}, u32[]{:S(2)}, u32[]{:S(2)}) collective-permute-start(bf16[80,1792]{1,0:T(8,128)(2,1)S(1)} %get-tuple-element.216), channel_id=1, source_target_pairs={{0,8},{8,0},{16,24},{24,16},{1,9},{9,1},{17,25},{25,17},{2,10},{10... | collective-permute-start | bytes 860168 | tf_op jit(solution)/shard_map/ppermute | solution.py:79
  93.6 17.1 %collective-permute-start.36 = (bf16[80,1792]{1,0:T(8,128)(2,1)S(1)}, bf16[80,1792]{1,0:T(8,128)(2,1)S(1)}, u32[]{:S(2)}, u32[]{:S(2)}) collective-permute-start(bf16[80,1792]{1,0:T(8,128)(2,1)S(1)} %get-tuple-element.217), channel_id=1, source_target_pairs={{0,16},{8,24},{16,0},{24,8},{1,17},{9,25},{17,1},{25,9},{2,18},{10... | collective-permute-start | bytes 860168 | tf_op jit(solution)/shard_map/ppermute | solution.py:79
  95.6 10.3 %collective-permute-start.26 = (bf16[80,896]{1,0:T(8,128)(2,1)S(1)}, bf16[80,896]{1,0:T(8,128)(2,1)S(1)}, u32[]{:S(2)}, u32[]{:S(2)}) collective-permute-start(bf16[80,896]{1,0:T(8,128)(2,1)S(1)} %get-tuple-element.200), channel_id=1, source_target_pairs={{0,24},{8,16},{16,8},{24,0},{1,25},{9,17},{17,9},{25,1},{2,26},{10... | collective-permute-start | bytes 430088 | tf_op jit(solution)/shard_map/ppermute | solution.py:79
  96.4 16.4 %collective-permute-start.37 = (bf16[80,1792]{1,0:T(8,128)(2,1)S(1)}, bf16[80,1792]{1,0:T(8,128)(2,1)S(1)}, u32[]{:S(2)}, u32[]{:S(2)}) collective-permute-start(bf16[80,1792]{1,0:T(8,128)(2,1)S(1)} %get-tuple-element.218), channel_id=1, source_target_pairs={{0,24},{8,16},{16,8},{24,0},{1,25},{9,17},{17,9},{25,1},{2,26},{10... | collective-permute-start | bytes 860168 | tf_op jit(solution)/shard_map/ppermute | solution.py:79
  98.6 8.6 %collective-permute-start.41 = (bf16[80,1024]{1,0:T(8,128)(2,1)S(1)}, bf16[80,1024]{1,0:T(8,128)(2,1)S(1)}, u32[]{:S(2)}, u32[]{:S(2)}) collective-permute-start(bf16[80,1024]{1,0:T(8,128)(2,1)S(1)} %shard_map.234), channel_id=1, source_target_pairs={{0,1},{1,0},{2,3},{3,2},{4,5},{5,4},{6,7},{7,6},{8,9},{9,8},{10,11... | collective-permute-start | bytes 491528 | tf_op jit(solution)/shard_map/ppermute | solution.py:79
  105.8 7.8 %collective-permute-start.22 = (bf16[128,640]{1,0:T(8,128)(2,1)S(1)}, bf16[128,640]{1,0:T(8,128)(2,1)S(1)}, u32[]{:S(2)}, u32[]{:S(2)}) collective-permute-start(bf16[128,640]{1,0:T(8,128)(2,1)S(1)} %shard_map.225.a), channel_id=1, source_target_pairs={{0,1},{1,0},{2,3},{3,2},{4,5},{5,4},{6,7},{7,6},{8,9},{9,8},{10,11... | collective-permute-start | bytes 491528 | tf_op jit(solution)/shard_map/ppermute | solution.py:79
  107.2 7.2 %collective-permute-start.27 = (bf16[80,640]{1,0:T(8,128)(2,1)S(1)}, bf16[80,640]{1,0:T(8,128)(2,1)S(1)}, u32[]{:S(2)}, u32[]{:S(2)}) collective-permute-start(bf16[80,640]{1,0:T(8,128)(2,1)S(1)} %get-tuple-element.202.refs_0_), channel_id=1, source_target_pairs={{0,1},{1,0},{2,3},{3,2},{4,5},{5,4},{6,7},{7,6},{8,9},{9,8},{10,11... | collective-permute-start | bytes 307208 | tf_op jit(solution)/shard_map/ppermute | solution.py:79
  108.5 6.7 %collective-permute-start.28 = (bf16[80,640]{1,0:T(8,128)(2,1)S(1)}, bf16[80,640]{1,0:T(8,128)(2,1)S(1)}, u32[]{:S(2)}, u32[]{:S(2)}) collective-permute-start(bf16[80,640]{1,0:T(8,128)(2,1)S(1)} %get-tuple-element.202.refs_0_), channel_id=1, source_target_pairs={{0,2},{1,3},{2,0},{3,1},{4,6},{5,7},{6,4},{7,5},{8,10},{9,11},{10,... | collective-permute-start | bytes 307208 | tf_op jit(solution)/shard_map/ppermute | solution.py:79
  110.8 6.6 %collective-permute-start.29 = (bf16[80,640]{1,0:T(8,128)(2,1)S(1)}, bf16[80,640]{1,0:T(8,128)(2,1)S(1)}, u32[]{:S(2)}, u32[]{:S(2)}) collective-permute-start(bf16[80,640]{1,0:T(8,128)(2,1)S(1)} %get-tuple-element.202.refs_0_), channel_id=1, source_target_pairs={{0,3},{1,2},{2,1},{3,0},{4,7},{5,6},{6,5},{7,4},{8,11},{9,10},{10,... | collective-permute-start | bytes 307208 | tf_op jit(solution)/shard_map/ppermute | solution.py:79
  (3 other events, 3.2 us)

commit v3 on v2

--- a/solution.py
+++ b/solution.py
@@ -168,9 +168,10 @@
     def pre_body(*refs):
         sources, (gate, up, down, wq, wo) = refs[:7], refs[7:12]
         normed_o, kv_o, unit_o, scale_o, cos_o, sin_o, idx_o, start_o, gate_o, piece_o, wq_o, wo_o = refs[12:24]
-        col_pos, col_idx, sem = refs[24:27]
-        table, hid, pos, gains, hgains, freqs, wkv = refs[27:]
-        loads = [pltpu.make_async_copy(a, b, sem.at[i]) for i, (a, b) in enumerate(zip(sources, refs[27:]))]
+        key_o, hid, gains, hgains, wkv = refs[24:29]
+        col_pos, col_idx, sem, table, pos, freqs = refs[29:]
+        places = (table, hid, pos, gains, hgains, freqs, wkv)
+        loads = [pltpu.make_async_copy(a, b, sem.at[i]) for i, (a, b) in enumerate(zip(sources, places))]
         moves = [
             pltpu.make_async_copy(up.at[own_piece(width), :], piece_o.at[:up_piece, :ff], sem.at[7]),
             pltpu.make_async_copy(down.at[own_piece(ff), :], piece_o.at[:down_piece, ff:], sem.at[8]),
@@ -214,11 +215,26 @@
         scale_o[...] = scale
         kv_o[:, :head_dim] = rotate(unit * hgains[1:2, :], cos_o[...], sin_o[...]).astype(bf16)
         kv_o[:, head_dim:] = kv[:, head_dim:].astype(bf16)
+        low = lax.axis_index("tp") & 1
+        ctx = lax.axis_index("ctx")
+        order = [ctx, ctx ^ 1] if paired else list(range(n_ctx))
+        lane = lax.broadcasted_iota(jnp.int32, (1, seq), 1)
+        key_idx = lane
+        for m, rank in enumerate(order):
+            for at in range(0, rows, unit_len):
+                first = (low ^ (at // share)) * share + at % share
+                base = table[rank * blocks + lax.div(first, block_len)] * block_len
+                base = base + lax.rem(first, block_len)
+                begin = m * rows + at
+                key_idx = jnp.where(
+                    (lane >= begin) & (lane < begin + unit_len), lane + (base - begin), key_idx
+                )
+        key_o[...] = key_idx.astype(f32)
         for move in moves:
             move.wait()
 
     sources = (block_table, hidden, positions, norm_gains, head_norm_gains, freq, key_value_weight)
-    normed, kv_mine, unit_k, scale_k, cosine, sine, idx, start, gate_pack, piece_pack, wq_near, wo_near = kernel_call(
+    first = kernel_call(
         pre_body,
         tuple(
             pltpu.with_memory_space_constraint(x, pltpu.HBM)
@@ -237,12 +253,27 @@
             ((piece_rows, ff + width), bf16),
             (query_weight.shape, bf16),
             (output_weight.shape, bf16),
+            ((1, seq), f32),
+        ]
+        + [(x.shape, x.dtype) for x in (hidden, norm_gains, head_norm_gains, key_value_weight)],
+        scratch=[
+            pltpu.VMEM((rows, 1), f32),
+            pltpu.VMEM((rows, 1), f32),
+            pltpu.SemaphoreType.DMA((12,)),
+            pltpu.SMEM(block_table.shape, block_table.dtype),
+            pltpu.VMEM(positions.shape, positions.dtype),
+            pltpu.VMEM(freq.shape, freq.dtype),
         ],
-        scratch=[pltpu.VMEM((rows, 1), f32), pltpu.VMEM((rows, 1), f32), pltpu.SemaphoreType.DMA((12,))]
-        + [pltpu.SMEM(block_table.shape, block_table.dtype)]
-        + [pltpu.VMEM(x.shape, x.dtype) for x in sources[1:]],
         in_hbm=12,
     )
+    normed, kv_mine, unit_k, scale_k, cosine, sine, idx, start, gate_pack, piece_pack = first[:10]
+    wq_near, wo_near, key_places, hidden, norm_gains, head_norm_gains, key_value_weight = first[10:]
+
+    if paired:
+        kvs = [kv_mine, other_core(kv_mine)]
+    else:
+        kvs = [lax.all_gather(kv_mine, "ctx", axis=0, tiled=True)]
+
 
     gate_near = neighbour(gate_pack)
     piece_near = neighbour(piece_pack)
@@ -272,11 +303,6 @@
         halves + tuple(other_core(h) for h in halves),
         [((width, ff), bf16), ((width, ff), bf16), ((ff, width), bf16)],
     )
-
-    if paired:
-        kvs = [kv_mine, other_core(kv_mine)]
-    else:
-        kvs = [lax.all_gather(kv_mine, "ctx", axis=0, tiled=True)]
 
     def query_body(nrm, wq, hgains, cos, sin, q_o, unit_o, scale_o):
         raw = product(nrm[...], wq[...])
@@ -295,25 +321,10 @@
     )
 
     def attend_body(*refs):
-        table, q, idx_r, start_r, wo = refs[:5]
+        key_r, q, idx_r, start_r, wo = refs[:5]
         kv = refs[5 : 5 + len(kvs)]
         probs_o, context_o, mine_o, send_o = refs[5 + len(kvs) :]
-        low = lax.axis_index("tp") & 1
-        ctx = lax.axis_index("ctx")
-        order = [ctx, ctx ^ 1] if paired else list(range(n_ctx))
-        lane = lax.broadcasted_iota(jnp.int32, (1, seq), 1)
-        key_idx = lane
-        for m, rank in enumerate(order):
-            for at in range(0, rows, unit_len):
-                first = (low ^ (at // share)) * share + at % share
-                base = table[rank * blocks + lax.div(first, block_len)] * block_len
-                base = base + lax.rem(first, block_len)
-                begin = m * rows + at
-                key_idx = jnp.where(
-                    (lane >= begin) & (lane < begin + unit_len), lane + (base - begin), key_idx
-                )
-        key_idx = key_idx.astype(f32)
-        allowed = (key_idx <= idx_r[...]) & (key_idx >= start_r[...])
+        allowed = (key_r[...] <= idx_r[...]) & (key_r[...] >= start_r[...])
         length = seq // len(kvs)
         for h in range(heads):
             cols = slice(h * head_dim, (h + 1) * head_dim)
@@ -336,14 +347,13 @@
 
     probs, context, attn_mine, attn_send = kernel_call(
         attend_body,
-        (block_table, queries, idx, start, wo_near, *kvs),
+        (key_places, queries, idx, start, wo_near, *kvs),
         [
             ((heads, rows, seq), f32),
             ((rows, q_width), bf16),
             ((share, width), f32),
             ((share, width), bf16),
         ],
-        tables=1,
     )
 
     def meet_body(a, b, o):
@@ -550,12 +560,14 @@
     def ff_grad_fill(*refs):
         x, d_gate_v, d_up_v = (joined(refs[k * streams : (k + 1) * streams]) for k in range(3))
         near_acc, own_acc = refs[3 * streams :]
-        for at, right in enumerate((d_gate_v, d_up_v)):
-            total = lead_product(x, right)
-            own_acc[:, at * ff : (at + 1) * ff] = total[:, :ff]
-            near_acc[:, at * ff : (at + 1) * ff] = total[:, ff:]
-
-    near_grads, own_grads = grad_call(ff_grad_fill, (*ff_in, *d_gate, *d_up), 2 * ff, 2 * ff)
+        total = lead_product(x, d_gate_v)
+        near_acc[:, :ff] = total[:, ff:]
+        near_acc[:, 2 * ff :] = total[:, :ff]
+        total = lead_product(x, d_up_v)
+        near_acc[:, ff : 2 * ff] = total[:, ff:]
+        own_acc[...] = total[:, :ff]
+
+    near_grads, own_grads = grad_call(ff_grad_fill, (*ff_in, *d_gate, *d_up), 3 * ff, ff)
     mid_terms = reduce_grads(near_grads)
 
     def mix_back(k):
@@ -678,9 +690,11 @@
     dn_terms = exchanged(meet(dn_mine, neighbour(dn_send)))
 
     def mid_body(*refs):
-        refs[-1][...] = summed(refs[:-1]).astype(bf16)
-
-    (mid_send,) = kernel_call(mid_body, tuple(mid_terms), [((out_rows, 2 * ff), bf16)])
+        total = summed(refs[:-2])
+        refs[-2][...] = total[:, : 2 * ff].astype(bf16)
+        refs[-1][...] = total[:, 2 * ff :]
+
+    mid_send, mid_gate = kernel_call(mid_body, tuple(mid_terms), [((out_rows, 2 * ff), bf16), ((out_rows, ff), f32)])
     mid_near = neighbour(mid_send)
 
     def down_grad_fill(*refs):
@@ -697,14 +711,14 @@
 
     def side_body(*refs):
         total = summed(refs[: len(side_terms)])
-        near, gate_o, up_o, down_o, out_o = refs[len(side_terms) :]
-        gate_o[...] = total[:, :ff] + near[:, :ff].astype(f32)
-        up_o[...] = total[:, ff : 2 * ff] + near[:, ff:].astype(f32)
-        down_o[...] = total[:, 2 * ff : 3 * ff]
-        out_o[...] = total[:, 3 * ff :]
+        mine, near, gate_o, up_o, down_o, out_o = refs[len(side_terms) :]
+        gate_o[...] = mine[...] + near[:, :ff].astype(f32)
+        up_o[...] = total[:, :ff] + near[:, ff:].astype(f32)
+        down_o[...] = total[:, ff : 2 * ff]
+        out_o[...] = total[:, 2 * ff :]
 
     gate_grad, up_grad, down_grad, out_grad = kernel_call(
-        side_body, (*side_terms, mid_near), [((out_rows, ff), f32)] * 3 + [((out_rows, q_width), f32)]
+        side_body, (*side_terms, mid_gate, mid_near), [((out_rows, ff), f32)] * 3 + [((out_rows, q_width), f32)]
     )
 
     lanes = 128
@@ -748,19 +762,27 @@
     query_grad, kv_mine_sum = kernel_call(
         last_body, tuple(last_terms), [((out_rows, q_width), f32), ((out_rows, 2 * head_dim + lanes), bf16)]
     )
-    kv_sums = [kv_mine_sum] + [swap(kv_mine_sum, "tp", n_tp, k) for k in range(1, n_tp)]
-
-    def kv_body(*refs):
-        terms = [r[...].astype(f32) for r in refs[:n_tp]]
-        while len(terms) > 1:
-            terms = [a + b for a, b in zip(terms[::2], terms[1::2])]
-        refs[n_tp][...] = terms[0][:, : 2 * head_dim]
-        lines = terms[0][:, 2 * head_dim :].T
-        refs[n_tp + 1][...] = lines[:4]
-        refs[n_tp + 2][...] = lines[4:6, :head_rows]
-
+
+    def pair_body(a, b, o):
+        o[...] = (a[...].astype(f32) + b[...].astype(f32)).astype(bf16)
+
+    def kv_body(a, b, kv_o, gain_o, head_o):
+        total = a[...].astype(f32) + b[...].astype(f32)
+        kv_o[...] = total[:, : 2 * head_dim]
+        lines = total[:, 2 * head_dim :].T
+        gain_o[...] = lines[:4]
+        head_o[...] = lines[4:6, :head_rows]
+
+    kv_sum = kv_mine_sum
+    bit = n_tp // 2
+    while bit > 1:
+        pair = (kv_sum, swap(kv_sum, "tp", n_tp, bit))
+        (kv_sum,) = kernel_call(pair_body, pair, [(kv_sum.shape, bf16)])
+        bit //= 2
     kv_grad, gain_grad, head_gain_grad = kernel_call(
-        kv_body, tuple(kv_sums), [((out_rows, 2 * head_dim), f32), ((4, out_rows), f32), ((2, head_rows), f32)]
+        kv_body,
+        (kv_sum, swap(kv_sum, "tp", n_tp, bit)),
+        [((out_rows, 2 * head_dim), f32), ((4, out_rows), f32), ((2, head_rows), f32)],
     )
 
     def input_back_body(hid, gains, *refs):

time: 118 us -> 119 us (level)
  waiting for transfers between devices: 54.9 us -> 61.5 us
  starting transfers between devices: 41.1 us -> 37.3 us
  local copies, waits for them, and re-layouts: 1.37 us -> 0.03 us
    ppermute x42 -> x41, waiting for transfers between devices: 54.9 us -> 61.5 us  [swap(): return lax.ppermute(x, axis, [(i, i ^ k) for i in range(size)])]
    ppermute x42 -> x41, starting transfers between devices: 41.1 us -> 37.3 us  [swap(): return lax.ppermute(x, axis, [(i, i ^ k) for i in range(size)])]
    unnamed x18 -> x8, local copies, waits for them, and re-layouts: 1.37 us -> 0.03 us
    pallas_call x32 -> x33, Pallas kernels: 19.7 us -> 19.3 us  [kernel_call(): pl.pallas_call(body, out_shape=[jax.ShapeDtypeStruct(s, d) for s, d in ou...]
  transfers between devices with their start and end apart: 42 -> 41, of which waited for: 19 -> 22; matrix products, arithmetic and copies ran while one was open for 0% -> 0% of each run, Pallas kernels for 10% -> 9%
where the time goes in v3:
time: 119 us
  waiting for transfers between devices  61.5 us (52%)
  starting transfers between devices  37.3 us (31%)
  Pallas kernels  19.3 us (16%)
    ppermute x41, waiting for transfers between devices, swap(): return lax.ppermute(x, axis, [(i, i ^ k) for i in range(size)])  61.5 us
    ppermute x41, starting transfers between devices, swap(): return lax.ppermute(x, axis, [(i, i ^ k) for i in range(size)])  37.3 us
    pallas_call x33, Pallas kernels, kernel_call(): pl.pallas_call(body, out_shape=[jax.ShapeDtypeStruct(s, d) for s, d in ou...  19.3 us
  transfers between devices with their start and end apart: 41, of which 22 were waited for; matrix products, arithmetic and copies ran while one was open for 0% of the time, Pallas kernels for 9%

profile of v3, /device:TPU:0, one launch (start us, length us, event | category | flops | bytes accessed | tf_op | source)
XLA Modules:
  0.0 119.0 jit_solution(11703209856070509689)
XLA Ops:
  0.6 2.3 %shard_map.204 = (bf16[256,640]{1,0:T(8,128)(2,1)S(1)}, bf16[256,512]{1,0:T(8,128)(2,1)S(1)}, f32[256,256]{1,0:T(8,128)S(1)}, f32[256,1]{1,0:T(8,128)S(1)}, f32[...) custom-call(s32[4]{0:T(128)} %refs_0_.1, ...), custom_call_target="tpu_custom_call" | custom-call | bytes 6901264 | tf_op jit(solution)/shard_map/pallas_call | solution.py:65
  2.9 3.1 %collective-permute-start.1 = (bf16[80,1152]{1,0:T(8,128)(2,1)S(1)}, bf16[80,1152]{1,0:T(8,128)(2,1)S(1)}, u32[]{:S(2)}, u32[]{:S(2)}) collective-permute-start(bf16[80,1152]{1,0:T(8,128)(2,1)S(1)} %get-tuple-element.129), channel_id=1, source_target_pairs={{0,1},{1,0},{2,3},{3,2},{4,5},{5,4},{6,7},{7,6},{8,9},{9,8},{10,11... | collective-permute-start | bytes 552968 | tf_op jit(solution)/shard_map/ppermute | solution.py:79
  6.1 5.4 %collective-permute-done.1.refs_0_ = bf16[80,1152]{1,0:T(8,128)(2,1)S(1)} collective-permute-done((bf16[80,1152]{1,0:T(8,128)(2,1)S(1)}, bf16[80,1152]{1,0:T(8,128)(2,1)S(1)}, u32[]{:S(2)}, u32[]{:S(2)}) %collective-permute-start.1) | collective-permute-done | bytes 184352 | tf_op jit(solution)/shard_map/ppermute | solution.py:79
  11.6 1.9 %collective-permute-start.2 = (bf16[80,1152]{1,0:T(8,128)(2,1)S(1)}, bf16[80,1152]{1,0:T(8,128)(2,1)S(1)}, u32[]{:S(2)}, u32[]{:S(2)}) collective-permute-start(bf16[80,1152]{1,0:T(8,128)(2,1)S(1)} %collective-permute-done.1.refs_0_), channel_id=1, source_target_pairs={{0,8},{8,0},{16,24},{24,16},{1,9},{9,1},{17,25},{25,17},{2,10},{10... | collective-permute-start | bytes 552968 | tf_op jit(solution)/shard_map/ppermute | solution.py:79
  13.5 1.5 %collective-permute-start.3 = (bf16[80,1152]{1,0:T(8,128)(2,1)S(1)}, bf16[80,1152]{1,0:T(8,128)(2,1)S(1)}, u32[]{:S(2)}, u32[]{:S(2)}) collective-permute-start(bf16[80,1152]{1,0:T(8,128)(2,1)S(1)} %collective-permute-done.1.refs_0_), channel_id=1, source_target_pairs={{0,16},{8,24},{16,0},{24,8},{1,17},{9,25},{17,1},{25,9},{2,18},{10... | collective-permute-start | bytes 552968 | tf_op jit(solution)/shard_map/ppermute | solution.py:79
  15.4 0.8 shard_map.208
  16.2 2.1 %collective-permute-start.9 = (bf16[128,640]{1,0:T(8,128)(2,1)S(1)}, bf16[128,640]{1,0:T(8,128)(2,1)S(1)}, u32[]{:S(2)}, u32[]{:S(2)}) collective-permute-start(bf16[128,640]{1,0:T(8,128)(2,1)S(1)} %get-tuple-element.147), channel_id=1, source_target_pairs={{0,1},{1,0},{2,3},{3,2},{4,5},{5,4},{6,7},{7,6},{8,9},{9,8},{10,11... | collective-permute-start | bytes 491528 | tf_op jit(solution)/shard_map/ppermute | solution.py:79
  18.8 3.2 %collective-permute-done.3.refs_2_ = bf16[80,1152]{1,0:T(8,128)(2,1)S(1)} collective-permute-done((bf16[80,1152]{1,0:T(8,128)(2,1)S(1)}, bf16[80,1152]{1,0:T(8,128)(2,1)S(1)}, u32[]{:S(2)}, u32[]{:S(2)}) %collective-permute-start.3) | collective-permute-done | bytes 184352 | tf_op jit(solution)/shard_map/ppermute | solution.py:79
  22.7 2.7 %collective-permute-start.10 = (bf16[128,640]{1,0:T(8,128)(2,1)S(1)}, bf16[128,640]{1,0:T(8,128)(2,1)S(1)}, u32[]{:S(2)}, u32[]{:S(2)}) collective-permute-start(bf16[128,640]{1,0:T(8,128)(2,1)S(1)} %shard_map.209.refs_8_), channel_id=1, source_target_pairs={{0,2},{1,3},{2,0},{3,1},{4,6},{5,7},{6,4},{7,5},{8,10},{9,11},{10,... | collective-permute-start | bytes 491528 | tf_op jit(solution)/shard_map/ppermute | solution.py:79
  25.5 7.8 %collective-permute-done.10.refs_9_ = bf16[128,640]{1,0:T(8,128)(2,1)S(1)} collective-permute-done((bf16[128,640]{1,0:T(8,128)(2,1)S(1)}, bf16[128,640]{1,0:T(8,128)(2,1)S(1)}, u32[]{:S(2)}, u32[]{:S(2)}) %collective-permute-start.10) | collective-permute-done | bytes 163872 | tf_op jit(solution)/shard_map/ppermute | solution.py:79
  33.4 1.1 shard_map.210
  34.5 1.1 shard_map.211
  35.6 3.0 %collective-permute-start.11 = (bf16[64,640]{1,0:T(8,128)(2,1)S(1)}, bf16[64,640]{1,0:T(8,128)(2,1)S(1)}, u32[]{:S(2)}, u32[]{:S(2)}) collective-permute-start(bf16[64,640]{1,0:T(8,128)(2,1)S(1)} %get-tuple-element.154.refs_11_), channel_id=1, source_target_pairs={{0,2},{1,3},{2,0},{3,1},{4,6},{5,7},{6,4},{7,5},{8,10},{9,11},{10,... | collective-permute-start | bytes 245768 | tf_op jit(solution)/shard_map/ppermute | solution.py:79
  39.0 2.9 %collective-permute-done.12.refs_12_ = bf16[64,640]{1,0:T(8,128)(2,1)S(1)} collective-permute-done((bf16[64,640]{1,0:T(8,128)(2,1)S(1)}, bf16[64,640]{1,0:T(8,128)(2,1)S(1)}, u32[]{:S(2)}, u32[]{:S(2)}) %collective-permute-start.12) | collective-permute-done | bytes 81952 | tf_op jit(solution)/shard_map/ppermute | solution.py:79
  41.9 1.6 %shard_map.214 = (bf16[64,640]{1,0:T(8,128)(2,1)S(1)}, f32[1,640]{1,0:T(1,128)S(1)}, bf16[64,640]{1,0:T(8,128)(2,1)S(1)}, bf16[64,1024]{1,0:T(8,128)(2,1)S(1)}, ...) custom-call(f32[4,640]{1,0:T(4,128)S(1)} %get-tuple-element.126.refs_1_.refs_0_.gains, ...), custom_call_target="tpu_custom_call" | custom-call | bytes 5632512 | tf_op jit(solution)/shard_map/pallas_call | solution.py:65
  43.5 1.0 collective-permute-done.11.refs_12_
  44.5 1.6 %shard_map.215 = (bf16[128,640]{1,0:T(8,128)(2,1)S(1)}, f32[1,640]{1,0:T(1,128)S(1)}, bf16[128,640]{1,0:T(8,128)(2,1)S(1)}, bf16[64,1024]{1,0:T(8,128)(2,1)S(1)}...) custom-call(f32[4,640]{1,0:T(4,128)S(1)} %get-tuple-element.126.refs_1_.refs_0_.gains, ...), custom_call_target="tpu_custom_call" | custom-call | bytes 5960192 | tf_op jit(solution)/shard_map/pallas_call | solution.py:65
  46.1 1.1 shard_map.218
  47.4 2.9 %collective-permute-start.14 = (bf16[64,640]{1,0:T(8,128)(2,1)S(1)}, bf16[64,640]{1,0:T(8,128)(2,1)S(1)}, u32[]{:S(2)}, u32[]{:S(2)}) collective-permute-start(bf16[64,640]{1,0:T(8,128)(2,1)S(1)} %get-tuple-element.166.refs_0_), channel_id=1, source_target_pairs={{0,2},{1,3},{2,0},{3,1},{4,6},{5,7},{6,4},{7,5},{8,10},{9,11},{10,... | collective-permute-start | bytes 245768 | tf_op jit(solution)/shard_map/ppermute | solution.py:79
  50.3 6.3 %collective-permute-done.15.refs_1_ = bf16[64,640]{1,0:T(8,128)(2,1)S(1)} collective-permute-done((bf16[64,640]{1,0:T(8,128)(2,1)S(1)}, bf16[64,640]{1,0:T(8,128)(2,1)S(1)}, u32[]{:S(2)}, u32[]{:S(2)}) %collective-permute-start.15) | collective-permute-done | bytes 81952 | tf_op jit(solution)/shard_map/ppermute | solution.py:79
  57.0 1.3 %collective-permute-done.14.refs_1_ = bf16[64,640]{1,0:T(8,128)(2,1)S(1)} collective-permute-done((bf16[64,640]{1,0:T(8,128)(2,1)S(1)}, bf16[64,640]{1,0:T(8,128)(2,1)S(1)}, u32[]{:S(2)}, u32[]{:S(2)}) %collective-permute-start.14) | collective-permute-done | bytes 81952 | tf_op jit(solution)/shard_map/ppermute | solution.py:79
  58.6 0.8 collective-permute-start.16
  59.6 1.9 %collective-permute-done.17.refs_8_.refs_3_ = bf16[64,640]{1,0:T(8,128)(2,1)S(1)} collective-permute-done((bf16[64,640]{1,0:T(8,128)(2,1)S(1)}, bf16[64,640]{1,0:T(8,128)(2,1)S(1)}, u32[]{:S(2)}, u32[]{:S(2)}) %collective-permute-start.17) | collective-permute-done | bytes 81952 | tf_op jit(solution)/shard_map/ppermute | solution.py:79
  61.5 1.7 %collective-permute-done.16.refs_7_.refs_2_ = bf16[64,640]{1,0:T(8,128)(2,1)S(1)} collective-permute-done((bf16[64,640]{1,0:T(8,128)(2,1)S(1)}, bf16[64,640]{1,0:T(8,128)(2,1)S(1)}, u32[]{:S(2)}, u32[]{:S(2)}) %collective-permute-start.16) | collective-permute-done | bytes 81952 | tf_op jit(solution)/shard_map/ppermute | solution.py:79
  63.2 1.0 shard_map.221
  64.6 1.1 collective-permute-done.19.refs_1_
  67.9 1.3 %collective-permute-start.31 = (bf16[128,512]{1,0:T(8,128)(2,1)S(1)}, bf16[128,512]{1,0:T(8,128)(2,1)S(1)}, u32[]{:S(2)}, u32[]{:S(2)}) collective-permute-start(bf16[128,512]{1,0:T(8,128)(2,1)S(1)} %get-tuple-element.221), channel_id=1, source_target_pairs={{0,1},{1,0},{2,3},{3,2},{4,5},{5,4},{6,7},{7,6},{8,9},{9,8},{10,11... | collective-permute-start | bytes 393224 | tf_op jit(solution)/shard_map/ppermute | solution.py:79
  69.2 7.3 %collective-permute-done.31.refs_4_ = bf16[128,512]{1,0:T(8,128)(2,1)S(1)} collective-permute-done((bf16[128,512]{1,0:T(8,128)(2,1)S(1)}, bf16[128,512]{1,0:T(8,128)(2,1)S(1)}, u32[]{:S(2)}, u32[]{:S(2)}) %collective-permute-start.31) | collective-permute-done | bytes 131104 | tf_op jit(solution)/shard_map/ppermute | solution.py:79
  77.0 0.7 collective-permute-start.13
  78.3 1.3 %collective-permute-start.20 = (bf16[128,640]{1,0:T(8,128)(2,1)S(1)}, bf16[128,640]{1,0:T(8,128)(2,1)S(1)}, u32[]{:S(2)}, u32[]{:S(2)}) collective-permute-start(bf16[128,640]{1,0:T(8,128)(2,1)S(1)} %get-tuple-element.196.refs_7_), channel_id=1, source_target_pairs={{0,1},{1,0},{2,3},{3,2},{4,5},{5,4},{6,7},{7,6},{8,9},{9,8},{10,11... | collective-permute-start | bytes 491528 | tf_op jit(solution)/shard_map/ppermute | solution.py:79
  79.8 4.4 %collective-permute-done.13.b = bf16[128,640]{1,0:T(8,128)(2,1)S(1)} collective-permute-done((bf16[128,640]{1,0:T(8,128)(2,1)S(1)}, bf16[128,640]{1,0:T(8,128)(2,1)S(1)}, u32[]{:S(2)}, u32[]{:S(2)}) %collective-permute-start.13) | collective-permute-done | bytes 163872 | tf_op jit(solution)/shard_map/ppermute | solution.py:79
  84.3 1.9 %collective-permute-start.37 = (bf16[80,1536]{1,0:T(8,128)(2,1)S(1)}, bf16[80,1536]{1,0:T(8,128)(2,1)S(1)}, u32[]{:S(2)}, u32[]{:S(2)}) collective-permute-start(bf16[80,1536]{1,0:T(8,128)(2,1)S(1)} %get-tuple-element.231), channel_id=1, source_target_pairs={{0,8},{8,0},{16,24},{24,16},{1,9},{9,1},{17,25},{25,17},{2,10},{10... | collective-permute-start | bytes 737288 | tf_op jit(solution)/shard_map/ppermute | solution.py:79
  86.2 1.3 %collective-permute-start.25 = (bf16[80,896]{1,0:T(8,128)(2,1)S(1)}, bf16[80,896]{1,0:T(8,128)(2,1)S(1)}, u32[]{:S(2)}, u32[]{:S(2)}) collective-permute-start(bf16[80,896]{1,0:T(8,128)(2,1)S(1)} %get-tuple-element.211), channel_id=1, source_target_pairs={{0,16},{8,24},{16,0},{24,8},{1,17},{9,25},{17,1},{25,9},{2,18},{10... | collective-permute-start | bytes 430088 | tf_op jit(solution)/shard_map/ppermute | solution.py:79
  87.4 0.8 collective-permute-start.38
  88.2 0.8 collective-permute-start.39
  89.0 1.8 %collective-permute-done.24.refs_1_ = bf16[80,896]{1,0:T(8,128)(2,1)S(1)} collective-permute-done((bf16[80,896]{1,0:T(8,128)(2,1)S(1)}, bf16[80,896]{1,0:T(8,128)(2,1)S(1)}, u32[]{:S(2)}, u32[]{:S(2)}) %collective-permute-start.24) | collective-permute-done | bytes 143392 | tf_op jit(solution)/shard_map/ppermute | solution.py:79
  91.5 1.3 %collective-permute-done.25.refs_2_ = bf16[80,896]{1,0:T(8,128)(2,1)S(1)} collective-permute-done((bf16[80,896]{1,0:T(8,128)(2,1)S(1)}, bf16[80,896]{1,0:T(8,128)(2,1)S(1)}, u32[]{:S(2)}, u32[]{:S(2)}) %collective-permute-start.25) | collective-permute-done | bytes 143392 | tf_op jit(solution)/shard_map/ppermute | solution.py:79
  93.6 9.6 %collective-permute-done.26.refs_3_ = bf16[80,896]{1,0:T(8,128)(2,1)S(1)} collective-permute-done((bf16[80,896]{1,0:T(8,128)(2,1)S(1)}, bf16[80,896]{1,0:T(8,128)(2,1)S(1)}, u32[]{:S(2)}, u32[]{:S(2)}) %collective-permute-start.26) | collective-permute-done | bytes 143392 | tf_op jit(solution)/shard_map/ppermute | solution.py:79
  104.8 0.8 collective-permute-start.35
  105.6 2.4 %collective-permute-start.36 = (bf16[80,1280]{1,0:T(8,128)(2,1)S(1)}, bf16[80,1280]{1,0:T(8,128)(2,1)S(1)}, u32[]{:S(2)}, u32[]{:S(2)}) collective-permute-start(bf16[80,1280]{1,0:T(8,128)(2,1)S(1)} %get-tuple-element.230), channel_id=1, source_target_pairs={{0,24},{8,16},{16,8},{24,0},{1,25},{9,17},{17,9},{25,1},{2,26},{10... | collective-permute-start | bytes 614408 | tf_op jit(solution)/shard_map/ppermute | solution.py:79
  108.1 1.4 %collective-permute-start.40 = (bf16[80,1024]{1,0:T(8,128)(2,1)S(1)}, bf16[80,1024]{1,0:T(8,128)(2,1)S(1)}, u32[]{:S(2)}, u32[]{:S(2)}) collective-permute-start(bf16[80,1024]{1,0:T(8,128)(2,1)S(1)} %get-tuple-element.235), channel_id=1, source_target_pairs={{0,1},{1,0},{2,3},{3,2},{4,5},{5,4},{6,7},{7,6},{8,9},{9,8},{10,11... | collective-permute-start | bytes 491528 | tf_op jit(solution)/shard_map/ppermute | solution.py:79
  109.8 1.1 collective-permute-done.27.b
  111.0 2.1 %collective-permute-start.28 = (bf16[80,640]{1,0:T(8,128)(2,1)S(1)}, bf16[80,640]{1,0:T(8,128)(2,1)S(1)}, u32[]{:S(2)}, u32[]{:S(2)}) collective-permute-start(bf16[80,640]{1,0:T(8,128)(2,1)S(1)} %shard_map.230.a), channel_id=1, source_target_pairs={{0,1},{1,0},{2,3},{3,2},{4,5},{5,4},{6,7},{7,6},{8,9},{9,8},{10,11... | collective-permute-start | bytes 307208 | tf_op jit(solution)/shard_map/ppermute | solution.py:79
  113.0 0.8 shard_map.216
  114.0 1.2 %collective-permute-done.40.refs_5_ = bf16[80,1024]{1,0:T(8,128)(2,1)S(1)} collective-permute-done((bf16[80,1024]{1,0:T(8,128)(2,1)S(1)}, bf16[80,1024]{1,0:T(8,128)(2,1)S(1)}, u32[]{:S(2)}, u32[]{:S(2)}) %collective-permute-start.40) | collective-permute-done | bytes 163872 | tf_op jit(solution)/shard_map/ppermute | solution.py:79
  115.3 0.9 shard_map.236
  116.1 1.1 collective-permute-done.22.b
  117.2 0.8 shard_map.226
  (75 shorter events, 12.0 us)
Async XLA Ops:
  2.9 8.6 %collective-permute-start.1 = (bf16[80,1152]{1,0:T(8,128)(2,1)S(1)}, bf16[80,1152]{1,0:T(8,128)(2,1)S(1)}, u32[]{:S(2)}, u32[]{:S(2)}) collective-permute-start(bf16[80,1152]{1,0:T(8,128)(2,1)S(1)} %get-tuple-element.129), channel_id=1, source_target_pairs={{0,1},{1,0},{2,3},{3,2},{4,5},{5,4},{6,7},{7,6},{8,9},{9,8},{10,11... | collective-permute-start | bytes 552968 | tf_op jit(solution)/shard_map/ppermute | solution.py:79
  6.1 12.5 %collective-permute-start = (bf16[320,512]{1,0:T(8,128)(2,1)S(1)}, bf16[320,512]{1,0:T(8,128)(2,1)S(1)}, u32[]{:S(2)}, u32[]{:S(2)}) collective-permute-start(bf16[320,512]{1,0:T(8,128)(2,1)S(1)} %get-tuple-element.128), channel_id=1, source_target_pairs={{0,1},{1,0},{2,3},{3,2},{4,5},{5,4},{6,7},{7,6},{8,9},{9,8},{10,11... | collective-permute-start | bytes 983048 | tf_op jit(solution)/shard_map/ppermute | solution.py:79
  6.1 9.3 %collective-permute-start.8 = (bf16[256,512]{1,0:T(8,128)(2,1)S(1)}, bf16[256,512]{1,0:T(8,128)(2,1)S(1)}, u32[]{:S(2)}, u32[]{:S(2)}) collective-permute-start(bf16[256,512]{1,0:T(8,128)(2,1)S(1)} %get-tuple-element.145.refs_5_.refs_3_), channel_id=1, source_target_pairs={{0,4},{4,0},{1,5},{5,1},{2,6},{6,2},{3,7},{7,3},{8,12},{12,8},{9,1... | collective-permute-start | bytes 786440 | tf_op jit(solution)/shard_map/ppermute | solution.py:79
  11.6 7.2 %collective-permute-start.2 = (bf16[80,1152]{1,0:T(8,128)(2,1)S(1)}, bf16[80,1152]{1,0:T(8,128)(2,1)S(1)}, u32[]{:S(2)}, u32[]{:S(2)}) collective-permute-start(bf16[80,1152]{1,0:T(8,128)(2,1)S(1)} %collective-permute-done.1.refs_0_), channel_id=1, source_target_pairs={{0,8},{8,0},{16,24},{24,16},{1,9},{9,1},{17,25},{25,17},{2,10},{10... | collective-permute-start | bytes 552968 | tf_op jit(solution)/shard_map/ppermute | solution.py:79
  13.5 8.5 %collective-permute-start.3 = (bf16[80,1152]{1,0:T(8,128)(2,1)S(1)}, bf16[80,1152]{1,0:T(8,128)(2,1)S(1)}, u32[]{:S(2)}, u32[]{:S(2)}) collective-permute-start(bf16[80,1152]{1,0:T(8,128)(2,1)S(1)} %collective-permute-done.1.refs_0_), channel_id=1, source_target_pairs={{0,16},{8,24},{16,0},{24,8},{1,17},{9,25},{17,1},{25,9},{2,18},{10... | collective-permute-start | bytes 552968 | tf_op jit(solution)/shard_map/ppermute | solution.py:79
  15.0 7.0 %collective-permute-start.4 = (bf16[80,1152]{1,0:T(8,128)(2,1)S(1)}, bf16[80,1152]{1,0:T(8,128)(2,1)S(1)}, u32[]{:S(2)}, u32[]{:S(2)}) collective-permute-start(bf16[80,1152]{1,0:T(8,128)(2,1)S(1)} %collective-permute-done.1.refs_0_), channel_id=1, source_target_pairs={{0,24},{8,16},{16,8},{24,0},{1,25},{9,17},{17,9},{25,1},{2,26},{10... | collective-permute-start | bytes 552968 | tf_op jit(solution)/shard_map/ppermute | solution.py:79
  16.2 6.4 %collective-permute-start.9 = (bf16[128,640]{1,0:T(8,128)(2,1)S(1)}, bf16[128,640]{1,0:T(8,128)(2,1)S(1)}, u32[]{:S(2)}, u32[]{:S(2)}) collective-permute-start(bf16[128,640]{1,0:T(8,128)(2,1)S(1)} %get-tuple-element.147), channel_id=1, source_target_pairs={{0,1},{1,0},{2,3},{3,2},{4,5},{5,4},{6,7},{7,6},{8,9},{9,8},{10,11... | collective-permute-start | bytes 491528 | tf_op jit(solution)/shard_map/ppermute | solution.py:79
  18.6 6.8 %collective-permute-start.5 = (bf16[320,512]{1,0:T(8,128)(2,1)S(1)}, bf16[320,512]{1,0:T(8,128)(2,1)S(1)}, u32[]{:S(2)}, u32[]{:S(2)}) collective-permute-start(bf16[320,512]{1,0:T(8,128)(2,1)S(1)} %collective-permute-done.refs_0_), channel_id=1, source_target_pairs={{0,4},{4,0},{1,5},{5,1},{2,6},{6,2},{3,7},{7,3},{8,12},{12,8},{9,1... | collective-permute-start | bytes 983048 | tf_op jit(solution)/shard_map/ppermute | solution.py:79
  22.0 3.3 %collective-permute-start.6 = (bf16[320,512]{1,0:T(8,128)(2,1)S(1)}, bf16[320,512]{1,0:T(8,128)(2,1)S(1)}, u32[]{:S(2)}, u32[]{:S(2)}) collective-permute-start(bf16[320,512]{1,0:T(8,128)(2,1)S(1)} %get-tuple-element.130.refs_1_), channel_id=1, source_target_pairs={{0,4},{4,0},{1,5},{5,1},{2,6},{6,2},{3,7},{7,3},{8,12},{12,8},{9,1... | collective-permute-start | bytes 983048 | tf_op jit(solution)/shard_map/ppermute | solution.py:79
  22.1 3.3 %collective-permute-start.7 = (bf16[256,640]{1,0:T(8,128)(2,1)S(1)}, bf16[256,640]{1,0:T(8,128)(2,1)S(1)}, u32[]{:S(2)}, u32[]{:S(2)}) collective-permute-start(bf16[256,640]{1,0:T(8,128)(2,1)S(1)} %get-tuple-element.131.refs_2_), channel_id=1, source_target_pairs={{0,4},{4,0},{1,5},{5,1},{2,6},{6,2},{3,7},{7,3},{8,12},{12,8},{9,1... | collective-permute-start | bytes 983048 | tf_op jit(solution)/shard_map/ppermute | solution.py:79
  22.7 10.7 %copy-start = (bf16[640,512]{1,0:T(8,128)(2,1)S(1)}, bf16[640,512]{1,0:T(8,128)(2,1)}, u32[]{:S(2)}) copy-start(bf16[640,512]{1,0:T(8,128)(2,1)} %refs_5_.3) | copy-start | bytes 1966084
  22.7 10.7 %copy-start.1 = (bf16[640,512]{1,0:T(8,128)(2,1)S(1)}, bf16[640,512]{1,0:T(8,128)(2,1)}, u32[]{:S(2)}) copy-start(bf16[640,512]{1,0:T(8,128)(2,1)} %refs_6_.5) | copy-start | bytes 1966084
  22.7 10.7 %copy-start.2 = (bf16[512,640]{1,0:T(8,128)(2,1)S(1)}, bf16[512,640]{1,0:T(8,128)(2,1)}, u32[]{:S(2)}) copy-start(bf16[512,640]{1,0:T(8,128)(2,1)} %refs_7_.5) | copy-start | bytes 1966084
  22.7 10.7 %collective-permute-start.10 = (bf16[128,640]{1,0:T(8,128)(2,1)S(1)}, bf16[128,640]{1,0:T(8,128)(2,1)S(1)}, u32[]{:S(2)}, u32[]{:S(2)}) collective-permute-start(bf16[128,640]{1,0:T(8,128)(2,1)S(1)} %shard_map.209.refs_8_), channel_id=1, source_target_pairs={{0,2},{1,3},{2,0},{3,1},{4,6},{5,7},{6,4},{7,5},{8,10},{9,11},{10,... | collective-permute-start | bytes 491528 | tf_op jit(solution)/shard_map/ppermute | solution.py:79
  34.4 7.5 %collective-permute-start.12 = (bf16[64,640]{1,0:T(8,128)(2,1)S(1)}, bf16[64,640]{1,0:T(8,128)(2,1)S(1)}, u32[]{:S(2)}, u32[]{:S(2)}) collective-permute-start(bf16[64,640]{1,0:T(8,128)(2,1)S(1)} %get-tuple-element.160.refs_11_), channel_id=1, source_target_pairs={{0,2},{1,3},{2,0},{3,1},{4,6},{5,7},{6,4},{7,5},{8,10},{9,11},{10,... | collective-permute-start | bytes 245768 | tf_op jit(solution)/shard_map/ppermute | solution.py:79
  35.6 8.9 %collective-permute-start.11 = (bf16[64,640]{1,0:T(8,128)(2,1)S(1)}, bf16[64,640]{1,0:T(8,128)(2,1)S(1)}, u32[]{:S(2)}, u32[]{:S(2)}) collective-permute-start(bf16[64,640]{1,0:T(8,128)(2,1)S(1)} %get-tuple-element.154.refs_11_), channel_id=1, source_target_pairs={{0,2},{1,3},{2,0},{3,1},{4,6},{5,7},{6,4},{7,5},{8,10},{9,11},{10,... | collective-permute-start | bytes 245768 | tf_op jit(solution)/shard_map/ppermute | solution.py:79
  38.8 3.1 %copy-start.3 = (bf16[1,2,128,640]{3,2,1,0:T(8,128)(2,1)S(1)}, bf16[1,2,128,640]{3,2,1,0:T(8,128)(2,1)}, u32[]{:S(2)}) copy-start(bf16[1,2,128,640]{3,2,1,0:T(8,128)(2,1)} %param.24) | copy-start | bytes 983044
  47.2 12.2 %collective-permute-start.18 = (bf16[320,1536]{1,0:T(8,128)(2,1)S(1)}, bf16[320,1536]{1,0:T(8,128)(2,1)S(1)}, u32[]{:S(2)}, u32[]{:S(2)}) collective-permute-start(bf16[320,1536]{1,0:T(8,128)(2,1)S(1)} %get-tuple-element.183), channel_id=1, source_target_pairs={{0,4},{4,0},{1,5},{5,1},{2,6},{6,2},{3,7},{7,3},{8,12},{12,8},{9,1... | collective-permute-start | bytes 2949128 | tf_op jit(solution)/shard_map/ppermute | solution.py:79
  47.3 9.3 %collective-permute-start.15 = (bf16[64,640]{1,0:T(8,128)(2,1)S(1)}, bf16[64,640]{1,0:T(8,128)(2,1)S(1)}, u32[]{:S(2)}, u32[]{:S(2)}) collective-permute-start(bf16[64,640]{1,0:T(8,128)(2,1)S(1)} %get-tuple-element.170.refs_0_), channel_id=1, source_target_pairs={{0,2},{1,3},{2,0},{3,1},{4,6},{5,7},{6,4},{7,5},{8,10},{9,11},{10,... | collective-permute-start | bytes 245768 | tf_op jit(solution)/shard_map/ppermute | solution.py:79
  47.4 10.9 %collective-permute-start.14 = (bf16[64,640]{1,0:T(8,128)(2,1)S(1)}, bf16[64,640]{1,0:T(8,128)(2,1)S(1)}, u32[]{:S(2)}, u32[]{:S(2)}) collective-permute-start(bf16[64,640]{1,0:T(8,128)(2,1)S(1)} %get-tuple-element.166.refs_0_), channel_id=1, source_target_pairs={{0,2},{1,3},{2,0},{3,1},{4,6},{5,7},{6,4},{7,5},{8,10},{9,11},{10,... | collective-permute-start | bytes 245768 | tf_op jit(solution)/shard_map/ppermute | solution.py:79
  56.9 4.6 %collective-permute-start.17 = (bf16[64,640]{1,0:T(8,128)(2,1)S(1)}, bf16[64,640]{1,0:T(8,128)(2,1)S(1)}, u32[]{:S(2)}, u32[]{:S(2)}) collective-permute-start(bf16[64,640]{1,0:T(8,128)(2,1)S(1)} %get-tuple-element.182.refs_6_.refs_1_), channel_id=1, source_target_pairs={{0,1},{1,0},{2,3},{3,2},{4,5},{5,4},{6,7},{7,6},{8,9},{9,8},{10,11... | collective-permute-start | bytes 245768 | tf_op jit(solution)/shard_map/ppermute | solution.py:79
  58.6 4.5 %collective-permute-start.16 = (bf16[64,640]{1,0:T(8,128)(2,1)S(1)}, bf16[64,640]{1,0:T(8,128)(2,1)S(1)}, u32[]{:S(2)}, u32[]{:S(2)}) collective-permute-start(bf16[64,640]{1,0:T(8,128)(2,1)S(1)} %get-tuple-element.181.refs_5_.refs_0_), channel_id=1, source_target_pairs={{0,1},{1,0},{2,3},{3,2},{4,5},{5,4},{6,7},{7,6},{8,9},{9,8},{10,11... | collective-permute-start | bytes 245768 | tf_op jit(solution)/shard_map/ppermute | solution.py:79
  64.1 1.6 %collective-permute-start.19 = (bf16[256,512]{1,0:T(8,128)(2,1)S(1)}, bf16[256,512]{1,0:T(8,128)(2,1)S(1)}, u32[]{:S(2)}, u32[]{:S(2)}) collective-permute-start(bf16[256,512]{1,0:T(8,128)(2,1)S(1)} %get-tuple-element.194), channel_id=1, source_target_pairs={{0,4},{4,0},{1,5},{5,1},{2,6},{6,2},{3,7},{7,3},{8,12},{12,8},{9,1... | collective-permute-start | bytes 786440 | tf_op jit(solution)/shard_map/ppermute | solution.py:79
  67.0 11.3 %collective-permute-start.23 = (bf16[320,896]{1,0:T(8,128)(2,1)S(1)}, bf16[320,896]{1,0:T(8,128)(2,1)S(1)}, u32[]{:S(2)}, u32[]{:S(2)}) collective-permute-start(bf16[320,896]{1,0:T(8,128)(2,1)S(1)} %get-tuple-element.208), channel_id=1, source_target_pairs={{0,4},{4,0},{1,5},{5,1},{2,6},{6,2},{3,7},{7,3},{8,12},{12,8},{9,1... | collective-permute-start | bytes 1720328 | tf_op jit(solution)/shard_map/ppermute | solution.py:79
  67.2 9.3 %collective-permute-start.30 = (bf16[128,640]{1,0:T(8,128)(2,1)S(1)}, bf16[128,640]{1,0:T(8,128)(2,1)S(1)}, u32[]{:S(2)}, u32[]{:S(2)}) collective-permute-start(bf16[128,640]{1,0:T(8,128)(2,1)S(1)} %get-tuple-element.218.refs_0_), channel_id=1, source_target_pairs={{0,1},{1,0},{2,3},{3,2},{4,5},{5,4},{6,7},{7,6},{8,9},{9,8},{10,11... | collective-permute-start | bytes 491528 | tf_op jit(solution)/shard_map/ppermute | solution.py:79
  67.9 8.6 %collective-permute-start.31 = (bf16[128,512]{1,0:T(8,128)(2,1)S(1)}, bf16[128,512]{1,0:T(8,128)(2,1)S(1)}, u32[]{:S(2)}, u32[]{:S(2)}) collective-permute-start(bf16[128,512]{1,0:T(8,128)(2,1)S(1)} %get-tuple-element.221), channel_id=1, source_target_pairs={{0,1},{1,0},{2,3},{3,2},{4,5},{5,4},{6,7},{7,6},{8,9},{9,8},{10,11... | collective-permute-start | bytes 393224 | tf_op jit(solution)/shard_map/ppermute | solution.py:79
  69.2 15.0 %collective-permute-start.29 = (bf16[320,512]{1,0:T(8,128)(2,1)S(1)}, bf16[320,512]{1,0:T(8,128)(2,1)S(1)}, u32[]{:S(2)}, u32[]{:S(2)}) collective-permute-start(bf16[320,512]{1,0:T(8,128)(2,1)S(1)} %get-tuple-element.217), channel_id=1, source_target_pairs={{0,4},{4,0},{1,5},{5,1},{2,6},{6,2},{3,7},{7,3},{8,12},{12,8},{9,1... | collective-permute-start | bytes 983048 | tf_op jit(solution)/shard_map/ppermute | solution.py:79
  76.9 9.3 %collective-permute-start.32 = (bf16[320,512]{1,0:T(8,128)(2,1)S(1)}, bf16[320,512]{1,0:T(8,128)(2,1)S(1)}, u32[]{:S(2)}, u32[]{:S(2)}) collective-permute-start(bf16[320,512]{1,0:T(8,128)(2,1)S(1)} %get-tuple-element.223), channel_id=1, source_target_pairs={{0,4},{4,0},{1,5},{5,1},{2,6},{6,2},{3,7},{7,3},{8,12},{12,8},{9,1... | collective-permute-start | bytes 983048 | tf_op jit(solution)/shard_map/ppermute | solution.py:79
  77.0 7.1 %collective-permute-start.13 = (bf16[128,640]{1,0:T(8,128)(2,1)S(1)}, bf16[128,640]{1,0:T(8,128)(2,1)S(1)}, u32[]{:S(2)}, u32[]{:S(2)}) collective-permute-start(bf16[128,640]{1,0:T(8,128)(2,1)S(1)} %get-tuple-element.163.a), channel_id=1, source_target_pairs={{0,1},{1,0},{2,3},{3,2},{4,5},{5,4},{6,7},{7,6},{8,9},{9,8},{10,11... | collective-permute-start | bytes 491528 | tf_op jit(solution)/shard_map/ppermute | solution.py:79
  78.1 9.4 %collective-permute-start.33 = (bf16[320,256]{1,0:T(8,128)(2,1)S(1)}, bf16[320,256]{1,0:T(8,128)(2,1)S(1)}, u32[]{:S(2)}, u32[]{:S(2)}) collective-permute-start(bf16[320,256]{1,0:T(8,128)(2,1)S(1)} %get-tuple-element.226), channel_id=1, source_target_pairs={{0,4},{4,0},{1,5},{5,1},{2,6},{6,2},{3,7},{7,3},{8,12},{12,8},{9,1... | collective-permute-start | bytes 491528 | tf_op jit(solution)/shard_map/ppermute | solution.py:79
  78.3 9.9 %collective-permute-start.20 = (bf16[128,640]{1,0:T(8,128)(2,1)S(1)}, bf16[128,640]{1,0:T(8,128)(2,1)S(1)}, u32[]{:S(2)}, u32[]{:S(2)}) collective-permute-start(bf16[128,640]{1,0:T(8,128)(2,1)S(1)} %get-tuple-element.196.refs_7_), channel_id=1, source_target_pairs={{0,1},{1,0},{2,3},{3,2},{4,5},{5,4},{6,7},{7,6},{8,9},{9,8},{10,11... | collective-permute-start | bytes 491528 | tf_op jit(solution)/shard_map/ppermute | solution.py:79
  84.1 6.6 %collective-permute-start.24 = (bf16[80,896]{1,0:T(8,128)(2,1)S(1)}, bf16[80,896]{1,0:T(8,128)(2,1)S(1)}, u32[]{:S(2)}, u32[]{:S(2)}) collective-permute-start(bf16[80,896]{1,0:T(8,128)(2,1)S(1)} %get-tuple-element.210), channel_id=1, source_target_pairs={{0,8},{8,0},{16,24},{24,16},{1,9},{9,1},{17,25},{25,17},{2,10},{10... | collective-permute-start | bytes 430088 | tf_op jit(solution)/shard_map/ppermute | solution.py:79
  84.3 19.9 %collective-permute-start.37 = (bf16[80,1536]{1,0:T(8,128)(2,1)S(1)}, bf16[80,1536]{1,0:T(8,128)(2,1)S(1)}, u32[]{:S(2)}, u32[]{:S(2)}) collective-permute-start(bf16[80,1536]{1,0:T(8,128)(2,1)S(1)} %get-tuple-element.231), channel_id=1, source_target_pairs={{0,8},{8,0},{16,24},{24,16},{1,9},{9,1},{17,25},{25,17},{2,10},{10... | collective-permute-start | bytes 737288 | tf_op jit(solution)/shard_map/ppermute | solution.py:79
  86.2 6.6 %collective-permute-start.25 = (bf16[80,896]{1,0:T(8,128)(2,1)S(1)}, bf16[80,896]{1,0:T(8,128)(2,1)S(1)}, u32[]{:S(2)}, u32[]{:S(2)}) collective-permute-start(bf16[80,896]{1,0:T(8,128)(2,1)S(1)} %get-tuple-element.211), channel_id=1, source_target_pairs={{0,16},{8,24},{16,0},{24,8},{1,17},{9,25},{17,1},{25,9},{2,18},{10... | collective-permute-start | bytes 430088 | tf_op jit(solution)/shard_map/ppermute | solution.py:79
  87.4 17.4 %collective-permute-start.38 = (bf16[80,1536]{1,0:T(8,128)(2,1)S(1)}, bf16[80,1536]{1,0:T(8,128)(2,1)S(1)}, u32[]{:S(2)}, u32[]{:S(2)}) collective-permute-start(bf16[80,1536]{1,0:T(8,128)(2,1)S(1)} %get-tuple-element.232), channel_id=1, source_target_pairs={{0,16},{8,24},{16,0},{24,8},{1,17},{9,25},{17,1},{25,9},{2,18},{10... | collective-permute-start | bytes 737288 | tf_op jit(solution)/shard_map/ppermute | solution.py:79
  88.2 17.4 %collective-permute-start.39 = (bf16[80,1536]{1,0:T(8,128)(2,1)S(1)}, bf16[80,1536]{1,0:T(8,128)(2,1)S(1)}, u32[]{:S(2)}, u32[]{:S(2)}) collective-permute-start(bf16[80,1536]{1,0:T(8,128)(2,1)S(1)} %get-tuple-element.233), channel_id=1, source_target_pairs={{0,24},{8,16},{16,8},{24,0},{1,25},{9,17},{17,9},{25,1},{2,26},{10... | collective-permute-start | bytes 737288 | tf_op jit(solution)/shard_map/ppermute | solution.py:79
  90.8 12.5 %collective-permute-start.26 = (bf16[80,896]{1,0:T(8,128)(2,1)S(1)}, bf16[80,896]{1,0:T(8,128)(2,1)S(1)}, u32[]{:S(2)}, u32[]{:S(2)}) collective-permute-start(bf16[80,896]{1,0:T(8,128)(2,1)S(1)} %get-tuple-element.212), channel_id=1, source_target_pairs={{0,24},{8,16},{16,8},{24,0},{1,25},{9,17},{17,9},{25,1},{2,26},{10... | collective-permute-start | bytes 430088 | tf_op jit(solution)/shard_map/ppermute | solution.py:79
  92.8 15.3 %collective-permute-start.21 = (bf16[128,640]{1,0:T(8,128)(2,1)S(1)}, bf16[128,640]{1,0:T(8,128)(2,1)S(1)}, u32[]{:S(2)}, u32[]{:S(2)}) collective-permute-start(bf16[128,640]{1,0:T(8,128)(2,1)S(1)} %shard_map.224.refs_2_), channel_id=1, source_target_pairs={{0,2},{1,3},{2,0},{3,1},{4,6},{5,7},{6,4},{7,5},{8,10},{9,11},{10,... | collective-permute-start | bytes 491528 | tf_op jit(solution)/shard_map/ppermute | solution.py:79
  103.2 7.7 %collective-permute-start.34 = (bf16[80,1280]{1,0:T(8,128)(2,1)S(1)}, bf16[80,1280]{1,0:T(8,128)(2,1)S(1)}, u32[]{:S(2)}, u32[]{:S(2)}) collective-permute-start(bf16[80,1280]{1,0:T(8,128)(2,1)S(1)} %get-tuple-element.228), channel_id=1, source_target_pairs={{0,8},{8,0},{16,24},{24,16},{1,9},{9,1},{17,25},{25,17},{2,10},{10... | collective-permute-start | bytes 614408 | tf_op jit(solution)/shard_map/ppermute | solution.py:79
  104.2 6.7 %collective-permute-start.27 = (bf16[80,640]{1,0:T(8,128)(2,1)S(1)}, bf16[80,640]{1,0:T(8,128)(2,1)S(1)}, u32[]{:S(2)}, u32[]{:S(2)}) collective-permute-start(bf16[80,640]{1,0:T(8,128)(2,1)S(1)} %get-tuple-element.214.a), channel_id=1, source_target_pairs={{0,2},{1,3},{2,0},{3,1},{4,6},{5,7},{6,4},{7,5},{8,10},{9,11},{10,... | collective-permute-start | bytes 307208 | tf_op jit(solution)/shard_map/ppermute | solution.py:79
  104.8 9.2 %collective-permute-start.35 = (bf16[80,1280]{1,0:T(8,128)(2,1)S(1)}, bf16[80,1280]{1,0:T(8,128)(2,1)S(1)}, u32[]{:S(2)}, u32[]{:S(2)}) collective-permute-start(bf16[80,1280]{1,0:T(8,128)(2,1)S(1)} %get-tuple-element.229), channel_id=1, source_target_pairs={{0,16},{8,24},{16,0},{24,8},{1,17},{9,25},{17,1},{25,9},{2,18},{10... | collective-permute-start | bytes 614408 | tf_op jit(solution)/shard_map/ppermute | solution.py:79
  105.6 8.4 %collective-permute-start.36 = (bf16[80,1280]{1,0:T(8,128)(2,1)S(1)}, bf16[80,1280]{1,0:T(8,128)(2,1)S(1)}, u32[]{:S(2)}, u32[]{:S(2)}) collective-permute-start(bf16[80,1280]{1,0:T(8,128)(2,1)S(1)} %get-tuple-element.230), channel_id=1, source_target_pairs={{0,24},{8,16},{16,8},{24,0},{1,25},{9,17},{17,9},{25,1},{2,26},{10... | collective-permute-start | bytes 614408 | tf_op jit(solution)/shard_map/ppermute | solution.py:79
  108.1 7.1 %collective-permute-start.40 = (bf16[80,1024]{1,0:T(8,128)(2,1)S(1)}, bf16[80,1024]{1,0:T(8,128)(2,1)S(1)}, u32[]{:S(2)}, u32[]{:S(2)}) collective-permute-start(bf16[80,1024]{1,0:T(8,128)(2,1)S(1)} %get-tuple-element.235), channel_id=1, source_target_pairs={{0,1},{1,0},{2,3},{3,2},{4,5},{5,4},{6,7},{7,6},{8,9},{9,8},{10,11... | collective-permute-start | bytes 491528 | tf_op jit(solution)/shard_map/ppermute | solution.py:79
  110.9 6.3 %collective-permute-start.22 = (bf16[128,640]{1,0:T(8,128)(2,1)S(1)}, bf16[128,640]{1,0:T(8,128)(2,1)S(1)}, u32[]{:S(2)}, u32[]{:S(2)}) collective-permute-start(bf16[128,640]{1,0:T(8,128)(2,1)S(1)} %shard_map.225.a), channel_id=1, source_target_pairs={{0,1},{1,0},{2,3},{3,2},{4,5},{5,4},{6,7},{7,6},{8,9},{9,8},{10,11... | collective-permute-start | bytes 491528 | tf_op jit(solution)/shard_map/ppermute | solution.py:79
  111.0 7.4 %collective-permute-start.28 = (bf16[80,640]{1,0:T(8,128)(2,1)S(1)}, bf16[80,640]{1,0:T(8,128)(2,1)S(1)}, u32[]{:S(2)}, u32[]{:S(2)}) collective-permute-start(bf16[80,640]{1,0:T(8,128)(2,1)S(1)} %shard_map.230.a), channel_id=1, source_target_pairs={{0,1},{1,0},{2,3},{3,2},{4,5},{5,4},{6,7},{7,6},{8,9},{9,8},{10,11... | collective-permute-start | bytes 307208 | tf_op jit(solution)/shard_map/ppermute | solution.py:79
